TPU v7x, 512 devices: a whole 4x8x8 slice. The times are simulated.
512 devices in a mesh: illum: 32 (over z, y_hi), slab: 8 (over x, core), cuts: 2 (over y_lo).
Axes of the slice: x: 4, y: 8 (y_hi: 4, y_lo: 2; y = y_hi * 2 + y_lo), z: 8, core: 2. Of those that a mesh axis runs over, the one named last changes fastest.
Arguments:
- phase_delay: float32 [4, 256, 1024], P('cuts', 'slab', 'illum'), may hold values from -1.5 to 1.5
- attenuation: float32 [4, 256, 1024], P('cuts', 'slab', 'illum'), may hold values from 0.02 to 0.3
- measured: float32 [32, 2, 256, 1024], P('illum', None, 'slab'), may hold values from -6 to 6
- angles: int32 [32, 2], P('illum'), may hold values from -16 to 16
Outputs:
- grad_phase: float32 [4, 256, 1024], P('cuts', 'slab', 'illum')
- grad_atten: float32 [4, 256, 1024], P('cuts', 'slab', 'illum')
All inputs are finite; a program needn't handle non-finite values.
Results may differ from a plain program's by a relative error of at most 0.0001.
Values sent between devices are 32-bit elements; how exact they have to be, the bound alone decides.
No kernel may reach another device: no remote copies, remote signals or barrier semaphores. Data moves between devices by JAX's collectives and lax.ppermute only.
A program may use at most 64 MiB of HBM per device.

v0:
```python
import math

import jax
import jax.numpy as jnp
from jax import lax
from jax.sharding import PartitionSpec as P

step_coeff = 0.08
square_coeff = 0.0032


def sent_together(arrays, axis, split_dim, concat_dim, along):
    widths = [a.shape[along] for a in arrays]
    both = jnp.concatenate(arrays, axis=along)
    result = lax.all_to_all(both, axis, split_axis=split_dim, concat_axis=concat_dim, tiled=True)
    return tuple(jnp.split(result, [sum(widths[:k]) for k in range(1, len(widths))], axis=along))


def padded_2(shard, sides, width):
    edges = {}
    for axis, dim in sides:
        size, length = (lax.axis_size(axis), shard.shape[dim])
        up = [(i, (i + 1) % size) for i in range(size - 1)]
        last = lax.slice_in_dim(shard, length - width, length, axis=dim)
        leading = lax.slice_in_dim(shard, 0, width, axis=dim)
        edges[dim] = (
            lax.ppermute(last, axis, up),
            lax.ppermute(leading, axis, [(b, a) for a, b in up]),
        )
    done = []
    for _, dim in sides:
        low, high = edges[dim]
        around = [(width, width) if d in done else (0, 0) for d in range(shard.ndim)]
        shard = jnp.concatenate([jnp.pad(low, around), shard, jnp.pad(high, around)], axis=dim)
        done.append(dim)
    return shard


def copy_for_each(shard, axis):
    size = lax.axis_size(axis)
    return lax.all_to_all(
        jnp.broadcast_to(shard[None], (size, *shard.shape)), axis, 0, 0, tiled=True
    )


def in_order(blocks, dim):
    dims = list(blocks.shape[1:])
    dims[dim] *= blocks.shape[0]
    return jnp.moveaxis(blocks, 0, dim).reshape(dims)


def collect(shard, axis, dim):
    blocks = copy_for_each(shard, axis)
    return in_order(blocks, dim)


def side_by_side(arrays, axis, dim, along):
    ends, at = ([], 0)
    for a in arrays[:-1]:
        at += a.shape[along]
        ends.append(at)
    both = jnp.concatenate(arrays, axis=along)
    return tuple(jnp.split(collect(both, axis, dim), ends, axis=along))


def in_blocks(shard, dim, size):
    before, after = (shard.shape[:dim], shard.shape[dim + 1 :])
    return jnp.moveaxis(shard.reshape(*before, size, -1, *after), dim, 0)


def sent_and_summed(shard, axis, dim):
    blocks = in_blocks(shard, dim, lax.axis_size(axis))
    arrived = lax.all_to_all(blocks, axis, split_axis=0, concat_axis=0, tiled=True)
    return arrived.sum(axis=0)


def in_one_piece(arrays, axis, dim, along):
    both = jnp.concatenate(arrays, axis=along)
    result, at, done = (sent_and_summed(both, axis, dim), 0, [])
    for a in arrays:
        done.append(lax.slice_in_dim(result, at, at + a.shape[along], axis=along))
        at += a.shape[along]
    return tuple(done)


def lap_rows(padded):
    center = padded[..., 1:-1, :]
    widths = ((0, 0),) * (center.ndim - 1) + ((1, 1),)
    sideways = jnp.pad(center, widths)
    return (
        padded[..., :-2, :]
        + padded[..., 2:, :]
        + sideways[..., :-2]
        + sideways[..., 2:]
        - 4.0 * center
    )


def incident_wave(angles, row_ids, total_rows, total_cols):
    column_ids = jnp.arange(total_cols, dtype=jnp.int32)
    row_turns = angles[:, 0][:, None, None]
    col_turns = angles[:, 1][:, None, None]
    fraction = (
        jnp.mod(row_turns * row_ids[None, :, None], total_rows).astype(jnp.float32) / total_rows
        + jnp.mod(col_turns * column_ids[None, None, :], total_cols).astype(jnp.float32)
        / total_cols
    )
    phase_angle = 2.0 * math.pi * fraction
    return jnp.stack((jnp.cos(phase_angle), jnp.sin(phase_angle)), axis=1)


def complex_times(pair, fields):
    trans_real, trans_imag = pair
    return jnp.stack(
        (
            trans_real * fields[:, 0] - trans_imag * fields[:, 1],
            trans_real * fields[:, 1] + trans_imag * fields[:, 0],
        ),
        axis=1,
    )


def conj_times(pair, fields):
    trans_real, trans_imag = pair
    return jnp.stack(
        (
            trans_real * fields[:, 0] + trans_imag * fields[:, 1],
            trans_real * fields[:, 1] - trans_imag * fields[:, 0],
        ),
        axis=1,
    )


def body(phase_delay, attenuation, measured, angles):
    n_cuts = lax.axis_size("cuts")
    cut_index = lax.axis_index("cuts")
    slab_index = lax.axis_index("slab")
    slab_rows = measured.shape[2]
    n_cols = measured.shape[3]
    total_rows = slab_rows * lax.axis_size("slab")
    n_rows = slab_rows // n_cuts
    row_start = (slab_index * n_cuts + cut_index) * n_rows
    local_phase, local_atten = sent_together((phase_delay, attenuation), "cuts", 1, 0, 2)
    measured_here = lax.dynamic_slice_in_dim(measured, cut_index * n_rows, n_rows, 2)
    slices_here = local_phase.shape[0]
    row_ids = row_start + jnp.arange(n_rows, dtype=jnp.int32)
    start_fields = incident_wave(angles, row_ids, total_rows, n_cols)

    def stencil(fields):
        padded = padded_2(fields, ((("slab", "cuts"), 2),), 2)
        wide_once = lap_rows(padded)
        wide_ids = row_start + jnp.arange(n_rows + 2, dtype=jnp.int32) - 1
        inside = (wide_ids >= 0) & (wide_ids < total_rows)
        wide_once = jnp.where(inside[:, None], wide_once, 0.0)
        laplace_one = wide_once[:, :, 1:-1]
        laplace_two = lap_rows(wide_once)
        return (laplace_one, laplace_two)

    def diffract(fields, orient):
        laplace_one, laplace_two = stencil(fields)
        real_part = (
            fields[:, 0]
            - orient * step_coeff * laplace_one[:, 1]
            - square_coeff * laplace_two[:, 0]
        )
        imag_part = (
            fields[:, 1]
            + orient * step_coeff * laplace_one[:, 0]
            - square_coeff * laplace_two[:, 1]
        )
        return jnp.stack((real_part, imag_part), axis=1)

    whole_phase, whole_atten = side_by_side((local_phase, local_atten), "illum", 2, 0)
    transmit = []
    for layer_index in range(slices_here):
        damping = jnp.exp(-whole_atten[layer_index])
        transmit.append(
            (
                damping * jnp.cos(whole_phase[layer_index]),
                damping * jnp.sin(whole_phase[layer_index]),
            )
        )
    phase_list = [None] * slices_here
    atten_list = [None] * slices_here

    def record(layer_index, passed, weighted):
        phase_part = -jnp.sum(passed[:, 1] * weighted[:, 0] - passed[:, 0] * weighted[:, 1], axis=0)
        atten_part = -jnp.sum(passed[:, 0] * weighted[:, 0] + passed[:, 1] * weighted[:, 1], axis=0)
        phase_list[layer_index] = phase_part
        atten_list[layer_index] = atten_part

    fields = start_fields
    stored = []
    for layer_index in range(slices_here):
        passed = complex_times(transmit[layer_index], fields)
        stored.append(passed)
        fields = diffract(passed, 1.0)
    adjoint = fields - measured_here
    for layer_index in reversed(range(slices_here)):
        weighted = diffract(adjoint, -1.0)
        record(layer_index, stored[layer_index], weighted)
        adjoint = conj_times(transmit[layer_index], weighted)
    grad_phase, grad_atten = in_one_piece(
        (jnp.stack(phase_list), jnp.stack(atten_list)), "illum", 2, 0
    )
    grad_phase, grad_atten = sent_together((grad_phase, grad_atten), "cuts", 0, 1, 2)
    return (grad_phase, grad_atten)


def solution(mesh):
    placed = (
        P("cuts", "slab", "illum"),
        P("cuts", "slab", "illum"),
        P("illum", None, "slab", None),
        P("illum", None),
    )
    return jax.shard_map(
        body,
        mesh=mesh,
        in_specs=placed,
        out_specs=(P("cuts", "slab", "illum"), P("cuts", "slab", "illum")),
        check_vma=False,
    )
```

profile of v0, /device:TPU:2, one launch (start us, length us, event | category | flops | bytes accessed | tf_op | source)
XLA Modules:
  0.0 199.6 jit_solution(14299081106411046641)
XLA Ops:
  2.4 6.5 %all_to_all.46 = f32[2,1,2048]{2,1,0:T(1,128)S(1)} all-to-all(f32[2,1,2048]{2,1,0:T(1,128)S(1)} %reshape.2659), channel_id=1, replica_groups=mesh['illum'=32,'slab'=8,'cuts'=2] {'cuts'}, dimensions={0} | all-to-all | bytes 32768 | tf_op jit(solution)/shard_map/all_to_all | solution.py:15
  10.7 1.7 reshape.2661
  12.4 15.7 %all-to-all-start.1 = ((f32[32,1,4096]{2,1,0:T(1,128)}), f32[32,1,4096]{2,1,0:T(1,128)S(1)}, u32[]{:S(2)}, u32[]{:S(2)}) async-start(f32[32,1,4096]{2,1,0:T(1,128)} %reshape.2661), calls=%async_computation.1 | async-start | bytes 1048576 | tf_op jit(solution)/shard_map/all_to_all | solution.py:41
  30.0 17.2 %all-to-all-done.1 = f32[32,1,4096]{2,1,0:T(1,128)S(1)} async-done(((f32[32,1,4096]{2,1,0:T(1,128)}), f32[32,1,4096]{2,1,0:T(1,128)S(1)}, u32[]{:S(2)}, u32[]{:S(2)}) %all-to-all-start.1) | async-done | bytes 524320 | tf_op jit(solution)/shard_map/all_to_all | solution.py:41
  47.2 1.9 reduce.1
  51.1 3.8 %cosine_multiply_fusion.3 = (f32[1,16,32,32]{3,2,1,0:T(8,128)S(1)}, f32[1,16,32,32]{3,2,1,0:T(8,128)S(1)}, f32[1,16,32,32]{3,2,1,0:T(8,128)S(1)}, f32[1,16,32,32...) fusion(f32[8,16,32,32]{3,2,1,0:T(8,128)S(1)} %bitcast.85), kind=kLoop, calls=%fused_computation.47 | loop fusion | flops 196608 | bytes 1048576 | tf_op jit(solution)/shard_map/mul | solution.py:179
  55.6 1.9 collective-permute-start
  57.5 4.5 %collective-permute-start.1 = (f32[1,2,2,1024]{3,2,1,0:T(2,128)S(1)}, f32[1,2,2,1024]{3,2,1,0:T(2,128)S(1)}, u32[]{:S(2)}, u32[]{:S(2)}) collective-permute-start(f32[1,2,2,1024]{3,2,1,0:T(2,128)S(1)} %get-tuple-element.84), channel_id=1, source_target_pairs={{1,0},{2,1},{3,2},{4,3},{5,4},{6,5},{7,6},{8,7},{9,8},{10,9},{11,1... | collective-permute-start | bytes 49160 | tf_op jit(solution)/shard_map/ppermute | solution.py:28
  63.9 1.9 collective-permute-start.2
  65.8 4.5 %collective-permute-start.3 = (f32[1,2,2,1024]{3,2,1,0:T(2,128)S(1)}, f32[1,2,2,1024]{3,2,1,0:T(2,128)S(1)}, u32[]{:S(2)}, u32[]{:S(2)}) collective-permute-start(f32[1,2,2,1024]{3,2,1,0:T(2,128)S(1)} %get-tuple-element.82), channel_id=1, source_target_pairs={{1,0},{2,1},{3,2},{4,3},{5,4},{6,5},{7,6},{8,7},{9,8},{10,9},{11,1... | collective-permute-start | bytes 49160 | tf_op jit(solution)/shard_map/ppermute | solution.py:28
  72.3 3.6 %collective-permute-start.4 = (f32[1,2,2,1024]{3,2,1,0:T(2,128)S(1)}, f32[1,2,2,1024]{3,2,1,0:T(2,128)S(1)}, u32[]{:S(2)}, u32[]{:S(2)}) collective-permute-start(f32[1,2,2,1024]{3,2,1,0:T(2,128)S(1)} %get-tuple-element.79), channel_id=1, source_target_pairs={{0,1},{1,2},{2,3},{3,4},{4,5},{5,6},{6,7},{7,8},{8,9},{9,10},{10,1... | collective-permute-start | bytes 49160 | tf_op jit(solution)/shard_map/ppermute | solution.py:27
  75.9 2.8 %collective-permute-start.5 = (f32[1,2,2,1024]{3,2,1,0:T(2,128)S(1)}, f32[1,2,2,1024]{3,2,1,0:T(2,128)S(1)}, u32[]{:S(2)}, u32[]{:S(2)}) collective-permute-start(f32[1,2,2,1024]{3,2,1,0:T(2,128)S(1)} %get-tuple-element.80), channel_id=1, source_target_pairs={{1,0},{2,1},{3,2},{4,3},{5,4},{6,5},{7,6},{8,7},{9,8},{10,9},{11,1... | collective-permute-start | bytes 49160 | tf_op jit(solution)/shard_map/ppermute | solution.py:28
  79.1 2.6 %collective-permute-done.5 = f32[1,2,2,1024]{3,2,1,0:T(2,128)S(1)} collective-permute-done((f32[1,2,2,1024]{3,2,1,0:T(2,128)S(1)}, f32[1,2,2,1024]{3,2,1,0:T(2,128)S(1)}, u32[]{:S(2)}, u32[]{:S(2)}) %collective-permute-start.5) | collective-permute-done | bytes 16416 | tf_op jit(solution)/shard_map/ppermute | solution.py:28
  82.7 2.4 %collective-permute-start.6 = (f32[1,2,2,1024]{3,2,1,0:T(2,128)S(1)}, f32[1,2,2,1024]{3,2,1,0:T(2,128)S(1)}, u32[]{:S(2)}, u32[]{:S(2)}) collective-permute-start(f32[1,2,2,1024]{3,2,1,0:T(2,128)S(1)} %get-tuple-element.77), channel_id=1, source_target_pairs={{0,1},{1,2},{2,3},{3,4},{4,5},{5,6},{6,7},{7,8},{8,9},{9,10},{10,1... | collective-permute-start | bytes 49160 | tf_op jit(solution)/shard_map/ppermute | solution.py:27
  85.1 4.1 %collective-permute-start.7 = (f32[1,2,2,1024]{3,2,1,0:T(2,128)S(1)}, f32[1,2,2,1024]{3,2,1,0:T(2,128)S(1)}, u32[]{:S(2)}, u32[]{:S(2)}) collective-permute-start(f32[1,2,2,1024]{3,2,1,0:T(2,128)S(1)} %get-tuple-element.78), channel_id=1, source_target_pairs={{1,0},{2,1},{3,2},{4,3},{5,4},{6,5},{7,6},{8,7},{9,8},{10,9},{11,1... | collective-permute-start | bytes 49160 | tf_op jit(solution)/shard_map/ppermute | solution.py:28
  91.3 2.6 %collective-permute-start.8 = (f32[1,2,2,1024]{3,2,1,0:T(2,128)S(1)}, f32[1,2,2,1024]{3,2,1,0:T(2,128)S(1)}, u32[]{:S(2)}, u32[]{:S(2)}) collective-permute-start(f32[1,2,2,1024]{3,2,1,0:T(2,128)S(1)} %get-tuple-element.75), channel_id=1, source_target_pairs={{0,1},{1,2},{2,3},{3,4},{4,5},{5,6},{6,7},{7,8},{8,9},{9,10},{10,1... | collective-permute-start | bytes 49160 | tf_op jit(solution)/shard_map/ppermute | solution.py:27
  93.9 3.9 %collective-permute-start.9 = (f32[1,2,2,1024]{3,2,1,0:T(2,128)S(1)}, f32[1,2,2,1024]{3,2,1,0:T(2,128)S(1)}, u32[]{:S(2)}, u32[]{:S(2)}) collective-permute-start(f32[1,2,2,1024]{3,2,1,0:T(2,128)S(1)} %get-tuple-element.76), channel_id=1, source_target_pairs={{1,0},{2,1},{3,2},{4,3},{5,4},{6,5},{7,6},{8,7},{9,8},{10,9},{11,1... | collective-permute-start | bytes 49160 | tf_op jit(solution)/shard_map/ppermute | solution.py:28
  97.7 1.8 collective-permute-done.9
  100.0 2.9 %collective-permute-start.10 = (f32[1,2,2,1024]{3,2,1,0:T(2,128)S(1)}, f32[1,2,2,1024]{3,2,1,0:T(2,128)S(1)}, u32[]{:S(2)}, u32[]{:S(2)}) collective-permute-start(f32[1,2,2,1024]{3,2,1,0:T(2,128)S(1)} %get-tuple-element.73), channel_id=1, source_target_pairs={{0,1},{1,2},{2,3},{3,4},{4,5},{5,6},{6,7},{7,8},{8,9},{9,10},{10,1... | collective-permute-start | bytes 49160 | tf_op jit(solution)/shard_map/ppermute | solution.py:27
  102.9 3.5 %collective-permute-start.11 = (f32[1,2,2,1024]{3,2,1,0:T(2,128)S(1)}, f32[1,2,2,1024]{3,2,1,0:T(2,128)S(1)}, u32[]{:S(2)}, u32[]{:S(2)}) collective-permute-start(f32[1,2,2,1024]{3,2,1,0:T(2,128)S(1)} %get-tuple-element.74), channel_id=1, source_target_pairs={{1,0},{2,1},{3,2},{4,3},{5,4},{6,5},{7,6},{8,7},{9,8},{10,9},{11,1... | collective-permute-start | bytes 49160 | tf_op jit(solution)/shard_map/ppermute | solution.py:28
  106.5 2.1 %collective-permute-done.11 = f32[1,2,2,1024]{3,2,1,0:T(2,128)S(1)} collective-permute-done((f32[1,2,2,1024]{3,2,1,0:T(2,128)S(1)}, f32[1,2,2,1024]{3,2,1,0:T(2,128)S(1)}, u32[]{:S(2)}, u32[]{:S(2)}) %collective-permute-start.11) | collective-permute-done | bytes 16416 | tf_op jit(solution)/shard_map/ppermute | solution.py:28
  109.7 2.5 %collective-permute-start.12 = (f32[1,2,2,1024]{3,2,1,0:T(2,128)S(1)}, f32[1,2,2,1024]{3,2,1,0:T(2,128)S(1)}, u32[]{:S(2)}, u32[]{:S(2)}) collective-permute-start(f32[1,2,2,1024]{3,2,1,0:T(2,128)S(1)} %get-tuple-element.71), channel_id=1, source_target_pairs={{0,1},{1,2},{2,3},{3,4},{4,5},{5,6},{6,7},{7,8},{8,9},{9,10},{10,1... | collective-permute-start | bytes 49160 | tf_op jit(solution)/shard_map/ppermute | solution.py:27
  112.2 3.9 %collective-permute-start.13 = (f32[1,2,2,1024]{3,2,1,0:T(2,128)S(1)}, f32[1,2,2,1024]{3,2,1,0:T(2,128)S(1)}, u32[]{:S(2)}, u32[]{:S(2)}) collective-permute-start(f32[1,2,2,1024]{3,2,1,0:T(2,128)S(1)} %get-tuple-element.72), channel_id=1, source_target_pairs={{1,0},{2,1},{3,2},{4,3},{5,4},{6,5},{7,6},{8,7},{9,8},{10,9},{11,1... | collective-permute-start | bytes 49160 | tf_op jit(solution)/shard_map/ppermute | solution.py:28
  119.7 2.5 %collective-permute-start.14 = (f32[1,2,2,1024]{3,2,1,0:T(2,128)}, f32[1,2,2,1024]{3,2,1,0:T(2,128)}, u32[]{:S(2)}, u32[]{:S(2)}) collective-permute-start(f32[1,2,2,1024]{3,2,1,0:T(2,128)} %get-tuple-element.69), channel_id=1, source_target_pairs={{0,1},{1,2},{2,3},{3,4},{4,5},{5,6},{6,7},{7,8},{8,9},{9,10},{10,1... | collective-permute-start | bytes 49160 | tf_op jit(solution)/shard_map/ppermute | solution.py:27
  122.2 4.2 %collective-permute-start.15 = (f32[1,2,2,1024]{3,2,1,0:T(2,128)}, f32[1,2,2,1024]{3,2,1,0:T(2,128)}, u32[]{:S(2)}, u32[]{:S(2)}) collective-permute-start(f32[1,2,2,1024]{3,2,1,0:T(2,128)} %get-tuple-element.70), channel_id=1, source_target_pairs={{1,0},{2,1},{3,2},{4,3},{5,4},{6,5},{7,6},{8,7},{9,8},{10,9},{11,1... | collective-permute-start | bytes 49160 | tf_op jit(solution)/shard_map/ppermute | solution.py:28
  145.8 1.7 mul.3026
  151.7 1.7 mul.3034
  153.4 1.7 mul.3044
  155.1 2.9 %negate_dynamic-update-slice_fusion.7 = (f32[8,16,32,32]{3,2,1,0:T(8,128)S(1)}, f32[1,16,32,32]{3,2,1,0:T(8,128)S(1)}, f32[1,16,32,32]{3,2,1,0:T(8,128)S(1)}, f3...) fusion(f32[1,16,32,32]{3,2,1,0:T(8,128)} %mul.3037, ...), kind=kLoop, calls=%fused_computation.28 | loop fusion | flops 688127 | bytes 3805248
  162.6 22.0 %all_to_all.47 = f32[32,1,4096]{2,1,0:T(1,128)S(1)} all-to-all(f32[32,1,4096]{2,1,0:T(1,128)S(1)} %reshape.2663), channel_id=1, replica_groups=mesh['illum'=32,'slab'=8,'cuts'=2] {'illum'}, dimensions={0} | all-to-all | bytes 1048576 | tf_op jit(solution)/shard_map/all_to_all | solution.py:73
  184.6 1.9 reduce.2
  187.6 10.5 %all_to_all.48 = f32[2,1,2048]{2,1,0:T(1,128)S(1)} all-to-all(f32[2,1,2048]{2,1,0:T(1,128)S(1)} %reshape.2665), channel_id=1, replica_groups=mesh['illum'=32,'slab'=8,'cuts'=2] {'cuts'}, dimensions={0} | all-to-all | bytes 32768 | tf_op jit(solution)/shard_map/all_to_all | solution.py:15
  (169 shorter events, 50.5 us)
Async XLA Ops:
  10.7 17.4 %copy-start.17 = (s32[1,2]{1,0:T(1,128)S(1)}, s32[1,2]{1,0:T(1,128)}, u32[]{:S(2)}) copy-start(s32[1,2]{1,0:T(1,128)} %param.7) | copy-start | bytes 28
  12.4 34.8 %all-to-all-start.1 = ((f32[32,1,4096]{2,1,0:T(1,128)}), f32[32,1,4096]{2,1,0:T(1,128)S(1)}, u32[]{:S(2)}, u32[]{:S(2)}) async-start(f32[32,1,4096]{2,1,0:T(1,128)} %reshape.2661), calls=%async_computation.1 | async-start | bytes 1048576 | tf_op jit(solution)/shard_map/all_to_all | solution.py:41
  29.4 25.8 %copy-start.16 = (f32[16]{0:T(128)}, f32[16]{0:T(128)S(1)}, u32[]{:S(2)}) copy-start(f32[16]{0:T(128)S(1)} %fusion.82) | copy-start | bytes 196
  55.6 6.8 %collective-permute-start = (f32[1,2,2,1024]{3,2,1,0:T(2,128)S(1)}, f32[1,2,2,1024]{3,2,1,0:T(2,128)S(1)}, u32[]{:S(2)}, u32[]{:S(2)}) collective-permute-start(f32[1,2,2,1024]{3,2,1,0:T(2,128)S(1)} %get-tuple-element.83), channel_id=1, source_target_pairs={{0,1},{1,2},{2,3},{3,4},{4,5},{5,6},{6,7},{7,8},{8,9},{9,10},{10,1... | collective-permute-start | bytes 49160 | tf_op jit(solution)/shard_map/ppermute | solution.py:27
  57.5 6.0 %collective-permute-start.1 = (f32[1,2,2,1024]{3,2,1,0:T(2,128)S(1)}, f32[1,2,2,1024]{3,2,1,0:T(2,128)S(1)}, u32[]{:S(2)}, u32[]{:S(2)}) collective-permute-start(f32[1,2,2,1024]{3,2,1,0:T(2,128)S(1)} %get-tuple-element.84), channel_id=1, source_target_pairs={{1,0},{2,1},{3,2},{4,3},{5,4},{6,5},{7,6},{8,7},{9,8},{10,9},{11,1... | collective-permute-start | bytes 49160 | tf_op jit(solution)/shard_map/ppermute | solution.py:28
  62.1 55.9 %copy-start.15 = (pred[18]{0:T(512)(128)(4,1)}, pred[18]{0:T(512)(128)(4,1)S(1)}, u32[]{:S(2)}) copy-start(pred[18]{0:T(512)(128)(4,1)S(1)} %compare_and_fusion) | copy-start | bytes 58
  63.9 6.8 %collective-permute-start.2 = (f32[1,2,2,1024]{3,2,1,0:T(2,128)S(1)}, f32[1,2,2,1024]{3,2,1,0:T(2,128)S(1)}, u32[]{:S(2)}, u32[]{:S(2)}) collective-permute-start(f32[1,2,2,1024]{3,2,1,0:T(2,128)S(1)} %get-tuple-element.81), channel_id=1, source_target_pairs={{0,1},{1,2},{2,3},{3,4},{4,5},{5,6},{6,7},{7,8},{8,9},{9,10},{10,1... | collective-permute-start | bytes 49160 | tf_op jit(solution)/shard_map/ppermute | solution.py:27
  65.8 6.0 %collective-permute-start.3 = (f32[1,2,2,1024]{3,2,1,0:T(2,128)S(1)}, f32[1,2,2,1024]{3,2,1,0:T(2,128)S(1)}, u32[]{:S(2)}, u32[]{:S(2)}) collective-permute-start(f32[1,2,2,1024]{3,2,1,0:T(2,128)S(1)} %get-tuple-element.82), channel_id=1, source_target_pairs={{1,0},{2,1},{3,2},{4,3},{5,4},{6,5},{7,6},{8,7},{9,8},{10,9},{11,1... | collective-permute-start | bytes 49160 | tf_op jit(solution)/shard_map/ppermute | solution.py:28
  72.3 6.8 %collective-permute-start.4 = (f32[1,2,2,1024]{3,2,1,0:T(2,128)S(1)}, f32[1,2,2,1024]{3,2,1,0:T(2,128)S(1)}, u32[]{:S(2)}, u32[]{:S(2)}) collective-permute-start(f32[1,2,2,1024]{3,2,1,0:T(2,128)S(1)} %get-tuple-element.79), channel_id=1, source_target_pairs={{0,1},{1,2},{2,3},{3,4},{4,5},{5,6},{6,7},{7,8},{8,9},{9,10},{10,1... | collective-permute-start | bytes 49160 | tf_op jit(solution)/shard_map/ppermute | solution.py:27
  75.9 5.7 %collective-permute-start.5 = (f32[1,2,2,1024]{3,2,1,0:T(2,128)S(1)}, f32[1,2,2,1024]{3,2,1,0:T(2,128)S(1)}, u32[]{:S(2)}, u32[]{:S(2)}) collective-permute-start(f32[1,2,2,1024]{3,2,1,0:T(2,128)S(1)} %get-tuple-element.80), channel_id=1, source_target_pairs={{1,0},{2,1},{3,2},{4,3},{5,4},{6,5},{7,6},{8,7},{9,8},{10,9},{11,1... | collective-permute-start | bytes 49160 | tf_op jit(solution)/shard_map/ppermute | solution.py:28
  82.7 6.5 %collective-permute-start.6 = (f32[1,2,2,1024]{3,2,1,0:T(2,128)S(1)}, f32[1,2,2,1024]{3,2,1,0:T(2,128)S(1)}, u32[]{:S(2)}, u32[]{:S(2)}) collective-permute-start(f32[1,2,2,1024]{3,2,1,0:T(2,128)S(1)} %get-tuple-element.77), channel_id=1, source_target_pairs={{0,1},{1,2},{2,3},{3,4},{4,5},{5,6},{6,7},{7,8},{8,9},{9,10},{10,1... | collective-permute-start | bytes 49160 | tf_op jit(solution)/shard_map/ppermute | solution.py:27
  85.1 5.6 %collective-permute-start.7 = (f32[1,2,2,1024]{3,2,1,0:T(2,128)S(1)}, f32[1,2,2,1024]{3,2,1,0:T(2,128)S(1)}, u32[]{:S(2)}, u32[]{:S(2)}) collective-permute-start(f32[1,2,2,1024]{3,2,1,0:T(2,128)S(1)} %get-tuple-element.78), channel_id=1, source_target_pairs={{1,0},{2,1},{3,2},{4,3},{5,4},{6,5},{7,6},{8,7},{9,8},{10,9},{11,1... | collective-permute-start | bytes 49160 | tf_op jit(solution)/shard_map/ppermute | solution.py:28
  89.2 2.0 copy-start.14
  91.3 6.5 %collective-permute-start.8 = (f32[1,2,2,1024]{3,2,1,0:T(2,128)S(1)}, f32[1,2,2,1024]{3,2,1,0:T(2,128)S(1)}, u32[]{:S(2)}, u32[]{:S(2)}) collective-permute-start(f32[1,2,2,1024]{3,2,1,0:T(2,128)S(1)} %get-tuple-element.75), channel_id=1, source_target_pairs={{0,1},{1,2},{2,3},{3,4},{4,5},{5,6},{6,7},{7,8},{8,9},{9,10},{10,1... | collective-permute-start | bytes 49160 | tf_op jit(solution)/shard_map/ppermute | solution.py:27
  93.9 5.6 %collective-permute-start.9 = (f32[1,2,2,1024]{3,2,1,0:T(2,128)S(1)}, f32[1,2,2,1024]{3,2,1,0:T(2,128)S(1)}, u32[]{:S(2)}, u32[]{:S(2)}) collective-permute-start(f32[1,2,2,1024]{3,2,1,0:T(2,128)S(1)} %get-tuple-element.76), channel_id=1, source_target_pairs={{1,0},{2,1},{3,2},{4,3},{5,4},{6,5},{7,6},{8,7},{9,8},{10,9},{11,1... | collective-permute-start | bytes 49160 | tf_op jit(solution)/shard_map/ppermute | solution.py:28
  100.0 6.5 %collective-permute-start.10 = (f32[1,2,2,1024]{3,2,1,0:T(2,128)S(1)}, f32[1,2,2,1024]{3,2,1,0:T(2,128)S(1)}, u32[]{:S(2)}, u32[]{:S(2)}) collective-permute-start(f32[1,2,2,1024]{3,2,1,0:T(2,128)S(1)} %get-tuple-element.73), channel_id=1, source_target_pairs={{0,1},{1,2},{2,3},{3,4},{4,5},{5,6},{6,7},{7,8},{8,9},{9,10},{10,1... | collective-permute-start | bytes 49160 | tf_op jit(solution)/shard_map/ppermute | solution.py:27
  102.9 5.6 %collective-permute-start.11 = (f32[1,2,2,1024]{3,2,1,0:T(2,128)S(1)}, f32[1,2,2,1024]{3,2,1,0:T(2,128)S(1)}, u32[]{:S(2)}, u32[]{:S(2)}) collective-permute-start(f32[1,2,2,1024]{3,2,1,0:T(2,128)S(1)} %get-tuple-element.74), channel_id=1, source_target_pairs={{1,0},{2,1},{3,2},{4,3},{5,4},{6,5},{7,6},{8,7},{9,8},{10,9},{11,1... | collective-permute-start | bytes 49160 | tf_op jit(solution)/shard_map/ppermute | solution.py:28
  109.7 6.5 %collective-permute-start.12 = (f32[1,2,2,1024]{3,2,1,0:T(2,128)S(1)}, f32[1,2,2,1024]{3,2,1,0:T(2,128)S(1)}, u32[]{:S(2)}, u32[]{:S(2)}) collective-permute-start(f32[1,2,2,1024]{3,2,1,0:T(2,128)S(1)} %get-tuple-element.71), channel_id=1, source_target_pairs={{0,1},{1,2},{2,3},{3,4},{4,5},{5,6},{6,7},{7,8},{8,9},{9,10},{10,1... | collective-permute-start | bytes 49160 | tf_op jit(solution)/shard_map/ppermute | solution.py:27
  112.2 5.6 %collective-permute-start.13 = (f32[1,2,2,1024]{3,2,1,0:T(2,128)S(1)}, f32[1,2,2,1024]{3,2,1,0:T(2,128)S(1)}, u32[]{:S(2)}, u32[]{:S(2)}) collective-permute-start(f32[1,2,2,1024]{3,2,1,0:T(2,128)S(1)} %get-tuple-element.72), channel_id=1, source_target_pairs={{1,0},{2,1},{3,2},{4,3},{5,4},{6,5},{7,6},{8,7},{9,8},{10,9},{11,1... | collective-permute-start | bytes 49160 | tf_op jit(solution)/shard_map/ppermute | solution.py:28
  118.1 15.5 %copy-start.12 = (f32[1,1,16,1024]{3,2,1,0:T(8,128)S(1)}, f32[1,1,16,1024]{3,2,1,0:T(8,128)}, u32[]{:S(2)}) copy-start(f32[1,1,16,1024]{3,2,1,0:T(8,128)} %get-tuple-element.43) | copy-start | bytes 196612
  119.7 27.8 %collective-permute-start.14 = (f32[1,2,2,1024]{3,2,1,0:T(2,128)}, f32[1,2,2,1024]{3,2,1,0:T(2,128)}, u32[]{:S(2)}, u32[]{:S(2)}) collective-permute-start(f32[1,2,2,1024]{3,2,1,0:T(2,128)} %get-tuple-element.69), channel_id=1, source_target_pairs={{0,1},{1,2},{2,3},{3,4},{4,5},{5,6},{6,7},{7,8},{8,9},{9,10},{10,1... | collective-permute-start | bytes 49160 | tf_op jit(solution)/shard_map/ppermute | solution.py:27
  122.2 25.4 %collective-permute-start.15 = (f32[1,2,2,1024]{3,2,1,0:T(2,128)}, f32[1,2,2,1024]{3,2,1,0:T(2,128)}, u32[]{:S(2)}, u32[]{:S(2)}) collective-permute-start(f32[1,2,2,1024]{3,2,1,0:T(2,128)} %get-tuple-element.70), channel_id=1, source_target_pairs={{1,0},{2,1},{3,2},{4,3},{5,4},{6,5},{7,6},{8,7},{9,8},{10,9},{11,1... | collective-permute-start | bytes 49160 | tf_op jit(solution)/shard_map/ppermute | solution.py:28
  127.8 9.4 %copy-start.13 = (f32[1,1,16,1024]{3,2,1,0:T(8,128)S(1)}, f32[1,1,16,1024]{3,2,1,0:T(8,128)}, u32[]{:S(2)}) copy-start(f32[1,1,16,1024]{3,2,1,0:T(8,128)} %get-tuple-element.50) | copy-start | bytes 196612
  155.1 3.0 %copy-start.7 = (f32[1,16,32,32]{3,2,1,0:T(8,128)S(1)}, f32[1,16,32,32]{3,2,1,0:T(8,128)}, u32[]{:S(2)}) copy-start(f32[1,16,32,32]{3,2,1,0:T(8,128)} %mul.3048) | copy-start | bytes 196612
  155.1 3.0 %copy-start.8 = (f32[1,16,32,32]{3,2,1,0:T(8,128)S(1)}, f32[1,16,32,32]{3,2,1,0:T(8,128)}, u32[]{:S(2)}) copy-start(f32[1,16,32,32]{3,2,1,0:T(8,128)} %mul.3049) | copy-start | bytes 196612
  155.1 3.0 %copy-start.10 = (f32[1,16,32,32]{3,2,1,0:T(8,128)S(1)}, f32[1,16,32,32]{3,2,1,0:T(8,128)}, u32[]{:S(2)}) copy-start(f32[1,16,32,32]{3,2,1,0:T(8,128)} %mul.3051) | copy-start | bytes 196612
  155.1 3.0 %copy-start.11 = (f32[1,16,32,32]{3,2,1,0:T(8,128)S(1)}, f32[1,16,32,32]{3,2,1,0:T(8,128)}, u32[]{:S(2)}) copy-start(f32[1,16,32,32]{3,2,1,0:T(8,128)} %mul.3052) | copy-start | bytes 196612
  158.1 1.2 copy-start.9
  158.4 1.1 copy-start
  158.4 1.1 copy-start.1
  158.5 1.2 copy-start.2
  158.5 1.2 copy-start.5
  (3 other events, 3.1 us)
where the time goes:
time: 201 us; the launch traced here: 200 us
  starting transfers between devices  67.5 us (34%)
  blocking collectives  39 us (19%)
  local copies, waits for them, and re-layouts  38.4 us (19%)
  waiting for transfers between devices  29.1 us (14%)
  other arithmetic  24 us (12%)
    ppermute x8, starting transfers between devices, padded_2(): lax.ppermute(leading, axis, [(b, a) for a, b in up])  31.5 us
    all_to_all x1, blocking collectives, sent_and_summed(): lax.all_to_all(blocks, axis, split_axis=0, concat_axis=0, tiled=True)  22 us
    ppermute x8, starting transfers between devices, padded_2(): lax.ppermute(last, axis, up)  20.4 us
    all_to_all x1, waiting for transfers between devices, copy_for_each(): lax.all_to_all(jnp.broadcast_to(shard[None], (size, *shard.shape)), axis,...  17.2 us
    all_to_all x2, blocking collectives, sent_together(): lax.all_to_all(both, axis, split_axis=split_dim, concat_axis=concat_dim,...  17 us
    all_to_all x1, starting transfers between devices, copy_for_each(): lax.all_to_all(jnp.broadcast_to(shard[None], (size, *shard.shape)), axis,...  15.7 us
    ppermute x8, waiting for transfers between devices, padded_2(): lax.ppermute(leading, axis, [(b, a) for a, b in up])  11.9 us
    unnamed x46, local copies, waits for them, and re-layouts  6.9 us
  transfers between devices with their start and end apart: 17, of which 8 were waited for; matrix products, arithmetic and copies ran while one was open for 12% of the time, Pallas kernels for 0%

commit v1 on v0

v1 whole, which is shorter than its diff:
```python
import functools
import math

import jax
import jax.numpy as jnp
from jax import lax
from jax.experimental import pallas as pl
from jax.experimental.pallas import tpu as pltpu
from jax.sharding import PartitionSpec as P

step_coeff = 0.08
square_coeff = 0.0032
ratio = step_coeff / square_coeff
two_pi = 2.0 * math.pi

HALO = 8
REACH = 16
VMEM = pl.BlockSpec(memory_space=pltpu.VMEM)
SMEM = pl.BlockSpec(memory_space=pltpu.SMEM)
small = pltpu.CompilerParams(vmem_limit_bytes=1 << 20)
large = pltpu.CompilerParams(vmem_limit_bytes=8 << 20)


def f32(*shape):
    return jax.ShapeDtypeStruct(shape, jnp.float32)


def lanes_of(shape):
    return lax.broadcasted_iota(jnp.int32, shape, 1)


def turn(x, by):
    by %= 128
    return pltpu.roll(x, by, 1) if by else x


def pack_object(phase_ref, atten_ref, out_ref):
    for n, (ref, layer) in enumerate(
        ((phase_ref, 0), (phase_ref, 1), (atten_ref, 0), (atten_ref, 1))
    ):
        out_ref[:, 32 * n : 32 * n + 32] = ref[layer]


def pack_edges(ids_ref, mine_ref, other_ref, out_ref):
    first = ids_ref[2] == 0
    for pair, (a, b) in enumerate(((mine_ref, other_ref), (other_ref, mine_ref))):
        out_ref[pair] = jnp.where(
            first, jnp.where(first, a[0:8], b[0:8]), jnp.where(first, a[24:32], b[24:32])
        )


def pack_rows(ids_ref, mine_ref, other_ref, edge_ref, out_ref):
    first = ids_ref[2] == 0
    for pair in range(2):
        for block in range(4):
            rows = slice(8 * block, 8 * block + 8)
            above = edge_ref[pair] if block == 0 else None
            below = edge_ref[pair] if block == 3 else None
            refs = (mine_ref, other_ref) if pair == 0 else (other_ref, mine_ref)
            if above is None:
                above = refs[0][8 * block - 8 : 8 * block]
            if below is None:
                below = refs[1][8 * block + 8 : 8 * block + 16]
            out_ref[pair, rows] = jnp.where(first, above, below)


def pack_measured(ids_ref, angles_ref, measured_ref, out_ref):
    lane = lanes_of((8, 128))
    row = lax.broadcasted_iota(jnp.int32, (8, 128), 0)
    turns = [angles_ref[0, k].astype(jnp.float32) for k in range(2)]
    zero = jnp.zeros((8, 128), jnp.float32)
    for comp in range(2):
        halves = []
        for a in range(2):
            full = measured_ref[0, comp, 8 * a : 8 * a + 8, :]
            halves.append([full[:, 128 * n : 128 * n + 128] for n in range(8)])
        for j in range(32):
            v, r = divmod(32 * j - REACH, 128)
            parts = []
            for a in range(2):
                regs = halves[a]
                left = regs[v] if v >= 0 else zero
                part = turn(left, 64 * a - r)
                if r > 64:
                    right = regs[v + 1] if v + 1 < 8 else zero
                    part = jnp.where(lane - 64 * a < 128 - r, part, turn(right, 64 * a - r))
                parts.append(part)
            both = jnp.where(lane < 64, parts[0], parts[1])
            if comp == 0:
                both = jnp.where(lane == 0, turns[0], jnp.where(lane == 1, turns[1], both))
            out_ref[j, 8 * comp : 8 * comp + 8] = both


def side_sum(x):
    return turn(x, 1) + turn(x, 127)


def march(
    ids_ref, here_ref, left_ref, right_ref, got_ref,
    mine_ref, other_ref, across_ref, along_ref,
    plain, table, field, stored, acc, low, high,
):
    block, slab, cut = ids_ref[0], ids_ref[1], ids_ref[2]
    first = cut == 0
    lane = lanes_of((8, 128))
    sub = lax.broadcasted_iota(jnp.int32, (8, 128), 0)
    window = jnp.bitwise_and(lane, 63)
    upper = lane < 64
    column = 32 * block - REACH + window
    top = 32 * slab + 16 * cut - HALO
    column_inside = (column >= 0) & (column < 1024)

    for q in range(2):
        row = top + sub + 8 * q + jnp.where(upper, 0, 16)
        inside = column_inside & (row >= 0) & (row < 256)
        plain[8, 8 * q : 8 * q + 8] = jnp.where(inside, square_coeff, 0.0)
        for layer in range(4):
            pair, sl = divmod(layer, 2)
            values = []
            for n in (sl, 2 + sl):
                halves = []
                for a in range(2):
                    rows = slice(16 * a + 8 * q, 16 * a + 8 * q + 8)
                    at = 64 * a - 32 * n
                    halves.append(
                        jnp.where(
                            window < 16,
                            turn(left_ref[pair, rows], at - 16),
                            jnp.where(
                                window < 48,
                                turn(here_ref[pair, rows], at + 16),
                                turn(right_ref[pair, rows], at + 48),
                            ),
                        )
                    )
                values.append(jnp.where(upper, halves[0], halves[1]))
            damping = jnp.where(inside, jnp.exp(-values[1]), 0.0)
            plain[2 * layer, 8 * q : 8 * q + 8] = damping * jnp.cos(values[0])
            plain[2 * layer + 1, 8 * q : 8 * q + 8] = damping * jnp.sin(values[0])
    upper_row = lanes_of((1, 128)) < 64
    for n in range(9):
        for r in range(16):
            table[n, r : r + 1] = jnp.where(
                upper_row, plain[n, r : r + 1], plain[n, 15 - r : 16 - r]
            )
    acc[...] = jnp.zeros_like(acc)
    column_mask = jnp.where(column_inside, 1.0, 0.0)

    def spread(n, r):
        return jnp.broadcast_to(table[n, r : r + 1], (8, 128))

    def diffract(source, begin, inner, orient, emit):
        rows, scaled = {}, {}

        def around(values, r, k):
            parts = [values[n][k] for n in (r - 1, r + 1) if n in values]
            if r in values:
                parts.append(side_sum(values[r][k]))
            return functools.reduce(lambda x, y: x + y, parts)

        def scale(r):
            mask = spread(8, r)
            out = []
            for k in range(2):
                total = around(rows, r, k)
                if r in rows:
                    total = total - 4.0 * rows[r][k]
                out.append(mask * total)
            scaled[r] = tuple(out)

        def finish(r):
            re, im = (-around(scaled, r, k) for k in range(2))
            if r in rows:
                re, im = re + rows[r][0], im + rows[r][1]
            if r in scaled:
                mre, mim = scaled[r]
                turned = orient * ratio
                re = re + (4.0 * mre - turned * mim)
                im = im + (4.0 * mim + turned * mre)
            emit(r, re, im)

        def advance(r):
            if r - 1 >= begin + inner:
                scale(r - 1)
            if r - 2 >= begin + 2 * inner:
                finish(r - 2)

        for r in range(begin, 16):
            rows[r] = source(r)
            advance(r)
        rows[16] = tuple(turn(x, 64) for x in rows[15])
        advance(16)
        scaled[16] = tuple(turn(x, 64) for x in scaled[15])
        finish(15)

    @pl.loop(0, 4)
    def _(group):
        start = group * 128

        def received(comp, k):
            return got_ref[pl.ds(start + 8 * comp + k, 8, stride=16), :]

        head = received(0, 0)
        row_turns = jnp.broadcast_to(head[:, 0:1], (8, 128))
        col_turns = jnp.broadcast_to(head[:, 1:2], (8, 128))
        row0 = (top + jnp.where(upper, 0, 31)).astype(jnp.float32)
        row_part = row_turns * row0 * (1.0 / 256.0)
        col_part = col_turns * column.astype(jnp.float32) * (1.0 / 1024.0)
        row_part = row_part - jnp.floor(row_part)
        col_part = col_part - jnp.floor(col_part)
        t = two_pi * (row_part + col_part)
        wave = [(jnp.cos(t), jnp.sin(t))]
        t = two_pi / 256.0 * row_turns * jnp.where(upper, 1.0, -1.0)
        step = (jnp.cos(t), jnp.sin(t))

        def from_wave(r):
            re, im = wave[-1]
            wave.append((re * step[0] - im * step[1], re * step[1] + im * step[0]))
            return (re, im)

        def from_field(r):
            return (field[0, r], field[1, r])

        def forward(layer):
            def source(r):
                re, im = from_wave(r) if layer == 0 else from_field(r)
                a, b = spread(2 * layer, r), spread(2 * layer + 1, r)
                v = (a * re - b * im, a * im + b * re)
                stored[2 * layer, r], stored[2 * layer + 1, r] = v
                return v

            def emit(r, re, im):
                if layer == 3:
                    k = r - 8
                    field[0, r] = column_mask * (
                        re - jnp.where(upper, received(0, k), received(0, 7 - k))
                    )
                    field[1, r] = column_mask * (
                        im - jnp.where(upper, received(1, k), received(1, 7 - k))
                    )
                else:
                    field[0, r], field[1, r] = re, im

            diffract(source, 2 * layer, 1, 1.0, emit)

        def backward(layer):
            def emit(r, re, im):
                vre, vim = stored[2 * layer, r], stored[2 * layer + 1, r]
                acc[2 * layer, r] += vre * im - vim * re
                acc[2 * layer + 1, r] -= vre * re + vim * im
                if layer:
                    a, b = spread(2 * layer, r), spread(2 * layer + 1, r)
                    field[0, r], field[1, r] = a * re + b * im, a * im - b * re

            diffract(from_field, 2 * layer + 2, -1, -1.0, emit)

        for layer in range(4):
            forward(layer)
        for layer in (3, 2, 1, 0):
            backward(layer)

    for n in range(8):
        for r in range(16):
            row = jnp.sum(acc[n, r], axis=0, keepdims=True)
            low[n, r : r + 1] = row
            high[n, 15 - r : 16 - r] = row
    blocks = []
    for pair in range(2):
        parts = []
        for b in range(4):
            ref, shift = (low, 16) if b < 2 else (high, 80)
            rows = slice(8 * (b % 2), 8 * (b % 2) + 8)
            total = None
            for n in range(4):
                out, sl = divmod(n, 2)
                x = turn(ref[2 * (2 * pair + sl) + out, rows], 32 * n - shift)
                total = x if total is None else jnp.where(lane < 32 * n, total, x)
            parts.append(total)
        blocks.append(parts)
    mine = [jnp.where(first, a, b) for a, b in zip(*blocks)]
    other = [jnp.where(first, b, a) for a, b in zip(*blocks)]
    none = jnp.zeros((8, 128), jnp.float32)
    for parts, ref in ((mine, mine_ref), (other, other_ref)):
        for b in range(4):
            ref[8 * b : 8 * b + 8] = jnp.where(
                first, parts[b + 1] if b < 3 else none, parts[b - 1] if b > 0 else none
            )
    across_ref[...] = jnp.where(first, other[0], other[3])
    along_ref[...] = jnp.where(first, mine[0], mine[3])


def combine(ids_ref, mine_ref, other_ref, across_ref, along_ref, phase_ref, atten_ref):
    first = ids_ref[2] == 0
    for b in range(4):
        rows = slice(8 * b, 8 * b + 8)
        total = mine_ref[rows] + other_ref[rows]
        if b == 0:
            total = total + jnp.where(first, across_ref[...], along_ref[...])
        if b == 3:
            total = total + jnp.where(first, along_ref[...], across_ref[...])
        for sl in range(2):
            phase_ref[sl, rows] = turn(total, -32 * sl)[:, 0:32]
            atten_ref[sl, rows] = turn(total, -64 - 32 * sl)[:, 0:32]


def body(phase_delay, attenuation, measured, angles):
    block = lax.axis_index("illum")
    slab = lax.axis_index("slab")
    cut = lax.axis_index("cuts")
    ids = jnp.stack([block, slab, cut]).astype(jnp.int32)
    n_slabs, n_blocks = lax.axis_size("slab"), lax.axis_size("illum")
    rows_axis = ("slab", "cuts")

    def both_ways(pairs):
        return pairs + [(b, a) for a, b in pairs]

    partner = both_ways([(2 * s, 2 * s + 1) for s in range(n_slabs)])
    across = both_ways([(2 * s + 1, 2 * s + 2) for s in range(n_slabs - 1)])
    along = [(2 * s + 1, 2 * s + 3) for s in range(n_slabs - 1)]
    along += [(2 * s + 2, 2 * s) for s in range(n_slabs - 1)]

    mine = pl.pallas_call(
        pack_object,
        out_shape=f32(32, 128),
        in_specs=[VMEM, VMEM],
        out_specs=VMEM,
        compiler_params=small,
    )(phase_delay, attenuation)
    other = lax.ppermute(mine, rows_axis, partner)
    edges = pl.pallas_call(
        pack_edges,
        out_shape=f32(2, 8, 128),
        in_specs=[SMEM, VMEM, VMEM],
        out_specs=VMEM,
        compiler_params=small,
    )(ids, mine, other)
    edges = lax.ppermute(edges, rows_axis, across)
    here = pl.pallas_call(
        pack_rows,
        out_shape=f32(2, 32, 128),
        in_specs=[SMEM] + [VMEM] * 3,
        out_specs=VMEM,
        compiler_params=small,
    )(ids, mine, other, edges)
    from_left = lax.ppermute(here, "illum", [(i, i + 1) for i in range(n_blocks - 1)])
    from_right = lax.ppermute(here, "illum", [(i + 1, i) for i in range(n_blocks - 1)])

    sent = pl.pallas_call(
        pack_measured,
        out_shape=f32(32, 16, 128),
        grid_spec=pltpu.PrefetchScalarGridSpec(
            num_scalar_prefetch=1,
            grid=(1,),
            in_specs=[
                SMEM,
                pl.BlockSpec((1, 2, 16, 1024), lambda g, ids: (0, 0, ids[2], 0)),
            ],
            out_specs=pl.BlockSpec((32, 16, 128), lambda g, ids: (0, 0, 0)),
        ),
        compiler_params=large,
    )(ids, angles, measured)
    got = lax.all_to_all(sent, "illum", 0, 0, tiled=True)

    mine, other, across_part, along_part = pl.pallas_call(
        march,
        out_shape=(f32(32, 128), f32(32, 128), f32(8, 128), f32(8, 128)),
        in_specs=[SMEM] + [VMEM] * 4,
        out_specs=(VMEM,) * 4,
        scratch_shapes=[
            pltpu.VMEM((9, 16, 128), jnp.float32),
            pltpu.VMEM((9, 16, 128), jnp.float32),
            pltpu.VMEM((2, 16, 8, 128), jnp.float32),
            pltpu.VMEM((8, 16, 8, 128), jnp.float32),
            pltpu.VMEM((8, 16, 8, 128), jnp.float32),
            pltpu.VMEM((8, 16, 128), jnp.float32),
            pltpu.VMEM((8, 16, 128), jnp.float32),
        ],
        compiler_params=large,
    )(ids, here, from_left, from_right, got.reshape(512, 128))
    other = lax.ppermute(other, rows_axis, partner)
    across_part = lax.ppermute(across_part, rows_axis, across)
    along_part = lax.ppermute(along_part, rows_axis, along)
    return pl.pallas_call(
        combine,
        out_shape=(f32(2, 32, 32), f32(2, 32, 32)),
        in_specs=[SMEM] + [VMEM] * 4,
        out_specs=(VMEM, VMEM),
        compiler_params=small,
    )(ids, mine, other, across_part, along_part)


def solution(mesh):
    placed = (
        P("cuts", "slab", "illum"),
        P("cuts", "slab", "illum"),
        P("illum", None, "slab", None),
        P("illum", None),
    )
    return jax.shard_map(
        body,
        mesh=mesh,
        in_specs=placed,
        out_specs=(P("cuts", "slab", "illum"), P("cuts", "slab", "illum")),
        check_vma=False,
    )
```

time: 201 us -> 67.2 us (0.33)
  the two profiles are of different devices: /device:TPU:2 before, /device:TPU:69 now
where the time goes in v1:
time: 67.2 us; the launch traced here: 66.8 us
  starting transfers between devices  40 us (60%)
  waiting for transfers between devices  13.3 us (20%)
  Pallas kernels  11.1 us (17%)
  local copies, waits for them, and re-layouts  1.53 us (2%)
  between operations  0.76 us (1%)
    all_to_all x1, starting transfers between devices, body(): got = lax.all_to_all(sent, 'illum', 0, 0, tiled=True)  15 us
    pallas_call x1, Pallas kernels, body(): pl.pallas_call(march, out_shape=(f32(32, 128), f32(32, 128), f32(8, 128),...  6.75 us
    ppermute x1, waiting for transfers between devices, body(): lax.ppermute(here, 'illum', [(i, i + 1) for i in range(n_blocks - 1)])  5.83 us
    ppermute x1, starting transfers between devices, body(): lax.ppermute(here, 'illum', [(i + 1, i) for i in range(n_blocks - 1)])  5.5 us
    ppermute x1, starting transfers between devices, body(): across_part = lax.ppermute(across_part, rows_axis, across)  5.27 us
    ppermute x1, starting transfers between devices, body(): edges = lax.ppermute(edges, rows_axis, across)  4.93 us
    ppermute x1, starting transfers between devices, body(): other = lax.ppermute(other, rows_axis, partner)  3.16 us
    ppermute x1, waiting for transfers between devices, body(): along_part = lax.ppermute(along_part, rows_axis, along)  2.99 us
  transfers between devices with their start and end apart: 8, of which 4 were waited for; matrix products, arithmetic and copies ran while one was open for 0% of the time, Pallas kernels for 2%

profile of v1, /device:TPU:69, one launch (start us, length us, event | category | flops | bytes accessed | tf_op | source)
XLA Modules:
  0.0 66.8 jit_solution(1525062313724862524)
XLA Ops:
  0.6 0.0 copy-start.3
  0.6 0.1 pad_add_fusion.ids_ref
  0.7 0.6 copy-done.3
  1.3 0.0 copy-start
  1.3 0.9 %copy-done = f32[1,2,32,1024]{3,2,1,0:T(8,128)S(1)} copy-done((f32[1,2,32,1024]{3,2,1,0:T(8,128)S(1)}, f32[1,2,32,1024]{3,2,1,0:T(8,128)}, u32[]{:S(2)}) %copy-start) | copy-done | bytes 262168
  2.2 2.0 %shard_map.62 = f32[32,16,128]{2,1,0:T(8,128)} custom-call(s32[3]{0:T(128)S(1)} %pad_add_fusion.ids_ref, s32[1,2]{1,0:T(1,128)S(1)} %copy-done.3, f32[1,2,32,1024]{3,2,1,0:T(8,128)S(1)} %copy-done), custom_call_target="tpu_custom_call" | custom-call | tf_op jit(solution)/shard_map/pallas_call | solution.py:348
  4.2 0.0 copy-start.1
  4.2 0.0 copy-start.2
  4.2 15.0 %all-to-all-start = ((f32[32,16,128]{2,1,0:T(8,128)}), f32[32,16,128]{2,1,0:T(8,128)S(1)}, u32[]{:S(2)}, u32[]{:S(2)}) async-start(f32[32,16,128]{2,1,0:T(8,128)} %shard_map.62), calls=%async_computation | async-start | bytes 524288 | tf_op jit(solution)/shard_map/all_to_all | solution.py:362
  19.2 0.0 copy-done.1
  19.2 0.0 copy-done.2
  19.2 0.1 shard_map.59.mine_ref
  19.3 2.3 %collective-permute-start = (f32[32,128]{1,0:T(8,128)S(1)}, f32[32,128]{1,0:T(8,128)S(1)}, u32[]{:S(2)}, u32[]{:S(2)}) collective-permute-start(f32[32,128]{1,0:T(8,128)S(1)} %shard_map.59.mine_ref), channel_id=1, source_target_pairs={{0,1},{2,3},{4,5},{6,7},{8,9},{10,11},{12,13},{14,15},{1,0},{3,2},... | collective-permute-start | bytes 49160 | tf_op jit(solution)/shard_map/ppermute | solution.py:329
  21.6 2.9 %collective-permute-done.other_ref = f32[32,128]{1,0:T(8,128)S(1)} collective-permute-done((f32[32,128]{1,0:T(8,128)S(1)}, f32[32,128]{1,0:T(8,128)S(1)}, u32[]{:S(2)}, u32[]{:S(2)}) %collective-permute-start) | collective-permute-done | bytes 16416 | tf_op jit(solution)/shard_map/ppermute | solution.py:329
  24.5 0.5 shard_map.60
  25.0 4.9 %collective-permute-start.1 = (f32[2,8,128]{2,1,0:T(8,128)S(1)}, f32[2,8,128]{2,1,0:T(8,128)S(1)}, u32[]{:S(2)}, u32[]{:S(2)}) collective-permute-start(f32[2,8,128]{2,1,0:T(8,128)S(1)} %shard_map.60), channel_id=1, source_target_pairs={{1,2},{3,4},{5,6},{7,8},{9,10},{11,12},{13,14},{2,1},{4,3},{6,5},{... | collective-permute-start | bytes 24584 | tf_op jit(solution)/shard_map/ppermute | solution.py:337
  30.0 1.6 %collective-permute-done.1.edge_ref = f32[2,8,128]{2,1,0:T(8,128)S(1)} collective-permute-done((f32[2,8,128]{2,1,0:T(8,128)S(1)}, f32[2,8,128]{2,1,0:T(8,128)S(1)}, u32[]{:S(2)}, u32[]{:S(2)}) %collective-permute-start.1) | collective-permute-done | bytes 8224 | tf_op jit(solution)/shard_map/ppermute | solution.py:337
  31.6 0.5 shard_map.61.here_ref
  32.2 5.5 %collective-permute-start.3 = (f32[2,32,128]{2,1,0:T(8,128)S(1)}, f32[2,32,128]{2,1,0:T(8,128)S(1)}, u32[]{:S(2)}, u32[]{:S(2)}) collective-permute-start(f32[2,32,128]{2,1,0:T(8,128)S(1)} %shard_map.61.here_ref), channel_id=1, source_target_pairs={{16,0},{32,16},{48,32},{64,48},{80,64},{96,80},{112,96},{128,112},... | collective-permute-start | bytes 98312 | tf_op jit(solution)/shard_map/ppermute | solution.py:346
  37.7 1.9 %collective-permute-start.2 = (f32[2,32,128]{2,1,0:T(8,128)S(1)}, f32[2,32,128]{2,1,0:T(8,128)S(1)}, u32[]{:S(2)}, u32[]{:S(2)}) collective-permute-start(f32[2,32,128]{2,1,0:T(8,128)S(1)} %shard_map.61.here_ref), channel_id=1, source_target_pairs={{0,16},{16,32},{32,48},{48,64},{64,80},{80,96},{96,112},{112,128},... | collective-permute-start | bytes 98312 | tf_op jit(solution)/shard_map/ppermute | solution.py:345
  39.6 0.0 collective-permute-done.3.right_ref
  39.6 5.8 %collective-permute-done.2.left_ref = f32[2,32,128]{2,1,0:T(8,128)S(1)} collective-permute-done((f32[2,32,128]{2,1,0:T(8,128)S(1)}, f32[2,32,128]{2,1,0:T(8,128)S(1)}, u32[]{:S(2)}, u32[]{:S(2)}) %collective-permute-start.2) | collective-permute-done | bytes 32800 | tf_op jit(solution)/shard_map/ppermute | solution.py:345
  45.4 0.0 all-to-all-done
  45.4 6.8 %shard_map.63 = (f32[32,128]{1,0:T(8,128)S(1)}, f32[32,128]{1,0:T(8,128)S(1)}, f32[8,128]{1,0:T(8,128)S(1)}, f32[8,128]{1,0:T(8,128)S(1)}) custom-call(s32[3]{0:T(128)S(1)} %pad_add_fusion.ids_ref, f32[2,32,128]{2,1,0:T(8,128)S(1)} %shard_map.61.here_ref, f32[2,32,128]{2,1,0:T(8,128)S(1)} %collective-permute-done.2.left_ref, ...), custom_call_target="tpu_custom_call" | custom-call | tf_op jit(solution)/shard_map/pallas_call | solution.py:364
  52.2 3.2 %collective-permute-start.4 = (f32[32,128]{1,0:T(8,128)S(1)}, f32[32,128]{1,0:T(8,128)S(1)}, u32[]{:S(2)}, u32[]{:S(2)}) collective-permute-start(f32[32,128]{1,0:T(8,128)S(1)} %get-tuple-element.7), channel_id=1, source_target_pairs={{0,1},{2,3},{4,5},{6,7},{8,9},{10,11},{12,13},{14,15},{1,0},{3,2},... | collective-permute-start | bytes 49160 | tf_op jit(solution)/shard_map/ppermute | solution.py:380
  55.4 5.3 %collective-permute-start.5 = (f32[8,128]{1,0:T(8,128)S(1)}, f32[8,128]{1,0:T(8,128)S(1)}, u32[]{:S(2)}, u32[]{:S(2)}) collective-permute-start(f32[8,128]{1,0:T(8,128)S(1)} %get-tuple-element.8), channel_id=1, source_target_pairs={{1,2},{3,4},{5,6},{7,8},{9,10},{11,12},{13,14},{2,1},{4,3},{6,5},{... | collective-permute-start | bytes 12296 | tf_op jit(solution)/shard_map/ppermute | solution.py:381
  60.6 1.9 %collective-permute-start.6 = (f32[8,128]{1,0:T(8,128)S(1)}, f32[8,128]{1,0:T(8,128)S(1)}, u32[]{:S(2)}, u32[]{:S(2)}) collective-permute-start(f32[8,128]{1,0:T(8,128)S(1)} %get-tuple-element.9), channel_id=1, source_target_pairs={{1,3},{3,5},{5,7},{7,9},{9,11},{11,13},{13,15},{2,0},{4,2},{6,4},{... | collective-permute-start | bytes 12296 | tf_op jit(solution)/shard_map/ppermute | solution.py:382
  62.6 0.0 collective-permute-done.5.across_ref
  62.6 3.0 %collective-permute-done.6.along_ref = f32[8,128]{1,0:T(8,128)S(1)} collective-permute-done((f32[8,128]{1,0:T(8,128)S(1)}, f32[8,128]{1,0:T(8,128)S(1)}, u32[]{:S(2)}, u32[]{:S(2)}) %collective-permute-start.6) | collective-permute-done | bytes 4128 | tf_op jit(solution)/shard_map/ppermute | solution.py:382
  65.6 0.0 collective-permute-done.4.other_ref
  65.6 1.2 %shard_map.64 = (f32[2,32,32]{2,1,0:T(8,128)}, f32[2,32,32]{2,1,0:T(8,128)}) custom-call(s32[3]{0:T(128)S(1)} %pad_add_fusion.ids_ref, f32[32,128]{1,0:T(8,128)S(1)} %get-tuple-element.6.mine_ref, f32[32,128]{1,0:T(8,128)S(1)} %collective-permute-done.4.other_ref, f32[8,128]{1,0:T(8,128)S(1)} %collective-permute-done.5.across_ref, ...), custom_call_target="tpu_custom_call" | custom-call | tf_op jit(solution)/shard_map/pallas_call | solution.py:383
Async XLA Ops:
  0.6 0.7 copy-start.3
  1.3 0.9 %copy-start = (f32[1,2,32,1024]{3,2,1,0:T(8,128)S(1)}, f32[1,2,32,1024]{3,2,1,0:T(8,128)}, u32[]{:S(2)}) copy-start(f32[1,2,32,1024]{3,2,1,0:T(8,128)} %measured_ref.1) | copy-start | bytes 786436
  4.2 15.0 %copy-start.1 = (f32[2,32,32]{2,1,0:T(8,128)S(1)}, f32[2,32,32]{2,1,0:T(8,128)}, u32[]{:S(2)}) copy-start(f32[2,32,32]{2,1,0:T(8,128)} %phase_ref.1) | copy-start | bytes 24580
  4.2 15.0 %copy-start.2 = (f32[2,32,32]{2,1,0:T(8,128)S(1)}, f32[2,32,32]{2,1,0:T(8,128)}, u32[]{:S(2)}) copy-start(f32[2,32,32]{2,1,0:T(8,128)} %atten_ref.1) | copy-start | bytes 24580
  4.2 41.2 %all-to-all-start = ((f32[32,16,128]{2,1,0:T(8,128)}), f32[32,16,128]{2,1,0:T(8,128)S(1)}, u32[]{:S(2)}, u32[]{:S(2)}) async-start(f32[32,16,128]{2,1,0:T(8,128)} %shard_map.62), calls=%async_computation | async-start | bytes 524288 | tf_op jit(solution)/shard_map/all_to_all | solution.py:362
  19.3 5.2 %collective-permute-start = (f32[32,128]{1,0:T(8,128)S(1)}, f32[32,128]{1,0:T(8,128)S(1)}, u32[]{:S(2)}, u32[]{:S(2)}) collective-permute-start(f32[32,128]{1,0:T(8,128)S(1)} %shard_map.59.mine_ref), channel_id=1, source_target_pairs={{0,1},{2,3},{4,5},{6,7},{8,9},{10,11},{12,13},{14,15},{1,0},{3,2},... | collective-permute-start | bytes 49160 | tf_op jit(solution)/shard_map/ppermute | solution.py:329
  25.0 6.6 %collective-permute-start.1 = (f32[2,8,128]{2,1,0:T(8,128)S(1)}, f32[2,8,128]{2,1,0:T(8,128)S(1)}, u32[]{:S(2)}, u32[]{:S(2)}) collective-permute-start(f32[2,8,128]{2,1,0:T(8,128)S(1)} %shard_map.60), channel_id=1, source_target_pairs={{1,2},{3,4},{5,6},{7,8},{9,10},{11,12},{13,14},{2,1},{4,3},{6,5},{... | collective-permute-start | bytes 24584 | tf_op jit(solution)/shard_map/ppermute | solution.py:337
  32.2 7.4 %collective-permute-start.3 = (f32[2,32,128]{2,1,0:T(8,128)S(1)}, f32[2,32,128]{2,1,0:T(8,128)S(1)}, u32[]{:S(2)}, u32[]{:S(2)}) collective-permute-start(f32[2,32,128]{2,1,0:T(8,128)S(1)} %shard_map.61.here_ref), channel_id=1, source_target_pairs={{16,0},{32,16},{48,32},{64,48},{80,64},{96,80},{112,96},{128,112},... | collective-permute-start | bytes 98312 | tf_op jit(solution)/shard_map/ppermute | solution.py:346
  37.7 7.8 %collective-permute-start.2 = (f32[2,32,128]{2,1,0:T(8,128)S(1)}, f32[2,32,128]{2,1,0:T(8,128)S(1)}, u32[]{:S(2)}, u32[]{:S(2)}) collective-permute-start(f32[2,32,128]{2,1,0:T(8,128)S(1)} %shard_map.61.here_ref), channel_id=1, source_target_pairs={{0,16},{16,32},{32,48},{48,64},{64,80},{80,96},{96,112},{112,128},... | collective-permute-start | bytes 98312 | tf_op jit(solution)/shard_map/ppermute | solution.py:345
  52.2 13.4 %collective-permute-start.4 = (f32[32,128]{1,0:T(8,128)S(1)}, f32[32,128]{1,0:T(8,128)S(1)}, u32[]{:S(2)}, u32[]{:S(2)}) collective-permute-start(f32[32,128]{1,0:T(8,128)S(1)} %get-tuple-element.7), channel_id=1, source_target_pairs={{0,1},{2,3},{4,5},{6,7},{8,9},{10,11},{12,13},{14,15},{1,0},{3,2},... | collective-permute-start | bytes 49160 | tf_op jit(solution)/shard_map/ppermute | solution.py:380
  55.4 7.2 %collective-permute-start.5 = (f32[8,128]{1,0:T(8,128)S(1)}, f32[8,128]{1,0:T(8,128)S(1)}, u32[]{:S(2)}, u32[]{:S(2)}) collective-permute-start(f32[8,128]{1,0:T(8,128)S(1)} %get-tuple-element.8), channel_id=1, source_target_pairs={{1,2},{3,4},{5,6},{7,8},{9,10},{11,12},{13,14},{2,1},{4,3},{6,5},{... | collective-permute-start | bytes 12296 | tf_op jit(solution)/shard_map/ppermute | solution.py:381
  60.6 4.9 %collective-permute-start.6 = (f32[8,128]{1,0:T(8,128)S(1)}, f32[8,128]{1,0:T(8,128)S(1)}, u32[]{:S(2)}, u32[]{:S(2)}) collective-permute-start(f32[8,128]{1,0:T(8,128)S(1)} %get-tuple-element.9), channel_id=1, source_target_pairs={{1,3},{3,5},{5,7},{7,9},{9,11},{11,13},{13,15},{2,0},{4,2},{6,4},{... | collective-permute-start | bytes 12296 | tf_op jit(solution)/shard_map/ppermute | solution.py:382

commit v2 on v1

--- a/solution.py
+++ b/solution.py
@@ -8,6 +8,7 @@
 from jax.experimental.pallas import tpu as pltpu
 from jax.sharding import PartitionSpec as P
 
+
 step_coeff = 0.08
 square_coeff = 0.0032
 ratio = step_coeff / square_coeff
@@ -17,6 +18,7 @@
 REACH = 16
 VMEM = pl.BlockSpec(memory_space=pltpu.VMEM)
 SMEM = pl.BlockSpec(memory_space=pltpu.SMEM)
+HBM = pl.BlockSpec(memory_space=pltpu.HBM)
 small = pltpu.CompilerParams(vmem_limit_bytes=1 << 20)
 large = pltpu.CompilerParams(vmem_limit_bytes=8 << 20)
 
@@ -34,11 +36,30 @@
     return pltpu.roll(x, by, 1) if by else x
 
 
-def pack_object(phase_ref, atten_ref, out_ref):
-    for n, (ref, layer) in enumerate(
-        ((phase_ref, 0), (phase_ref, 1), (atten_ref, 0), (atten_ref, 1))
-    ):
+def pack_object(
+    ids_ref, phase_ref, atten_ref, measured_ref, angles_ref,
+    out_ref, half_ref, head_ref,
+    phase, atten, turns, sems,
+):
+    copies = [
+        pltpu.make_async_copy(phase_ref, phase, sems.at[0]),
+        pltpu.make_async_copy(atten_ref, atten, sems.at[1]),
+        pltpu.make_async_copy(angles_ref, turns, sems.at[2]),
+        pltpu.make_async_copy(
+            measured_ref.at[0, :, pl.ds(pl.multiple_of(16 * ids_ref[2], 16), 16), :],
+            half_ref,
+            sems.at[3],
+        ),
+    ]
+    for copy in copies:
+        copy.start()
+    for copy in copies[:3]:
+        copy.wait()
+    for n, (ref, layer) in enumerate(((phase, 0), (phase, 1), (atten, 0), (atten, 1))):
         out_ref[:, 32 * n : 32 * n + 32] = ref[layer]
+    lane = lanes_of((8, 128))
+    head_ref[...] = jnp.where(lane == 0, turns[0, 0], turns[0, 1]).astype(jnp.float32)
+    copies[3].wait()
 
 
 def pack_edges(ids_ref, mine_ref, other_ref, out_ref):
@@ -64,31 +85,40 @@
             out_ref[pair, rows] = jnp.where(first, above, below)
 
 
-def pack_measured(ids_ref, angles_ref, measured_ref, out_ref):
+def pack_measured(half_ref, head_ref, out_ref, packed, sems):
     lane = lanes_of((8, 128))
-    row = lax.broadcasted_iota(jnp.int32, (8, 128), 0)
-    turns = [angles_ref[0, k].astype(jnp.float32) for k in range(2)]
     zero = jnp.zeros((8, 128), jnp.float32)
-    for comp in range(2):
-        halves = []
-        for a in range(2):
-            full = measured_ref[0, comp, 8 * a : 8 * a + 8, :]
-            halves.append([full[:, 128 * n : 128 * n + 128] for n in range(8)])
-        for j in range(32):
-            v, r = divmod(32 * j - REACH, 128)
+    regs = [
+        [
+            [half_ref[comp, 8 * a : 8 * a + 8, 128 * n : 128 * n + 128] for n in range(8)]
+            for a in range(2)
+        ]
+        for comp in range(2)
+    ]
+    copies = []
+    for j in range(32):
+        v, r = divmod(32 * j - REACH, 128)
+        for comp in range(2):
             parts = []
             for a in range(2):
-                regs = halves[a]
-                left = regs[v] if v >= 0 else zero
+                left = regs[comp][a][v] if v >= 0 else zero
                 part = turn(left, 64 * a - r)
                 if r > 64:
-                    right = regs[v + 1] if v + 1 < 8 else zero
+                    right = regs[comp][a][v + 1] if v + 1 < 8 else zero
                     part = jnp.where(lane - 64 * a < 128 - r, part, turn(right, 64 * a - r))
                 parts.append(part)
             both = jnp.where(lane < 64, parts[0], parts[1])
             if comp == 0:
-                both = jnp.where(lane == 0, turns[0], jnp.where(lane == 1, turns[1], both))
-            out_ref[j, 8 * comp : 8 * comp + 8] = both
+                both = jnp.where(lane < 2, head_ref[...], both)
+            packed[j, 8 * comp : 8 * comp + 8] = both
+        if j % 8 == 7:
+            part = pl.ds(j - 7, 8)
+            copies.append(
+                pltpu.make_async_copy(packed.at[part], out_ref.at[part], sems.at[j // 8])
+            )
+            copies[-1].start()
+    for copy in copies:
+        copy.wait()
 
 
 def side_sum(x):
@@ -213,7 +243,7 @@
         t = two_pi / 256.0 * row_turns * jnp.where(upper, 1.0, -1.0)
         step = (jnp.cos(t), jnp.sin(t))
 
-        def from_wave(r):
+        def from_wave():
             re, im = wave[-1]
             wave.append((re * step[0] - im * step[1], re * step[1] + im * step[0]))
             return (re, im)
@@ -223,7 +253,7 @@
 
         def forward(layer):
             def source(r):
-                re, im = from_wave(r) if layer == 0 else from_field(r)
+                re, im = from_wave() if layer == 0 else from_field(r)
                 a, b = spread(2 * layer, r), spread(2 * layer + 1, r)
                 v = (a * re - b * im, a * im + b * re)
                 stored[2 * layer, r], stored[2 * layer + 1, r] = v
@@ -319,14 +349,37 @@
     along = [(2 * s + 1, 2 * s + 3) for s in range(n_slabs - 1)]
     along += [(2 * s + 2, 2 * s) for s in range(n_slabs - 1)]
 
-    mine = pl.pallas_call(
+    mine, half, head = pl.pallas_call(
         pack_object,
-        out_shape=f32(32, 128),
+        out_shape=(f32(32, 128), f32(2, 16, 1024), f32(8, 128)),
+        in_specs=[SMEM] + [HBM] * 4,
+        out_specs=(VMEM,) * 3,
+        scratch_shapes=[
+            pltpu.VMEM((2, 32, 32), jnp.float32),
+            pltpu.VMEM((2, 32, 32), jnp.float32),
+            pltpu.SMEM((1, 2), jnp.int32),
+            pltpu.SemaphoreType.DMA((4,)),
+        ],
+        compiler_params=small,
+    )(
+        ids,
+        *(
+            pltpu.with_memory_space_constraint(x, pltpu.HBM)
+            for x in (phase_delay, attenuation, measured, angles)
+        ),
+    )
+    other = lax.ppermute(mine, rows_axis, partner)
+    sent = pl.pallas_call(
+        pack_measured,
+        out_shape=f32(32, 16, 128),
         in_specs=[VMEM, VMEM],
-        out_specs=VMEM,
+        out_specs=HBM,
+        scratch_shapes=[
+            pltpu.VMEM((32, 16, 128), jnp.float32),
+            pltpu.SemaphoreType.DMA((4,)),
+        ],
         compiler_params=small,
-    )(phase_delay, attenuation)
-    other = lax.ppermute(mine, rows_axis, partner)
+    )(half, head)
     edges = pl.pallas_call(
         pack_edges,
         out_shape=f32(2, 8, 128),
@@ -335,6 +388,7 @@
         compiler_params=small,
     )(ids, mine, other)
     edges = lax.ppermute(edges, rows_axis, across)
+    got = lax.all_to_all(sent, "illum", 0, 0, tiled=True)
     here = pl.pallas_call(
         pack_rows,
         out_shape=f32(2, 32, 128),
@@ -344,22 +398,6 @@
     )(ids, mine, other, edges)
     from_left = lax.ppermute(here, "illum", [(i, i + 1) for i in range(n_blocks - 1)])
     from_right = lax.ppermute(here, "illum", [(i + 1, i) for i in range(n_blocks - 1)])
-
-    sent = pl.pallas_call(
-        pack_measured,
-        out_shape=f32(32, 16, 128),
-        grid_spec=pltpu.PrefetchScalarGridSpec(
-            num_scalar_prefetch=1,
-            grid=(1,),
-            in_specs=[
-                SMEM,
-                pl.BlockSpec((1, 2, 16, 1024), lambda g, ids: (0, 0, ids[2], 0)),
-            ],
-            out_specs=pl.BlockSpec((32, 16, 128), lambda g, ids: (0, 0, 0)),
-        ),
-        compiler_params=large,
-    )(ids, angles, measured)
-    got = lax.all_to_all(sent, "illum", 0, 0, tiled=True)
 
     mine, other, across_part, along_part = pl.pallas_call(
         march,

time: 67.2 us -> 66 us (0.982)
  local copies, waits for them, and re-layouts: 1.53 us -> 0 us
    unnamed x8 -> x0, local copies, waits for them, and re-layouts: 1.53 us -> none
where the time goes in v2:
time: 66 us; the launch traced here: 65.6 us
  starting transfers between devices  40 us (61%)
  waiting for transfers between devices  13.3 us (20%)
  Pallas kernels  11.5 us (17%)
  between operations  0.75 us (1%)
    all_to_all x1, starting transfers between devices, body(): got = lax.all_to_all(sent, 'illum', 0, 0, tiled=True)  14.8 us
    pallas_call x1, Pallas kernels, body(): pl.pallas_call(march, out_shape=(f32(32, 128), f32(32, 128), f32(8, 128),...  6.75 us
    ppermute x1, waiting for transfers between devices, body(): lax.ppermute(here, 'illum', [(i, i + 1) for i in range(n_blocks - 1)])  5.83 us
    ppermute x1, starting transfers between devices, body(): lax.ppermute(here, 'illum', [(i + 1, i) for i in range(n_blocks - 1)])  5.5 us
    ppermute x1, starting transfers between devices, body(): across_part = lax.ppermute(across_part, rows_axis, across)  5.27 us
    ppermute x1, starting transfers between devices, body(): edges = lax.ppermute(edges, rows_axis, across)  5.1 us
    ppermute x1, starting transfers between devices, body(): other = lax.ppermute(other, rows_axis, partner)  3.16 us
    ppermute x1, waiting for transfers between devices, body(): along_part = lax.ppermute(along_part, rows_axis, along)  2.99 us
  transfers between devices with their start and end apart: 8, of which 4 were waited for; matrix products, arithmetic and copies ran while one was open for 0% of the time, Pallas kernels for 2%

profile of v2, /device:TPU:69, one launch (start us, length us, event | category | flops | bytes accessed | tf_op | source)
XLA Modules:
  0.0 65.6 jit_solution(11858561408651026804)
XLA Ops:
  0.6 0.1 pad_add_fusion.ids_ref
  0.7 1.5 %shard_map.59 = (f32[32,128]{1,0:T(8,128)S(1)}, f32[2,16,1024]{2,1,0:T(8,128)S(1)}, f32[8,128]{1,0:T(8,128)S(1)}) custom-call(s32[3]{0:T(128)S(1)} %pad_add_fusion.ids_ref, f32[2,32,32]{2,1,0:T(8,128)} %phase_ref.1, f32[2,32,32]{2,1,0:T(8,128)} %atten_ref.1, f32[1,2,32,1024]{3,2,1,0:T(8,128)} %measured_ref.1, s32[1,2]{1,0:T(1,128)} %angles_ref.1), custom_call_target="tpu_custom_call" | custom-call | tf_op jit(solution)/shard_map/pallas_call | solution.py:352
  2.2 0.9 %shard_map.62 = f32[32,16,128]{2,1,0:T(8,128)} custom-call(f32[2,16,1024]{2,1,0:T(8,128)S(1)} %get-tuple-element.10.half_ref, f32[8,128]{1,0:T(8,128)S(1)} %get-tuple-element.11.head_ref), custom_call_target="tpu_custom_call" | custom-call | tf_op jit(solution)/shard_map/pallas_call | solution.py:372
  3.1 14.8 %all-to-all-start = ((f32[32,16,128]{2,1,0:T(8,128)}), f32[32,16,128]{2,1,0:T(8,128)S(1)}, u32[]{:S(2)}, u32[]{:S(2)}) async-start(f32[32,16,128]{2,1,0:T(8,128)} %shard_map.62), calls=%async_computation | async-start | bytes 524288 | tf_op jit(solution)/shard_map/all_to_all | solution.py:391
  18.0 2.3 %collective-permute-start = (f32[32,128]{1,0:T(8,128)S(1)}, f32[32,128]{1,0:T(8,128)S(1)}, u32[]{:S(2)}, u32[]{:S(2)}) collective-permute-start(f32[32,128]{1,0:T(8,128)S(1)} %get-tuple-element.9.mine_ref), channel_id=1, source_target_pairs={{0,1},{2,3},{4,5},{6,7},{8,9},{10,11},{12,13},{14,15},{1,0},{3,2},... | collective-permute-start | bytes 49160 | tf_op jit(solution)/shard_map/ppermute | solution.py:371
  20.3 2.8 %collective-permute-done.other_ref = f32[32,128]{1,0:T(8,128)S(1)} collective-permute-done((f32[32,128]{1,0:T(8,128)S(1)}, f32[32,128]{1,0:T(8,128)S(1)}, u32[]{:S(2)}, u32[]{:S(2)}) %collective-permute-start) | collective-permute-done | bytes 16416 | tf_op jit(solution)/shard_map/ppermute | solution.py:371
  23.1 0.5 shard_map.60
  23.7 5.1 %collective-permute-start.1 = (f32[2,8,128]{2,1,0:T(8,128)S(1)}, f32[2,8,128]{2,1,0:T(8,128)S(1)}, u32[]{:S(2)}, u32[]{:S(2)}) collective-permute-start(f32[2,8,128]{2,1,0:T(8,128)S(1)} %shard_map.60), channel_id=1, source_target_pairs={{1,2},{3,4},{5,6},{7,8},{9,10},{11,12},{13,14},{2,1},{4,3},{6,5},{... | collective-permute-start | bytes 24584 | tf_op jit(solution)/shard_map/ppermute | solution.py:390
  28.8 1.6 %collective-permute-done.1.edge_ref = f32[2,8,128]{2,1,0:T(8,128)S(1)} collective-permute-done((f32[2,8,128]{2,1,0:T(8,128)S(1)}, f32[2,8,128]{2,1,0:T(8,128)S(1)}, u32[]{:S(2)}, u32[]{:S(2)}) %collective-permute-start.1) | collective-permute-done | bytes 8224 | tf_op jit(solution)/shard_map/ppermute | solution.py:390
  30.4 0.5 shard_map.61.here_ref
  30.9 5.5 %collective-permute-start.3 = (f32[2,32,128]{2,1,0:T(8,128)S(1)}, f32[2,32,128]{2,1,0:T(8,128)S(1)}, u32[]{:S(2)}, u32[]{:S(2)}) collective-permute-start(f32[2,32,128]{2,1,0:T(8,128)S(1)} %shard_map.61.here_ref), channel_id=1, source_target_pairs={{16,0},{32,16},{48,32},{64,48},{80,64},{96,80},{112,96},{128,112},... | collective-permute-start | bytes 98312 | tf_op jit(solution)/shard_map/ppermute | solution.py:400
  36.4 1.9 %collective-permute-start.2 = (f32[2,32,128]{2,1,0:T(8,128)S(1)}, f32[2,32,128]{2,1,0:T(8,128)S(1)}, u32[]{:S(2)}, u32[]{:S(2)}) collective-permute-start(f32[2,32,128]{2,1,0:T(8,128)S(1)} %shard_map.61.here_ref), channel_id=1, source_target_pairs={{0,16},{16,32},{32,48},{48,64},{64,80},{80,96},{96,112},{112,128},... | collective-permute-start | bytes 98312 | tf_op jit(solution)/shard_map/ppermute | solution.py:399
  38.4 0.0 collective-permute-done.3.right_ref
  38.4 5.8 %collective-permute-done.2.left_ref = f32[2,32,128]{2,1,0:T(8,128)S(1)} collective-permute-done((f32[2,32,128]{2,1,0:T(8,128)S(1)}, f32[2,32,128]{2,1,0:T(8,128)S(1)}, u32[]{:S(2)}, u32[]{:S(2)}) %collective-permute-start.2) | collective-permute-done | bytes 32800 | tf_op jit(solution)/shard_map/ppermute | solution.py:399
  44.2 0.0 all-to-all-done
  44.2 6.8 %shard_map.63 = (f32[32,128]{1,0:T(8,128)S(1)}, f32[32,128]{1,0:T(8,128)S(1)}, f32[8,128]{1,0:T(8,128)S(1)}, f32[8,128]{1,0:T(8,128)S(1)}) custom-call(s32[3]{0:T(128)S(1)} %pad_add_fusion.ids_ref, f32[2,32,128]{2,1,0:T(8,128)S(1)} %shard_map.61.here_ref, f32[2,32,128]{2,1,0:T(8,128)S(1)} %collective-permute-done.2.left_ref, ...), custom_call_target="tpu_custom_call" | custom-call | tf_op jit(solution)/shard_map/pallas_call | solution.py:402
  51.0 3.2 %collective-permute-start.4 = (f32[32,128]{1,0:T(8,128)S(1)}, f32[32,128]{1,0:T(8,128)S(1)}, u32[]{:S(2)}, u32[]{:S(2)}) collective-permute-start(f32[32,128]{1,0:T(8,128)S(1)} %get-tuple-element.13), channel_id=1, source_target_pairs={{0,1},{2,3},{4,5},{6,7},{8,9},{10,11},{12,13},{14,15},{1,0},{3,2},... | collective-permute-start | bytes 49160 | tf_op jit(solution)/shard_map/ppermute | solution.py:418
  54.1 5.3 %collective-permute-start.5 = (f32[8,128]{1,0:T(8,128)S(1)}, f32[8,128]{1,0:T(8,128)S(1)}, u32[]{:S(2)}, u32[]{:S(2)}) collective-permute-start(f32[8,128]{1,0:T(8,128)S(1)} %get-tuple-element.14), channel_id=1, source_target_pairs={{1,2},{3,4},{5,6},{7,8},{9,10},{11,12},{13,14},{2,1},{4,3},{6,5},{... | collective-permute-start | bytes 12296 | tf_op jit(solution)/shard_map/ppermute | solution.py:419
  59.4 1.9 %collective-permute-start.6 = (f32[8,128]{1,0:T(8,128)S(1)}, f32[8,128]{1,0:T(8,128)S(1)}, u32[]{:S(2)}, u32[]{:S(2)}) collective-permute-start(f32[8,128]{1,0:T(8,128)S(1)} %get-tuple-element.15), channel_id=1, source_target_pairs={{1,3},{3,5},{5,7},{7,9},{9,11},{11,13},{13,15},{2,0},{4,2},{6,4},{... | collective-permute-start | bytes 12296 | tf_op jit(solution)/shard_map/ppermute | solution.py:420
  61.3 0.0 collective-permute-done.5.across_ref
  61.3 3.0 %collective-permute-done.6.along_ref = f32[8,128]{1,0:T(8,128)S(1)} collective-permute-done((f32[8,128]{1,0:T(8,128)S(1)}, f32[8,128]{1,0:T(8,128)S(1)}, u32[]{:S(2)}, u32[]{:S(2)}) %collective-permute-start.6) | collective-permute-done | bytes 4128 | tf_op jit(solution)/shard_map/ppermute | solution.py:420
  64.3 0.0 collective-permute-done.4.other_ref
  64.3 1.2 %shard_map.64 = (f32[2,32,32]{2,1,0:T(8,128)}, f32[2,32,32]{2,1,0:T(8,128)}) custom-call(s32[3]{0:T(128)S(1)} %pad_add_fusion.ids_ref, f32[32,128]{1,0:T(8,128)S(1)} %get-tuple-element.12.mine_ref, f32[32,128]{1,0:T(8,128)S(1)} %collective-permute-done.4.other_ref, f32[8,128]{1,0:T(8,128)S(1)} %collective-permute-done.5.across_ref, ...), custom_call_target="tpu_custom_call" | custom-call | tf_op jit(solution)/shard_map/pallas_call | solution.py:421
Async XLA Ops:
  3.1 41.1 %all-to-all-start = ((f32[32,16,128]{2,1,0:T(8,128)}), f32[32,16,128]{2,1,0:T(8,128)S(1)}, u32[]{:S(2)}, u32[]{:S(2)}) async-start(f32[32,16,128]{2,1,0:T(8,128)} %shard_map.62), calls=%async_computation | async-start | bytes 524288 | tf_op jit(solution)/shard_map/all_to_all | solution.py:391
  18.0 5.1 %collective-permute-start = (f32[32,128]{1,0:T(8,128)S(1)}, f32[32,128]{1,0:T(8,128)S(1)}, u32[]{:S(2)}, u32[]{:S(2)}) collective-permute-start(f32[32,128]{1,0:T(8,128)S(1)} %get-tuple-element.9.mine_ref), channel_id=1, source_target_pairs={{0,1},{2,3},{4,5},{6,7},{8,9},{10,11},{12,13},{14,15},{1,0},{3,2},... | collective-permute-start | bytes 49160 | tf_op jit(solution)/shard_map/ppermute | solution.py:371
  23.7 6.7 %collective-permute-start.1 = (f32[2,8,128]{2,1,0:T(8,128)S(1)}, f32[2,8,128]{2,1,0:T(8,128)S(1)}, u32[]{:S(2)}, u32[]{:S(2)}) collective-permute-start(f32[2,8,128]{2,1,0:T(8,128)S(1)} %shard_map.60), channel_id=1, source_target_pairs={{1,2},{3,4},{5,6},{7,8},{9,10},{11,12},{13,14},{2,1},{4,3},{6,5},{... | collective-permute-start | bytes 24584 | tf_op jit(solution)/shard_map/ppermute | solution.py:390
  30.9 7.4 %collective-permute-start.3 = (f32[2,32,128]{2,1,0:T(8,128)S(1)}, f32[2,32,128]{2,1,0:T(8,128)S(1)}, u32[]{:S(2)}, u32[]{:S(2)}) collective-permute-start(f32[2,32,128]{2,1,0:T(8,128)S(1)} %shard_map.61.here_ref), channel_id=1, source_target_pairs={{16,0},{32,16},{48,32},{64,48},{80,64},{96,80},{112,96},{128,112},... | collective-permute-start | bytes 98312 | tf_op jit(solution)/shard_map/ppermute | solution.py:400
  36.4 7.8 %collective-permute-start.2 = (f32[2,32,128]{2,1,0:T(8,128)S(1)}, f32[2,32,128]{2,1,0:T(8,128)S(1)}, u32[]{:S(2)}, u32[]{:S(2)}) collective-permute-start(f32[2,32,128]{2,1,0:T(8,128)S(1)} %shard_map.61.here_ref), channel_id=1, source_target_pairs={{0,16},{16,32},{32,48},{48,64},{64,80},{80,96},{96,112},{112,128},... | collective-permute-start | bytes 98312 | tf_op jit(solution)/shard_map/ppermute | solution.py:399
  51.0 13.4 %collective-permute-start.4 = (f32[32,128]{1,0:T(8,128)S(1)}, f32[32,128]{1,0:T(8,128)S(1)}, u32[]{:S(2)}, u32[]{:S(2)}) collective-permute-start(f32[32,128]{1,0:T(8,128)S(1)} %get-tuple-element.13), channel_id=1, source_target_pairs={{0,1},{2,3},{4,5},{6,7},{8,9},{10,11},{12,13},{14,15},{1,0},{3,2},... | collective-permute-start | bytes 49160 | tf_op jit(solution)/shard_map/ppermute | solution.py:418
  54.1 7.2 %collective-permute-start.5 = (f32[8,128]{1,0:T(8,128)S(1)}, f32[8,128]{1,0:T(8,128)S(1)}, u32[]{:S(2)}, u32[]{:S(2)}) collective-permute-start(f32[8,128]{1,0:T(8,128)S(1)} %get-tuple-element.14), channel_id=1, source_target_pairs={{1,2},{3,4},{5,6},{7,8},{9,10},{11,12},{13,14},{2,1},{4,3},{6,5},{... | collective-permute-start | bytes 12296 | tf_op jit(solution)/shard_map/ppermute | solution.py:419
  59.4 4.9 %collective-permute-start.6 = (f32[8,128]{1,0:T(8,128)S(1)}, f32[8,128]{1,0:T(8,128)S(1)}, u32[]{:S(2)}, u32[]{:S(2)}) collective-permute-start(f32[8,128]{1,0:T(8,128)S(1)} %get-tuple-element.15), channel_id=1, source_target_pairs={{1,3},{3,5},{5,7},{7,9},{9,11},{11,13},{13,15},{2,0},{4,2},{6,4},{... | collective-permute-start | bytes 12296 | tf_op jit(solution)/shard_map/ppermute | solution.py:420

commit v3 on v2

v3 whole, which is shorter than its diff:
```python
import functools
import math

import jax
import jax.numpy as jnp
from jax import lax
from jax.experimental import pallas as pl
from jax.experimental.pallas import tpu as pltpu
from jax.sharding import PartitionSpec as P


step_coeff = 0.08
square_coeff = 0.0032
ratio = step_coeff / square_coeff
two_pi = 2.0 * math.pi

HALO = 8
REACH = 16
VMEM = pl.BlockSpec(memory_space=pltpu.VMEM)
SMEM = pl.BlockSpec(memory_space=pltpu.SMEM)
HBM = pl.BlockSpec(memory_space=pltpu.HBM)
small = pltpu.CompilerParams(vmem_limit_bytes=1 << 20)
large = pltpu.CompilerParams(vmem_limit_bytes=8 << 20)


def f32(*shape):
    return jax.ShapeDtypeStruct(shape, jnp.float32)


def lanes_of(shape):
    return lax.broadcasted_iota(jnp.int32, shape, 1)


def turn(x, by):
    by %= 128
    return pltpu.roll(x, by, 1) if by else x


def pack_object(
    ids_ref, phase_ref, atten_ref, measured_ref, angles_ref,
    out_ref, half_ref, head_ref,
    phase, atten, turns, sems,
):
    copies = [
        pltpu.make_async_copy(
            measured_ref.at[0, :, pl.ds(pl.multiple_of(16 * ids_ref[2], 16), 16), :],
            half_ref,
            sems.at[0],
        ),
        pltpu.make_async_copy(angles_ref, turns, sems.at[1]),
        pltpu.make_async_copy(phase_ref, phase, sems.at[2]),
        pltpu.make_async_copy(atten_ref, atten, sems.at[3]),
    ]
    for copy in copies:
        copy.start()
    for copy in copies[1:]:
        copy.wait()
    for n, (ref, layer) in enumerate(((phase, 0), (phase, 1), (atten, 0), (atten, 1))):
        out_ref[:, 32 * n : 32 * n + 32] = ref[layer]
    lane = lanes_of((8, 128))
    head_ref[...] = jnp.where(lane == 0, turns[0, 0], turns[0, 1]).astype(jnp.float32)
    copies[0].wait()


def pack_edges(ids_ref, mine_ref, other_ref, out_ref):
    first = ids_ref[2] == 0
    for pair, (a, b) in enumerate(((mine_ref, other_ref), (other_ref, mine_ref))):
        out_ref[pair] = jnp.where(
            first, jnp.where(first, a[0:8], b[0:8]), jnp.where(first, a[24:32], b[24:32])
        )


def pack_rows(ids_ref, mine_ref, other_ref, edge_ref, out_ref, right_ref, left_ref):
    first = ids_ref[2] == 0
    lane = lanes_of((8, 128))
    spots = 32 * jnp.bitwise_and(lane // 16, 3) + jnp.bitwise_and(lane, 15)
    for block in range(4):
        rows = slice(8 * block, 8 * block + 8)
        both = []
        for pair in range(2):
            refs = (mine_ref, other_ref) if pair == 0 else (other_ref, mine_ref)
            above = refs[0][8 * block - 8 : 8 * block] if block else edge_ref[pair]
            below = refs[1][8 * block + 8 : 8 * block + 16] if block < 3 else edge_ref[pair]
            both.append(jnp.where(first, above, below))
            out_ref[pair, rows] = both[pair]
        for ref, shift in ((right_ref, 16), (left_ref, 0)):
            parts = [picked(x, spots + shift) for x in both]
            ref[rows] = jnp.where(lane < 64, parts[0], parts[1])


def flipped(x):
    rows = 7 - lax.broadcasted_iota(jnp.int32, (8, 128), 0)
    return jnp.take_along_axis(x, rows, axis=0)


def picked(x, lanes):
    return jnp.take_along_axis(x, lanes, axis=1)


def pack_measured(ids_ref, half, head_ref, out_ref, packed, sems):
    lane = lanes_of((8, 128))
    head = head_ref[...]
    zero = jnp.zeros((8, 128), jnp.float32)
    m = jnp.bitwise_and(lane // 16 - ids_ref[0] // 8, 3)
    order = jnp.bitwise_and(lane, 64) + 4 * jnp.bitwise_and(lane, 15) + m
    regs = []
    for comp in range(2):
        first = [half[comp, 0:8, 128 * n : 128 * n + 128] for n in range(8)]
        second = [flipped(half[comp, 8:16, 128 * n : 128 * n + 128]) for n in range(8)]
        regs.append((first, second))
    copies = []
    for j in range(32):
        v, r = divmod(32 * j - REACH, 128)
        for comp in range(2):
            parts = []
            for a in range(2):
                left = regs[comp][a][v] if v >= 0 else zero
                part = turn(left, 64 * a - r)
                if r > 64:
                    right = regs[comp][a][v + 1] if v + 1 < 8 else zero
                    part = jnp.where(lane - 64 * a < 128 - r, part, turn(right, 64 * a - r))
                parts.append(part)
            both = jnp.where(lane < 64, parts[0], parts[1])
            if comp == 0:
                both = jnp.where(lane < 2, head, both)
            packed[j, 8 * comp : 8 * comp + 8] = picked(both, order)
        if j % 8 == 7:
            part = pl.ds(j - 7, 8)
            copies.append(
                pltpu.make_async_copy(packed.at[part], out_ref.at[part], sems.at[j // 8])
            )
            copies[-1].start()
    for copy in copies:
        copy.wait()


def march(
    ids_ref, here_ref, left_ref, right_ref, got_ref,
    mine_ref, other_ref, across_ref, along_ref,
    table, field, stored, sums,
):
    block, slab, cut = ids_ref[0], ids_ref[1], ids_ref[2]
    first = cut == 0
    lane = lanes_of((8, 128))
    sub = lax.broadcasted_iota(jnp.int32, (8, 128), 0)
    upper = lane < 64
    window = jnp.bitwise_and(lane, 63)
    half = jnp.bitwise_and(lane, 64)
    place = jnp.bitwise_and(lane, 15)
    group = jnp.bitwise_and(lane // 16, 3)
    top = 32 * slab + 16 * cut - HALO
    left_column = 32 * block - REACH

    def columns(m):
        return left_column + 4 * place + m

    for q in range(2):
        row = top + jnp.where(upper, 8 * q + sub, 31 - 8 * q - sub)
        row_inside = (row >= 0) & (row < 256)
        column = left_column + window
        inside = row_inside & (column >= 0) & (column < 1024)
        for m in range(4):
            column = columns(m)
            table[8, m, 8 * q : 8 * q + 8] = jnp.where(
                row_inside & (column >= 0) & (column < 1024), square_coeff, 0.0
            )
        for layer in range(4):
            pair, sl = divmod(layer, 2)
            values = []
            for n in (sl, 2 + sl):
                halves = []
                for a, b in ((0, q), (1, 3 - q)):
                    rows = slice(8 * b, 8 * b + 8)
                    at = 64 * (a - pair) - 16 * n
                    halves.append(
                        jnp.where(
                            window < 16,
                            turn(left_ref[rows], at),
                            jnp.where(
                                window < 48,
                                turn(here_ref[pair, rows], 64 * a - 32 * n + 16),
                                turn(right_ref[rows], at + 48),
                            ),
                        )
                    )
                values.append(jnp.where(upper, halves[0], flipped(halves[1])))
            damping = jnp.where(inside, jnp.exp(-values[1]), 0.0)
            re, im = damping * jnp.cos(values[0]), damping * jnp.sin(values[0])
            for m in range(4):
                lanes = half + 4 * place + m
                table[2 * layer, m, 8 * q : 8 * q + 8] = picked(re, lanes)
                table[2 * layer + 1, m, 8 * q : 8 * q + 8] = picked(im, lanes)

    def spread(n, m, r):
        return jnp.broadcast_to(table[n, m, r : r + 1], (8, 128))

    def side(x, m):
        before = x[m - 1] if m else turn(x[3], 1)
        after = x[m + 1] if m < 3 else turn(x[0], 127)
        return before + after

    def diffract(source, begin, inner, orient, emit):
        rows, scaled = {}, {}

        def around(values, r, k, m):
            parts = [values[n][k][m] for n in (r - 1, r + 1) if n in values]
            if r in values:
                parts.append(side(values[r][k], m))
            return functools.reduce(lambda x, y: x + y, parts)

        def scale(r):
            out = []
            for k in range(2):
                new = []
                for m in range(4):
                    total = around(rows, r, k, m)
                    if r in rows:
                        total = total - 4.0 * rows[r][k][m]
                    new.append(spread(8, m, r) * total)
                out.append(new)
            scaled[r] = out

        def finish(r):
            for m in range(4):
                re, im = (-around(scaled, r, k, m) for k in range(2))
                if r in rows:
                    re, im = re + rows[r][0][m], im + rows[r][1][m]
                if r in scaled:
                    mre, mim = scaled[r][0][m], scaled[r][1][m]
                    turned = orient * ratio
                    re = re + (4.0 * mre - turned * mim)
                    im = im + (4.0 * mim + turned * mre)
                emit(r, m, re, im)

        def advance(r):
            if r - 1 >= begin + inner:
                scale(r - 1)
            if r - 2 >= begin + 2 * inner:
                finish(r - 2)

        def opposite(row):
            return [[turn(x, 64) for x in part] for part in row]

        for r in range(begin, 16):
            rows[r] = source(r)
            advance(r)
        rows[16] = opposite(rows[15])
        advance(16)
        scaled[16] = opposite(scaled[15])
        finish(15)

    def received(comp, k):
        parts = [
            got_ref[pl.ds(128 * n + 8 * comp + k, 8, stride=16), :] for n in range(4)
        ]
        out = []
        for m in range(4):
            x = parts[3]
            for n in range(3):
                x = jnp.where(group == (m + n) % 4, parts[n], x)
            if m:
                x = picked(x, half + 16 * jnp.bitwise_and(group + m, 3) + place)
            out.append(x)
        return out

    head = received(0, 0)
    corner = jnp.bitwise_and(lane, 48)
    row_turns = picked(head[0], corner)
    col_turns = picked(head[1], corner)
    row0 = (top + jnp.where(upper, 0, 31)).astype(jnp.float32)
    row_part = row_turns * row0 * (1.0 / 256.0)
    col_part = col_turns * columns(0).astype(jnp.float32) * (1.0 / 1024.0)
    row_part = row_part - jnp.floor(row_part)
    col_part = col_part - jnp.floor(col_part)

    def unit(t):
        return jnp.cos(t), jnp.sin(t)

    def times(a, b):
        return a[0] * b[0] - a[1] * b[1], a[0] * b[1] + a[1] * b[0]

    wave = [unit(two_pi * (row_part + col_part))]
    step = unit(two_pi / 256.0 * row_turns * jnp.where(upper, 1.0, -1.0))
    across = unit(two_pi / 1024.0 * col_turns)
    for _ in range(3):
        wave.append(times(wave[-1], across))
    waves = [wave]

    def from_wave(r):
        while len(waves) <= r:
            waves.append([times(x, step) for x in waves[-1]])
        return [[x[k] for x in waves[r]] for k in range(2)]

    def from_field(r):
        return [[field[k, r, m] for m in range(4)] for k in range(2)]

    def forward(layer):
        def source(r):
            re, im = from_wave(r) if layer == 0 else from_field(r)
            out = ([], [])
            for m in range(4):
                v = times((spread(2 * layer, m, r), spread(2 * layer + 1, m, r)), (re[m], im[m]))
                for k in range(2):
                    stored[2 * layer + k, r, m] = v[k]
                    out[k].append(v[k])
            return out

        measured_rows = {}

        def emit(r, m, re, im):
            if layer < 3:
                field[0, r, m], field[1, r, m] = re, im
                return
            if r not in measured_rows:
                measured_rows[r] = [received(k, r - 8) for k in range(2)]
            column = columns(m)
            keep = (column >= 0) & (column < 1024)
            field[0, r, m] = jnp.where(keep, re - measured_rows[r][0][m], 0.0)
            field[1, r, m] = jnp.where(keep, im - measured_rows[r][1][m], 0.0)

        diffract(source, 2 * layer, 1, 1.0, emit)

    def backward(layer):
        def emit(r, m, re, im):
            vre, vim = stored[2 * layer, r, m], stored[2 * layer + 1, r, m]
            for out, x in enumerate((vre * im - vim * re, -(vre * re) - vim * im)):
                sums[2 * layer + out, m, r : r + 1] = jnp.sum(x, axis=0, keepdims=True)
            if layer:
                a, b = spread(2 * layer, m, r), spread(2 * layer + 1, m, r)
                field[0, r, m], field[1, r, m] = a * re + b * im, a * im - b * re

        diffract(from_field, 2 * layer + 2, -1, -1.0, emit)

    for layer in range(4):
        forward(layer)
        for n in range(2):
            for m in range(4):
                if layer:
                    sums[2 * layer + n, m, 0 : 2 * layer] = jnp.zeros((2 * layer, 128))
    for layer in (3, 2, 1, 0):
        backward(layer)

    spots = half + 48 + window // 4

    def plain(n, q):
        out = None
        for m in range(4):
            x = sums[n, m, 8 * q : 8 * q + 8]
            x = x + turn(x, 16)
            x = picked(x + turn(x, 32), spots)
            out = x if out is None else jnp.where(jnp.bitwise_and(lane, 3) == m, x, out)
        return out

    blocks = [[None] * 4 for _ in range(2)]
    for pair in range(2):
        for q in range(2):
            for n in range(4):
                out, sl = divmod(n, 2)
                x = plain(2 * (2 * pair + sl) + out, q)
                for b, y in ((q, turn(x, 32 * n - 16)), (3 - q, turn(x, 32 * n - 80))):
                    old = blocks[pair][b]
                    blocks[pair][b] = y if old is None else jnp.where(lane < 32 * n, old, y)
        for b in (2, 3):
            blocks[pair][b] = flipped(blocks[pair][b])
    mine = [jnp.where(first, a, b) for a, b in zip(*blocks)]
    other = [jnp.where(first, b, a) for a, b in zip(*blocks)]
    none = jnp.zeros((8, 128), jnp.float32)
    for parts, ref in ((mine, mine_ref), (other, other_ref)):
        for b in range(4):
            ref[8 * b : 8 * b + 8] = jnp.where(
                first, parts[b + 1] if b < 3 else none, parts[b - 1] if b > 0 else none
            )
    across_ref[...] = jnp.where(first, other[0], other[3])
    along_ref[...] = jnp.where(first, mine[0], mine[3])


def combine(ids_ref, mine_ref, other_ref, across_ref, along_ref, phase_ref, atten_ref):
    first = ids_ref[2] == 0
    for b in range(4):
        rows = slice(8 * b, 8 * b + 8)
        total = mine_ref[rows] + other_ref[rows]
        if b == 0:
            total = total + jnp.where(first, across_ref[...], along_ref[...])
        if b == 3:
            total = total + jnp.where(first, along_ref[...], across_ref[...])
        for sl in range(2):
            phase_ref[sl, rows] = turn(total, -32 * sl)[:, 0:32]
            atten_ref[sl, rows] = turn(total, -64 - 32 * sl)[:, 0:32]


def body(phase_delay, attenuation, measured, angles):
    block = lax.axis_index("illum")
    slab = lax.axis_index("slab")
    cut = lax.axis_index("cuts")
    ids = jnp.stack([block, slab, cut]).astype(jnp.int32)
    n_slabs, n_blocks = lax.axis_size("slab"), lax.axis_size("illum")
    rows_axis = ("slab", "cuts")

    def both_ways(pairs):
        return pairs + [(b, a) for a, b in pairs]

    partner = both_ways([(2 * s, 2 * s + 1) for s in range(n_slabs)])
    across = both_ways([(2 * s + 1, 2 * s + 2) for s in range(n_slabs - 1)])
    along = [(2 * s + 1, 2 * s + 3) for s in range(n_slabs - 1)]
    along += [(2 * s + 2, 2 * s) for s in range(n_slabs - 1)]

    phase_delay, attenuation, measured, angles = (
        pltpu.with_memory_space_constraint(x, pltpu.HBM)
        for x in (phase_delay, attenuation, measured, angles)
    )
    mine, half, head = pl.pallas_call(
        pack_object,
        out_shape=(f32(32, 128), f32(2, 16, 1024), f32(8, 128)),
        in_specs=[SMEM] + [HBM] * 4,
        out_specs=(VMEM,) * 3,
        scratch_shapes=[
            pltpu.VMEM((2, 32, 32), jnp.float32),
            pltpu.VMEM((2, 32, 32), jnp.float32),
            pltpu.SMEM((1, 2), jnp.int32),
            pltpu.SemaphoreType.DMA((4,)),
        ],
        compiler_params=small,
    )(ids, phase_delay, attenuation, measured, angles)
    other = lax.ppermute(mine, rows_axis, partner)
    sent = pl.pallas_call(
        pack_measured,
        out_shape=f32(32, 16, 128),
        in_specs=[SMEM, VMEM, VMEM],
        out_specs=HBM,
        scratch_shapes=[
            pltpu.VMEM((32, 16, 128), jnp.float32),
            pltpu.SemaphoreType.DMA((4,)),
        ],
        compiler_params=small,
    )(ids, half, head)
    edges = pl.pallas_call(
        pack_edges,
        out_shape=f32(2, 8, 128),
        in_specs=[SMEM, VMEM, VMEM],
        out_specs=VMEM,
        compiler_params=small,
    )(ids, mine, other)
    edges = lax.ppermute(edges, rows_axis, across)
    got = lax.all_to_all(sent, "illum", 0, 0, tiled=True)
    here, to_right, to_left = pl.pallas_call(
        pack_rows,
        out_shape=(f32(2, 32, 128), f32(32, 128), f32(32, 128)),
        in_specs=[SMEM] + [VMEM] * 3,
        out_specs=(VMEM,) * 3,
        compiler_params=small,
    )(ids, mine, other, edges)
    from_left = lax.ppermute(to_right, "illum", [(i, i + 1) for i in range(n_blocks - 1)])
    from_right = lax.ppermute(to_left, "illum", [(i + 1, i) for i in range(n_blocks - 1)])

    mine, other, across_part, along_part = pl.pallas_call(
        march,
        out_shape=(f32(32, 128), f32(32, 128), f32(8, 128), f32(8, 128)),
        in_specs=[SMEM] + [VMEM] * 4,
        out_specs=(VMEM,) * 4,
        scratch_shapes=[
            pltpu.VMEM((9, 4, 16, 128), jnp.float32),
            pltpu.VMEM((2, 16, 4, 8, 128), jnp.float32),
            pltpu.VMEM((8, 16, 4, 8, 128), jnp.float32),
            pltpu.VMEM((8, 4, 16, 128), jnp.float32),
        ],
        compiler_params=large,
    )(ids, here, from_left, from_right, got.reshape(512, 128))
    other = lax.ppermute(other, rows_axis, partner)
    across_part = lax.ppermute(across_part, rows_axis, across)
    along_part = lax.ppermute(along_part, rows_axis, along)
    return pl.pallas_call(
        combine,
        out_shape=(f32(2, 32, 32), f32(2, 32, 32)),
        in_specs=[SMEM] + [VMEM] * 4,
        out_specs=(VMEM, VMEM),
        compiler_params=small,
    )(ids, mine, other, across_part, along_part)


def solution(mesh):
    placed = (
        P("cuts", "slab", "illum"),
        P("cuts", "slab", "illum"),
        P("illum", None, "slab", None),
        P("illum", None),
    )
    return jax.shard_map(
        body,
        mesh=mesh,
        in_specs=placed,
        out_specs=(P("cuts", "slab", "illum"), P("cuts", "slab", "illum")),
        check_vma=False,
    )
```

time: 66 us -> 65.7 us (level)
  the two profiles are of different devices: /device:TPU:69 before, /device:TPU:21 now
where the time goes in v3:
time: 65.7 us; the launch traced here: 65.3 us
  starting transfers between devices  40.9 us (62%)
  waiting for transfers between devices  12 us (18%)
  Pallas kernels  11.6 us (18%)
  between operations  0.76 us (1%)
    all_to_all x1, starting transfers between devices, body(): got = lax.all_to_all(sent, 'illum', 0, 0, tiled=True)  15.5 us
    ppermute x1, starting transfers between devices, body(): across_part = lax.ppermute(across_part, rows_axis, across)  5.62 us
    ppermute x1, starting transfers between devices, body(): edges = lax.ppermute(edges, rows_axis, across)  5.09 us
    ppermute x1, starting transfers between devices, body(): lax.ppermute(to_right, 'illum', [(i, i + 1) for i in range(n_blocks - 1)])  4.99 us
    ppermute x1, waiting for transfers between devices, body(): lax.ppermute(to_left, 'illum', [(i + 1, i) for i in range(n_blocks - 1)])  4.65 us
    pallas_call x1, Pallas kernels, body(): pl.pallas_call(march, out_shape=(f32(32, 128), f32(32, 128), f32(8, 128),...  4.24 us
    ppermute x1, starting transfers between devices, body(): other = lax.ppermute(other, rows_axis, partner)  3.53 us
    pallas_call x1, Pallas kernels, body(): pl.pallas_call(pack_measured, out_shape=f32(32, 16, 128), in_specs=[SMEM,...  3.41 us
  transfers between devices with their start and end apart: 8, of which 4 were waited for; matrix products, arithmetic and copies ran while one was open for 0% of the time, Pallas kernels for 2%

profile of v3, /device:TPU:21, one launch (start us, length us, event | category | flops | bytes accessed | tf_op | source)
XLA Modules:
  0.0 65.3 jit_solution(16076503190218456192)
XLA Ops:
  0.6 0.1 pad_add_fusion.ids_ref
  0.7 1.5 %shard_map.59 = (f32[32,128]{1,0:T(8,128)S(1)}, f32[2,16,1024]{2,1,0:T(8,128)S(1)}, f32[8,128]{1,0:T(8,128)S(1)}) custom-call(s32[3]{0:T(128)S(1)} %pad_add_fusion.ids_ref, f32[2,32,32]{2,1,0:T(8,128)} %phase_ref.1, f32[2,32,32]{2,1,0:T(8,128)} %atten_ref.1, f32[1,2,32,1024]{3,2,1,0:T(8,128)} %measured_ref.1, s32[1,2]{1,0:T(1,128)} %angles_ref.1), custom_call_target="tpu_custom_call" | custom-call | tf_op jit(solution)/shard_map/pallas_call | solution.py:411
  2.2 3.4 %shard_map.62 = f32[32,16,128]{2,1,0:T(8,128)} custom-call(s32[3]{0:T(128)S(1)} %pad_add_fusion.ids_ref, f32[2,16,1024]{2,1,0:T(8,128)S(1)} %get-tuple-element.16.half, f32[8,128]{1,0:T(8,128)S(1)} %get-tuple-element.17.head_ref), custom_call_target="tpu_custom_call" | custom-call | tf_op jit(solution)/shard_map/pallas_call | solution.py:425
  5.6 15.5 %all-to-all-start = ((f32[32,16,128]{2,1,0:T(8,128)}), f32[32,16,128]{2,1,0:T(8,128)S(1)}, u32[]{:S(2)}, u32[]{:S(2)}) async-start(f32[32,16,128]{2,1,0:T(8,128)} %shard_map.62), calls=%async_computation | async-start | bytes 524288 | tf_op jit(solution)/shard_map/all_to_all | solution.py:444
  21.2 2.3 %collective-permute-start = (f32[32,128]{1,0:T(8,128)S(1)}, f32[32,128]{1,0:T(8,128)S(1)}, u32[]{:S(2)}, u32[]{:S(2)}) collective-permute-start(f32[32,128]{1,0:T(8,128)S(1)} %get-tuple-element.12.mine_ref), channel_id=1, source_target_pairs={{0,1},{2,3},{4,5},{6,7},{8,9},{10,11},{12,13},{14,15},{1,0},{3,2},... | collective-permute-start | bytes 49160 | tf_op jit(solution)/shard_map/ppermute | solution.py:424
  23.5 2.8 %collective-permute-done.other_ref = f32[32,128]{1,0:T(8,128)S(1)} collective-permute-done((f32[32,128]{1,0:T(8,128)S(1)}, f32[32,128]{1,0:T(8,128)S(1)}, u32[]{:S(2)}, u32[]{:S(2)}) %collective-permute-start) | collective-permute-done | bytes 16416 | tf_op jit(solution)/shard_map/ppermute | solution.py:424
  26.2 0.5 shard_map.60
  26.8 5.1 %collective-permute-start.1 = (f32[2,8,128]{2,1,0:T(8,128)S(1)}, f32[2,8,128]{2,1,0:T(8,128)S(1)}, u32[]{:S(2)}, u32[]{:S(2)}) collective-permute-start(f32[2,8,128]{2,1,0:T(8,128)S(1)} %shard_map.60), channel_id=1, source_target_pairs={{1,2},{3,4},{5,6},{7,8},{9,10},{11,12},{13,14},{2,1},{4,3},{6,5},{... | collective-permute-start | bytes 24584 | tf_op jit(solution)/shard_map/ppermute | solution.py:443
  31.9 1.6 %collective-permute-done.1.edge_ref = f32[2,8,128]{2,1,0:T(8,128)S(1)} collective-permute-done((f32[2,8,128]{2,1,0:T(8,128)S(1)}, f32[2,8,128]{2,1,0:T(8,128)S(1)}, u32[]{:S(2)}, u32[]{:S(2)}) %collective-permute-start.1) | collective-permute-done | bytes 8224 | tf_op jit(solution)/shard_map/ppermute | solution.py:443
  33.5 0.6 shard_map.61
  34.1 5.0 %collective-permute-start.2 = (f32[32,128]{1,0:T(8,128)S(1)}, f32[32,128]{1,0:T(8,128)S(1)}, u32[]{:S(2)}, u32[]{:S(2)}) collective-permute-start(f32[32,128]{1,0:T(8,128)S(1)} %get-tuple-element.14), channel_id=1, source_target_pairs={{0,16},{16,32},{32,48},{48,64},{64,80},{80,96},{96,112},{112,128},... | collective-permute-start | bytes 49160 | tf_op jit(solution)/shard_map/ppermute | solution.py:452
  39.1 1.9 %collective-permute-start.3 = (f32[32,128]{1,0:T(8,128)S(1)}, f32[32,128]{1,0:T(8,128)S(1)}, u32[]{:S(2)}, u32[]{:S(2)}) collective-permute-start(f32[32,128]{1,0:T(8,128)S(1)} %get-tuple-element.15), channel_id=1, source_target_pairs={{16,0},{32,16},{48,32},{64,48},{80,64},{96,80},{112,96},{128,112},... | collective-permute-start | bytes 49160 | tf_op jit(solution)/shard_map/ppermute | solution.py:453
  41.1 0.0 collective-permute-done.2.left_ref
  41.1 4.7 %collective-permute-done.3.right_ref = f32[32,128]{1,0:T(8,128)S(1)} collective-permute-done((f32[32,128]{1,0:T(8,128)S(1)}, f32[32,128]{1,0:T(8,128)S(1)}, u32[]{:S(2)}, u32[]{:S(2)}) %collective-permute-start.3) | collective-permute-done | bytes 16416 | tf_op jit(solution)/shard_map/ppermute | solution.py:453
  45.7 0.0 all-to-all-done
  45.7 4.2 %shard_map.63 = (f32[32,128]{1,0:T(8,128)S(1)}, f32[32,128]{1,0:T(8,128)S(1)}, f32[8,128]{1,0:T(8,128)S(1)}, f32[8,128]{1,0:T(8,128)S(1)}) custom-call(s32[3]{0:T(128)S(1)} %pad_add_fusion.ids_ref, f32[2,32,128]{2,1,0:T(8,128)S(1)} %get-tuple-element.13.here_ref, f32[32,128]{1,0:T(8,128)S(1)} %collective-permute-done.2.left_ref, ...), custom_call_target="tpu_custom_call" | custom-call | tf_op jit(solution)/shard_map/pallas_call | solution.py:455
  50.0 3.5 %collective-permute-start.4 = (f32[32,128]{1,0:T(8,128)S(1)}, f32[32,128]{1,0:T(8,128)S(1)}, u32[]{:S(2)}, u32[]{:S(2)}) collective-permute-start(f32[32,128]{1,0:T(8,128)S(1)} %get-tuple-element.19), channel_id=1, source_target_pairs={{0,1},{2,3},{4,5},{6,7},{8,9},{10,11},{12,13},{14,15},{1,0},{3,2},... | collective-permute-start | bytes 49160 | tf_op jit(solution)/shard_map/ppermute | solution.py:468
  53.5 5.6 %collective-permute-start.5 = (f32[8,128]{1,0:T(8,128)S(1)}, f32[8,128]{1,0:T(8,128)S(1)}, u32[]{:S(2)}, u32[]{:S(2)}) collective-permute-start(f32[8,128]{1,0:T(8,128)S(1)} %get-tuple-element.20), channel_id=1, source_target_pairs={{1,2},{3,4},{5,6},{7,8},{9,10},{11,12},{13,14},{2,1},{4,3},{6,5},{... | collective-permute-start | bytes 12296 | tf_op jit(solution)/shard_map/ppermute | solution.py:469
  59.2 1.9 %collective-permute-start.6 = (f32[8,128]{1,0:T(8,128)S(1)}, f32[8,128]{1,0:T(8,128)S(1)}, u32[]{:S(2)}, u32[]{:S(2)}) collective-permute-start(f32[8,128]{1,0:T(8,128)S(1)} %get-tuple-element.21), channel_id=1, source_target_pairs={{1,3},{3,5},{5,7},{7,9},{9,11},{11,13},{13,15},{2,0},{4,2},{6,4},{... | collective-permute-start | bytes 12296 | tf_op jit(solution)/shard_map/ppermute | solution.py:470
  61.1 0.0 collective-permute-done.5.across_ref
  61.1 3.0 %collective-permute-done.6.along_ref = f32[8,128]{1,0:T(8,128)S(1)} collective-permute-done((f32[8,128]{1,0:T(8,128)S(1)}, f32[8,128]{1,0:T(8,128)S(1)}, u32[]{:S(2)}, u32[]{:S(2)}) %collective-permute-start.6) | collective-permute-done | bytes 4128 | tf_op jit(solution)/shard_map/ppermute | solution.py:470
  64.1 0.0 collective-permute-done.4.other_ref
  64.1 1.2 %shard_map.64 = (f32[2,32,32]{2,1,0:T(8,128)}, f32[2,32,32]{2,1,0:T(8,128)}) custom-call(s32[3]{0:T(128)S(1)} %pad_add_fusion.ids_ref, f32[32,128]{1,0:T(8,128)S(1)} %get-tuple-element.18.mine_ref, f32[32,128]{1,0:T(8,128)S(1)} %collective-permute-done.4.other_ref, f32[8,128]{1,0:T(8,128)S(1)} %collective-permute-done.5.across_ref, ...), custom_call_target="tpu_custom_call" | custom-call | tf_op jit(solution)/shard_map/pallas_call | solution.py:471
Async XLA Ops:
  5.6 40.1 %all-to-all-start = ((f32[32,16,128]{2,1,0:T(8,128)}), f32[32,16,128]{2,1,0:T(8,128)S(1)}, u32[]{:S(2)}, u32[]{:S(2)}) async-start(f32[32,16,128]{2,1,0:T(8,128)} %shard_map.62), calls=%async_computation | async-start | bytes 524288 | tf_op jit(solution)/shard_map/all_to_all | solution.py:444
  21.2 5.1 %collective-permute-start = (f32[32,128]{1,0:T(8,128)S(1)}, f32[32,128]{1,0:T(8,128)S(1)}, u32[]{:S(2)}, u32[]{:S(2)}) collective-permute-start(f32[32,128]{1,0:T(8,128)S(1)} %get-tuple-element.12.mine_ref), channel_id=1, source_target_pairs={{0,1},{2,3},{4,5},{6,7},{8,9},{10,11},{12,13},{14,15},{1,0},{3,2},... | collective-permute-start | bytes 49160 | tf_op jit(solution)/shard_map/ppermute | solution.py:424
  26.8 6.7 %collective-permute-start.1 = (f32[2,8,128]{2,1,0:T(8,128)S(1)}, f32[2,8,128]{2,1,0:T(8,128)S(1)}, u32[]{:S(2)}, u32[]{:S(2)}) collective-permute-start(f32[2,8,128]{2,1,0:T(8,128)S(1)} %shard_map.60), channel_id=1, source_target_pairs={{1,2},{3,4},{5,6},{7,8},{9,10},{11,12},{13,14},{2,1},{4,3},{6,5},{... | collective-permute-start | bytes 24584 | tf_op jit(solution)/shard_map/ppermute | solution.py:443
  34.1 6.9 %collective-permute-start.2 = (f32[32,128]{1,0:T(8,128)S(1)}, f32[32,128]{1,0:T(8,128)S(1)}, u32[]{:S(2)}, u32[]{:S(2)}) collective-permute-start(f32[32,128]{1,0:T(8,128)S(1)} %get-tuple-element.14), channel_id=1, source_target_pairs={{0,16},{16,32},{32,48},{48,64},{64,80},{80,96},{96,112},{112,128},... | collective-permute-start | bytes 49160 | tf_op jit(solution)/shard_map/ppermute | solution.py:452
  39.1 6.6 %collective-permute-start.3 = (f32[32,128]{1,0:T(8,128)S(1)}, f32[32,128]{1,0:T(8,128)S(1)}, u32[]{:S(2)}, u32[]{:S(2)}) collective-permute-start(f32[32,128]{1,0:T(8,128)S(1)} %get-tuple-element.15), channel_id=1, source_target_pairs={{16,0},{32,16},{48,32},{64,48},{80,64},{96,80},{112,96},{128,112},... | collective-permute-start | bytes 49160 | tf_op jit(solution)/shard_map/ppermute | solution.py:453
  50.0 14.1 %collective-permute-start.4 = (f32[32,128]{1,0:T(8,128)S(1)}, f32[32,128]{1,0:T(8,128)S(1)}, u32[]{:S(2)}, u32[]{:S(2)}) collective-permute-start(f32[32,128]{1,0:T(8,128)S(1)} %get-tuple-element.19), channel_id=1, source_target_pairs={{0,1},{2,3},{4,5},{6,7},{8,9},{10,11},{12,13},{14,15},{1,0},{3,2},... | collective-permute-start | bytes 49160 | tf_op jit(solution)/shard_map/ppermute | solution.py:468
  53.5 7.6 %collective-permute-start.5 = (f32[8,128]{1,0:T(8,128)S(1)}, f32[8,128]{1,0:T(8,128)S(1)}, u32[]{:S(2)}, u32[]{:S(2)}) collective-permute-start(f32[8,128]{1,0:T(8,128)S(1)} %get-tuple-element.20), channel_id=1, source_target_pairs={{1,2},{3,4},{5,6},{7,8},{9,10},{11,12},{13,14},{2,1},{4,3},{6,5},{... | collective-permute-start | bytes 12296 | tf_op jit(solution)/shard_map/ppermute | solution.py:469
  59.2 4.9 %collective-permute-start.6 = (f32[8,128]{1,0:T(8,128)S(1)}, f32[8,128]{1,0:T(8,128)S(1)}, u32[]{:S(2)}, u32[]{:S(2)}) collective-permute-start(f32[8,128]{1,0:T(8,128)S(1)} %get-tuple-element.21), channel_id=1, source_target_pairs={{1,3},{3,5},{5,7},{7,9},{9,11},{11,13},{13,15},{2,0},{4,2},{6,4},{... | collective-permute-start | bytes 12296 | tf_op jit(solution)/shard_map/ppermute | solution.py:470

commit v4 on v3

--- a/solution.py
+++ b/solution.py
@@ -38,7 +38,7 @@
 
 def pack_object(
     ids_ref, phase_ref, atten_ref, measured_ref, angles_ref,
-    out_ref, half_ref, head_ref,
+    out_ref, half_ref, head_ref, place_ref,
     phase, atten, turns, sems,
 ):
     copies = [
@@ -53,6 +53,8 @@
     ]
     for copy in copies:
         copy.start()
+    for n in range(3):
+        place_ref[n] = jnp.full((8, 128), ids_ref[n], jnp.int32)
     for copy in copies[1:]:
         copy.wait()
     for n, (ref, layer) in enumerate(((phase, 0), (phase, 1), (atten, 0), (atten, 1))):
@@ -62,16 +64,16 @@
     copies[0].wait()
 
 
-def pack_edges(ids_ref, mine_ref, other_ref, out_ref):
-    first = ids_ref[2] == 0
+def pack_edges(place_ref, mine_ref, other_ref, out_ref):
+    first = place_ref[2] == 0
     for pair, (a, b) in enumerate(((mine_ref, other_ref), (other_ref, mine_ref))):
         out_ref[pair] = jnp.where(
             first, jnp.where(first, a[0:8], b[0:8]), jnp.where(first, a[24:32], b[24:32])
         )
 
 
-def pack_rows(ids_ref, mine_ref, other_ref, edge_ref, out_ref, right_ref, left_ref):
-    first = ids_ref[2] == 0
+def pack_rows(place_ref, mine_ref, other_ref, edge_ref, out_ref, right_ref, left_ref):
+    first = place_ref[2] == 0
     lane = lanes_of((8, 128))
     spots = 32 * jnp.bitwise_and(lane // 16, 3) + jnp.bitwise_and(lane, 15)
     for block in range(4):
@@ -97,12 +99,36 @@
     return jnp.take_along_axis(x, lanes, axis=1)
 
 
-def pack_measured(ids_ref, half, head_ref, out_ref, packed, sems):
+def thirds(x):
+    parts = []
+    for _ in range(3):
+        part = x.astype(jnp.bfloat16)
+        x = x - part.astype(jnp.float32)
+        parts.append(part)
+    return jnp.concatenate(parts, axis=1)
+
+
+def permuted(x, chosen):
+    ones = jnp.where(chosen, 1.0, 0.0).astype(jnp.bfloat16)
+    return jnp.dot(
+        thirds(x),
+        jnp.concatenate([ones] * 3, axis=0),
+        preferred_element_type=jnp.float32,
+    )
+
+
+def square_iotas(width=128):
+    shape = (128, width)
+    return lax.broadcasted_iota(jnp.int32, shape, 0), lanes_of(shape)
+
+
+def pack_measured(place_ref, half, head_ref, out_ref, plain, packed, sems):
     lane = lanes_of((8, 128))
     head = head_ref[...]
     zero = jnp.zeros((8, 128), jnp.float32)
-    m = jnp.bitwise_and(lane // 16 - ids_ref[0] // 8, 3)
-    order = jnp.bitwise_and(lane, 64) + 4 * jnp.bitwise_and(lane, 15) + m
+    source, target = square_iotas()
+    m = jnp.bitwise_and(target // 16 - jnp.tile(place_ref[0] // 8, (16, 1)), 3)
+    chosen = source == jnp.bitwise_and(target, 64) + 4 * jnp.bitwise_and(target, 15) + m
     regs = []
     for comp in range(2):
         first = [half[comp, 0:8, 128 * n : 128 * n + 128] for n in range(8)]
@@ -123,9 +149,11 @@
             both = jnp.where(lane < 64, parts[0], parts[1])
             if comp == 0:
                 both = jnp.where(lane < 2, head, both)
-            packed[j, 8 * comp : 8 * comp + 8] = picked(both, order)
+            plain[16 * j + 8 * comp : 16 * j + 8 * comp + 8] = both
         if j % 8 == 7:
             part = pl.ds(j - 7, 8)
+            moved = permuted(plain[16 * j - 112 : 16 * j + 16], chosen)
+            packed[part] = moved.reshape(8, 16, 128)
             copies.append(
                 pltpu.make_async_copy(packed.at[part], out_ref.at[part], sems.at[j // 8])
             )
@@ -135,11 +163,11 @@
 
 
 def march(
-    ids_ref, here_ref, left_ref, right_ref, got_ref,
+    place_ref, here_ref, left_ref, right_ref, got_ref,
     mine_ref, other_ref, across_ref, along_ref,
-    table, field, stored, sums,
+    table, flat, field, stored, sums,
 ):
-    block, slab, cut = ids_ref[0], ids_ref[1], ids_ref[2]
+    block, slab, cut = place_ref[0], place_ref[1], place_ref[2]
     first = cut == 0
     lane = lanes_of((8, 128))
     sub = lax.broadcasted_iota(jnp.int32, (8, 128), 0)
@@ -186,10 +214,13 @@
                 values.append(jnp.where(upper, halves[0], flipped(halves[1])))
             damping = jnp.where(inside, jnp.exp(-values[1]), 0.0)
             re, im = damping * jnp.cos(values[0]), damping * jnp.sin(values[0])
-            for m in range(4):
-                lanes = half + 4 * place + m
-                table[2 * layer, m, 8 * q : 8 * q + 8] = picked(re, lanes)
-                table[2 * layer + 1, m, 8 * q : 8 * q + 8] = picked(im, lanes)
+            flat[32 * layer + 8 * q : 32 * layer + 8 * q + 8] = re
+            flat[32 * layer + 8 * q + 16 : 32 * layer + 8 * q + 24] = im
+    source, target = square_iotas(512)
+    spot = jnp.bitwise_and(target, 64) + 4 * jnp.bitwise_and(target, 15) + target // 128
+    wide = permuted(flat[...], source == spot)
+    for m in range(4):
+        table[0:8, m] = wide[:, 128 * m : 128 * m + 128].reshape(8, 16, 128)
 
     def spread(n, m, r):
         return jnp.broadcast_to(table[n, m, r : r + 1], (8, 128))
@@ -222,9 +253,11 @@
 
         def finish(r):
             for m in range(4):
-                re, im = (-around(scaled, r, k, m) for k in range(2))
+                re, im = (around(scaled, r, k, m) for k in range(2))
                 if r in rows:
-                    re, im = re + rows[r][0][m], im + rows[r][1][m]
+                    re, im = rows[r][0][m] - re, rows[r][1][m] - im
+                else:
+                    re, im = -re, -im
                 if r in scaled:
                     mre, mim = scaled[r][0][m], scaled[r][1][m]
                     turned = orient * ratio
@@ -323,7 +356,7 @@
     def backward(layer):
         def emit(r, m, re, im):
             vre, vim = stored[2 * layer, r, m], stored[2 * layer + 1, r, m]
-            for out, x in enumerate((vre * im - vim * re, -(vre * re) - vim * im)):
+            for out, x in enumerate((vre * im - vim * re, vre * re + vim * im)):
                 sums[2 * layer + out, m, r : r + 1] = jnp.sum(x, axis=0, keepdims=True)
             if layer:
                 a, b = spread(2 * layer, m, r), spread(2 * layer + 1, m, r)
@@ -340,16 +373,19 @@
     for layer in (3, 2, 1, 0):
         backward(layer)
 
-    spots = half + 48 + window // 4
+    source, target = square_iotas()
+    near = (jnp.bitwise_and(source, 64) == jnp.bitwise_and(target, 64)) & (
+        jnp.bitwise_and(source, 15) == jnp.bitwise_and(target, 63) // 4
+    )
+    total = None
+    for m in range(4):
+        x = sums[:, m].reshape(128, 128)
+        x = permuted(x, near & (jnp.bitwise_and(target, 3) == m))
+        total = x if total is None else total + x
+    flat[...] = total
 
     def plain(n, q):
-        out = None
-        for m in range(4):
-            x = sums[n, m, 8 * q : 8 * q + 8]
-            x = x + turn(x, 16)
-            x = picked(x + turn(x, 32), spots)
-            out = x if out is None else jnp.where(jnp.bitwise_and(lane, 3) == m, x, out)
-        return out
+        return flat[16 * n + 8 * q : 16 * n + 8 * q + 8]
 
     blocks = [[None] * 4 for _ in range(2)]
     for pair in range(2):
@@ -357,6 +393,7 @@
             for n in range(4):
                 out, sl = divmod(n, 2)
                 x = plain(2 * (2 * pair + sl) + out, q)
+                x = -x if out else x
                 for b, y in ((q, turn(x, 32 * n - 16)), (3 - q, turn(x, 32 * n - 80))):
                     old = blocks[pair][b]
                     blocks[pair][b] = y if old is None else jnp.where(lane < 32 * n, old, y)
@@ -374,8 +411,8 @@
     along_ref[...] = jnp.where(first, mine[0], mine[3])
 
 
-def combine(ids_ref, mine_ref, other_ref, across_ref, along_ref, phase_ref, atten_ref):
-    first = ids_ref[2] == 0
+def combine(place_ref, mine_ref, other_ref, across_ref, along_ref, phase_ref, atten_ref):
+    first = place_ref[2] == 0
     for b in range(4):
         rows = slice(8 * b, 8 * b + 8)
         total = mine_ref[rows] + other_ref[rows]
@@ -408,11 +445,16 @@
         pltpu.with_memory_space_constraint(x, pltpu.HBM)
         for x in (phase_delay, attenuation, measured, angles)
     )
-    mine, half, head = pl.pallas_call(
+    mine, half, head, place = pl.pallas_call(
         pack_object,
-        out_shape=(f32(32, 128), f32(2, 16, 1024), f32(8, 128)),
+        out_shape=(
+            f32(32, 128),
+            f32(2, 16, 1024),
+            f32(8, 128),
+            jax.ShapeDtypeStruct((3, 8, 128), jnp.int32),
+        ),
         in_specs=[SMEM] + [HBM] * 4,
-        out_specs=(VMEM,) * 3,
+        out_specs=(VMEM,) * 4,
         scratch_shapes=[
             pltpu.VMEM((2, 32, 32), jnp.float32),
             pltpu.VMEM((2, 32, 32), jnp.float32),
@@ -425,56 +467,58 @@
     sent = pl.pallas_call(
         pack_measured,
         out_shape=f32(32, 16, 128),
-        in_specs=[SMEM, VMEM, VMEM],
+        in_specs=[VMEM] * 3,
         out_specs=HBM,
         scratch_shapes=[
+            pltpu.VMEM((512, 128), jnp.float32),
             pltpu.VMEM((32, 16, 128), jnp.float32),
             pltpu.SemaphoreType.DMA((4,)),
         ],
         compiler_params=small,
-    )(ids, half, head)
+    )(place, half, head)
     edges = pl.pallas_call(
         pack_edges,
         out_shape=f32(2, 8, 128),
-        in_specs=[SMEM, VMEM, VMEM],
+        in_specs=[VMEM] * 3,
         out_specs=VMEM,
         compiler_params=small,
-    )(ids, mine, other)
+    )(place, mine, other)
     edges = lax.ppermute(edges, rows_axis, across)
     got = lax.all_to_all(sent, "illum", 0, 0, tiled=True)
     here, to_right, to_left = pl.pallas_call(
         pack_rows,
         out_shape=(f32(2, 32, 128), f32(32, 128), f32(32, 128)),
-        in_specs=[SMEM] + [VMEM] * 3,
+        in_specs=[VMEM] * 4,
         out_specs=(VMEM,) * 3,
         compiler_params=small,
-    )(ids, mine, other, edges)
+    )(place, mine, other, edges)
     from_left = lax.ppermute(to_right, "illum", [(i, i + 1) for i in range(n_blocks - 1)])
     from_right = lax.ppermute(to_left, "illum", [(i + 1, i) for i in range(n_blocks - 1)])
 
     mine, other, across_part, along_part = pl.pallas_call(
         march,
         out_shape=(f32(32, 128), f32(32, 128), f32(8, 128), f32(8, 128)),
-        in_specs=[SMEM] + [VMEM] * 4,
+        in_specs=[VMEM] * 5,
         out_specs=(VMEM,) * 4,
         scratch_shapes=[
             pltpu.VMEM((9, 4, 16, 128), jnp.float32),
+            pltpu.VMEM((128, 128), jnp.float32),
             pltpu.VMEM((2, 16, 4, 8, 128), jnp.float32),
             pltpu.VMEM((8, 16, 4, 8, 128), jnp.float32),
             pltpu.VMEM((8, 4, 16, 128), jnp.float32),
         ],
         compiler_params=large,
-    )(ids, here, from_left, from_right, got.reshape(512, 128))
+    )(place, here, from_left, from_right, got.reshape(512, 128))
     other = lax.ppermute(other, rows_axis, partner)
     across_part = lax.ppermute(across_part, rows_axis, across)
     along_part = lax.ppermute(along_part, rows_axis, along)
     return pl.pallas_call(
         combine,
         out_shape=(f32(2, 32, 32), f32(2, 32, 32)),
-        in_specs=[SMEM] + [VMEM] * 4,
+        in_specs=[VMEM] * 5,
         out_specs=(VMEM, VMEM),
         compiler_params=small,
-    )(ids, mine, other, across_part, along_part)
+    )(place, mine, other, across_part, along_part)
 
 
 def solution(mesh):

time: 65.7 us -> 60.5 us (0.921)
  the two profiles are of different devices: /device:TPU:21 before, /device:TPU:19 now
where the time goes in v4:
time: 60.5 us; the launch traced here: 60.1 us
  starting transfers between devices  40.9 us (68%)
  waiting for transfers between devices  12 us (20%)
  Pallas kernels  6.37 us (11%)
  between operations  0.75 us (1%)
    all_to_all x1, starting transfers between devices, body(): got = lax.all_to_all(sent, 'illum', 0, 0, tiled=True)  15.5 us
    ppermute x1, starting transfers between devices, body(): across_part = lax.ppermute(across_part, rows_axis, across)  5.31 us
    ppermute x1, starting transfers between devices, body(): edges = lax.ppermute(edges, rows_axis, across)  5.07 us
    ppermute x1, starting transfers between devices, body(): lax.ppermute(to_right, 'illum', [(i, i + 1) for i in range(n_blocks - 1)])  4.99 us
    ppermute x1, waiting for transfers between devices, body(): lax.ppermute(to_left, 'illum', [(i + 1, i) for i in range(n_blocks - 1)])  4.65 us
    ppermute x1, starting transfers between devices, body(): other = lax.ppermute(other, rows_axis, partner)  3.83 us
    pallas_call x1, Pallas kernels, body(): pl.pallas_call(march, out_shape=(f32(32, 128), f32(32, 128), f32(8, 128),...  3.07 us
    ppermute x1, waiting for transfers between devices, body(): along_part = lax.ppermute(along_part, rows_axis, along)  2.99 us
  transfers between devices with their start and end apart: 8, of which 4 were waited for; matrix products, arithmetic and copies ran while one was open for 0% of the time, Pallas kernels for 0%

profile of v4, /device:TPU:19, one launch (start us, length us, event | category | flops | bytes accessed | tf_op | source)
XLA Modules:
  0.0 60.1 jit_solution(1800644200798741929)
XLA Ops:
  0.6 0.1 pad_add_fusion.ids_ref
  0.7 1.5 %shard_map.59 = (f32[32,128]{1,0:T(8,128)S(1)}, f32[2,16,1024]{2,1,0:T(8,128)S(1)}, f32[8,128]{1,0:T(8,128)S(1)}, s32[3,8,128]{2,1,0:T(8,128)S(1)}) custom-call(s32[3]{0:T(128)S(1)} %pad_add_fusion.ids_ref, f32[2,32,32]{2,1,0:T(8,128)} %phase_ref.1, f32[2,32,32]{2,1,0:T(8,128)} %atten_ref.1, f32[1,2,32,1024]{3,2,1,0:T(8,128)} %measured_ref.1, s32[1,2]{1,0:T(1,128)} %angles_ref.1), custom_call_target="tpu_custom_call" | custom-call | tf_op jit(solution)/shard_map/pallas_call | solution.py:448
  2.2 1.0 %shard_map.62 = f32[32,16,128]{2,1,0:T(8,128)} custom-call(s32[3,8,128]{2,1,0:T(8,128)S(1)} %get-tuple-element.13.place_ref, f32[2,16,1024]{2,1,0:T(8,128)S(1)} %get-tuple-element.18.half, f32[8,128]{1,0:T(8,128)S(1)} %get-tuple-element.19.head_ref), custom_call_target="tpu_custom_call" | custom-call | tf_op jit(solution)/shard_map/pallas_call | solution.py:467
  3.2 15.5 %all-to-all-start = ((f32[32,16,128]{2,1,0:T(8,128)}), f32[32,16,128]{2,1,0:T(8,128)S(1)}, u32[]{:S(2)}, u32[]{:S(2)}) async-start(f32[32,16,128]{2,1,0:T(8,128)} %shard_map.62), calls=%async_computation | async-start | bytes 524288 | tf_op jit(solution)/shard_map/all_to_all | solution.py:487
  18.7 2.3 %collective-permute-start = (f32[32,128]{1,0:T(8,128)S(1)}, f32[32,128]{1,0:T(8,128)S(1)}, u32[]{:S(2)}, u32[]{:S(2)}) collective-permute-start(f32[32,128]{1,0:T(8,128)S(1)} %get-tuple-element.14.mine_ref), channel_id=1, source_target_pairs={{0,1},{2,3},{4,5},{6,7},{8,9},{10,11},{12,13},{14,15},{1,0},{3,2},... | collective-permute-start | bytes 49160 | tf_op jit(solution)/shard_map/ppermute | solution.py:466
  21.1 2.8 %collective-permute-done.other_ref = f32[32,128]{1,0:T(8,128)S(1)} collective-permute-done((f32[32,128]{1,0:T(8,128)S(1)}, f32[32,128]{1,0:T(8,128)S(1)}, u32[]{:S(2)}, u32[]{:S(2)}) %collective-permute-start) | collective-permute-done | bytes 16416 | tf_op jit(solution)/shard_map/ppermute | solution.py:466
  23.8 5.1 %collective-permute-start.1 = (f32[2,8,128]{2,1,0:T(8,128)S(1)}, f32[2,8,128]{2,1,0:T(8,128)S(1)}, u32[]{:S(2)}, u32[]{:S(2)}) collective-permute-start(f32[2,8,128]{2,1,0:T(8,128)S(1)} %shard_map.60), channel_id=1, source_target_pairs={{1,2},{3,4},{5,6},{7,8},{9,10},{11,12},{13,14},{2,1},{4,3},{6,5},{... | collective-permute-start | bytes 24584 | tf_op jit(solution)/shard_map/ppermute | solution.py:486
  28.9 1.6 %collective-permute-done.1.edge_ref = f32[2,8,128]{2,1,0:T(8,128)S(1)} collective-permute-done((f32[2,8,128]{2,1,0:T(8,128)S(1)}, f32[2,8,128]{2,1,0:T(8,128)S(1)}, u32[]{:S(2)}, u32[]{:S(2)}) %collective-permute-start.1) | collective-permute-done | bytes 8224 | tf_op jit(solution)/shard_map/ppermute | solution.py:486
  30.5 0.1 shard_map.61
  30.6 5.0 %collective-permute-start.2 = (f32[32,128]{1,0:T(8,128)S(1)}, f32[32,128]{1,0:T(8,128)S(1)}, u32[]{:S(2)}, u32[]{:S(2)}) collective-permute-start(f32[32,128]{1,0:T(8,128)S(1)} %get-tuple-element.16), channel_id=1, source_target_pairs={{0,16},{16,32},{32,48},{48,64},{64,80},{80,96},{96,112},{112,128},... | collective-permute-start | bytes 49160 | tf_op jit(solution)/shard_map/ppermute | solution.py:495
  35.6 1.9 %collective-permute-start.3 = (f32[32,128]{1,0:T(8,128)S(1)}, f32[32,128]{1,0:T(8,128)S(1)}, u32[]{:S(2)}, u32[]{:S(2)}) collective-permute-start(f32[32,128]{1,0:T(8,128)S(1)} %get-tuple-element.17), channel_id=1, source_target_pairs={{16,0},{32,16},{48,32},{64,48},{80,64},{96,80},{112,96},{128,112},... | collective-permute-start | bytes 49160 | tf_op jit(solution)/shard_map/ppermute | solution.py:496
  37.6 0.0 collective-permute-done.2.left_ref
  37.6 4.7 %collective-permute-done.3.right_ref = f32[32,128]{1,0:T(8,128)S(1)} collective-permute-done((f32[32,128]{1,0:T(8,128)S(1)}, f32[32,128]{1,0:T(8,128)S(1)}, u32[]{:S(2)}, u32[]{:S(2)}) %collective-permute-start.3) | collective-permute-done | bytes 16416 | tf_op jit(solution)/shard_map/ppermute | solution.py:496
  42.2 0.0 all-to-all-done
  42.2 3.1 %shard_map.63 = (f32[32,128]{1,0:T(8,128)S(1)}, f32[32,128]{1,0:T(8,128)S(1)}, f32[8,128]{1,0:T(8,128)S(1)}, f32[8,128]{1,0:T(8,128)S(1)}) custom-call(s32[3,8,128]{2,1,0:T(8,128)S(1)} %get-tuple-element.13.place_ref, f32[2,32,128]{2,1,0:T(8,128)S(1)} %get-tuple-element.15.here_ref, f32[32,128]{1,0:T(8,128)S(1)} %collective-permute-done.2.left_ref, ...), custom_call_target="tpu_custom_call" | custom-call | tf_op jit(solution)/shard_map/pallas_call | solution.py:498
  45.3 3.8 %collective-permute-start.4 = (f32[32,128]{1,0:T(8,128)S(1)}, f32[32,128]{1,0:T(8,128)S(1)}, u32[]{:S(2)}, u32[]{:S(2)}) collective-permute-start(f32[32,128]{1,0:T(8,128)S(1)} %get-tuple-element.21), channel_id=1, source_target_pairs={{0,1},{2,3},{4,5},{6,7},{8,9},{10,11},{12,13},{14,15},{1,0},{3,2},... | collective-permute-start | bytes 49160 | tf_op jit(solution)/shard_map/ppermute | solution.py:512
  49.1 5.3 %collective-permute-start.5 = (f32[8,128]{1,0:T(8,128)S(1)}, f32[8,128]{1,0:T(8,128)S(1)}, u32[]{:S(2)}, u32[]{:S(2)}) collective-permute-start(f32[8,128]{1,0:T(8,128)S(1)} %get-tuple-element.22), channel_id=1, source_target_pairs={{1,2},{3,4},{5,6},{7,8},{9,10},{11,12},{13,14},{2,1},{4,3},{6,5},{... | collective-permute-start | bytes 12296 | tf_op jit(solution)/shard_map/ppermute | solution.py:513
  54.5 1.9 %collective-permute-start.6 = (f32[8,128]{1,0:T(8,128)S(1)}, f32[8,128]{1,0:T(8,128)S(1)}, u32[]{:S(2)}, u32[]{:S(2)}) collective-permute-start(f32[8,128]{1,0:T(8,128)S(1)} %get-tuple-element.23), channel_id=1, source_target_pairs={{1,3},{3,5},{5,7},{7,9},{9,11},{11,13},{13,15},{2,0},{4,2},{6,4},{... | collective-permute-start | bytes 12296 | tf_op jit(solution)/shard_map/ppermute | solution.py:514
  56.4 0.0 collective-permute-done.5.across_ref
  56.4 3.0 %collective-permute-done.6.along_ref = f32[8,128]{1,0:T(8,128)S(1)} collective-permute-done((f32[8,128]{1,0:T(8,128)S(1)}, f32[8,128]{1,0:T(8,128)S(1)}, u32[]{:S(2)}, u32[]{:S(2)}) %collective-permute-start.6) | collective-permute-done | bytes 4128 | tf_op jit(solution)/shard_map/ppermute | solution.py:514
  59.4 0.0 collective-permute-done.4.other_ref
  59.4 0.7 %shard_map.64 = (f32[2,32,32]{2,1,0:T(8,128)}, f32[2,32,32]{2,1,0:T(8,128)}) custom-call(s32[3,8,128]{2,1,0:T(8,128)S(1)} %get-tuple-element.13.place_ref, f32[32,128]{1,0:T(8,128)S(1)} %get-tuple-element.20.mine_ref, f32[32,128]{1,0:T(8,128)S(1)} %collective-permute-done.4.other_ref, f32[8,128]{1,0:T(8,128)S(1)} %collective-permute-done.5.across_ref, ...), custom_call_target="tpu_custom_call" | custom-call | tf_op jit(solution)/shard_map/pallas_call | solution.py:515
  (1 shorter events, 0.0 us)
Async XLA Ops:
  3.2 39.0 %all-to-all-start = ((f32[32,16,128]{2,1,0:T(8,128)}), f32[32,16,128]{2,1,0:T(8,128)S(1)}, u32[]{:S(2)}, u32[]{:S(2)}) async-start(f32[32,16,128]{2,1,0:T(8,128)} %shard_map.62), calls=%async_computation | async-start | bytes 524288 | tf_op jit(solution)/shard_map/all_to_all | solution.py:487
  18.7 5.1 %collective-permute-start = (f32[32,128]{1,0:T(8,128)S(1)}, f32[32,128]{1,0:T(8,128)S(1)}, u32[]{:S(2)}, u32[]{:S(2)}) collective-permute-start(f32[32,128]{1,0:T(8,128)S(1)} %get-tuple-element.14.mine_ref), channel_id=1, source_target_pairs={{0,1},{2,3},{4,5},{6,7},{8,9},{10,11},{12,13},{14,15},{1,0},{3,2},... | collective-permute-start | bytes 49160 | tf_op jit(solution)/shard_map/ppermute | solution.py:466
  23.8 6.7 %collective-permute-start.1 = (f32[2,8,128]{2,1,0:T(8,128)S(1)}, f32[2,8,128]{2,1,0:T(8,128)S(1)}, u32[]{:S(2)}, u32[]{:S(2)}) collective-permute-start(f32[2,8,128]{2,1,0:T(8,128)S(1)} %shard_map.60), channel_id=1, source_target_pairs={{1,2},{3,4},{5,6},{7,8},{9,10},{11,12},{13,14},{2,1},{4,3},{6,5},{... | collective-permute-start | bytes 24584 | tf_op jit(solution)/shard_map/ppermute | solution.py:486
  30.6 6.9 %collective-permute-start.2 = (f32[32,128]{1,0:T(8,128)S(1)}, f32[32,128]{1,0:T(8,128)S(1)}, u32[]{:S(2)}, u32[]{:S(2)}) collective-permute-start(f32[32,128]{1,0:T(8,128)S(1)} %get-tuple-element.16), channel_id=1, source_target_pairs={{0,16},{16,32},{32,48},{48,64},{64,80},{80,96},{96,112},{112,128},... | collective-permute-start | bytes 49160 | tf_op jit(solution)/shard_map/ppermute | solution.py:495
  35.6 6.6 %collective-permute-start.3 = (f32[32,128]{1,0:T(8,128)S(1)}, f32[32,128]{1,0:T(8,128)S(1)}, u32[]{:S(2)}, u32[]{:S(2)}) collective-permute-start(f32[32,128]{1,0:T(8,128)S(1)} %get-tuple-element.17), channel_id=1, source_target_pairs={{16,0},{32,16},{48,32},{64,48},{80,64},{96,80},{112,96},{128,112},... | collective-permute-start | bytes 49160 | tf_op jit(solution)/shard_map/ppermute | solution.py:496
  45.3 14.1 %collective-permute-start.4 = (f32[32,128]{1,0:T(8,128)S(1)}, f32[32,128]{1,0:T(8,128)S(1)}, u32[]{:S(2)}, u32[]{:S(2)}) collective-permute-start(f32[32,128]{1,0:T(8,128)S(1)} %get-tuple-element.21), channel_id=1, source_target_pairs={{0,1},{2,3},{4,5},{6,7},{8,9},{10,11},{12,13},{14,15},{1,0},{3,2},... | collective-permute-start | bytes 49160 | tf_op jit(solution)/shard_map/ppermute | solution.py:512
  49.1 7.2 %collective-permute-start.5 = (f32[8,128]{1,0:T(8,128)S(1)}, f32[8,128]{1,0:T(8,128)S(1)}, u32[]{:S(2)}, u32[]{:S(2)}) collective-permute-start(f32[8,128]{1,0:T(8,128)S(1)} %get-tuple-element.22), channel_id=1, source_target_pairs={{1,2},{3,4},{5,6},{7,8},{9,10},{11,12},{13,14},{2,1},{4,3},{6,5},{... | collective-permute-start | bytes 12296 | tf_op jit(solution)/shard_map/ppermute | solution.py:513
  54.5 4.9 %collective-permute-start.6 = (f32[8,128]{1,0:T(8,128)S(1)}, f32[8,128]{1,0:T(8,128)S(1)}, u32[]{:S(2)}, u32[]{:S(2)}) collective-permute-start(f32[8,128]{1,0:T(8,128)S(1)} %get-tuple-element.23), channel_id=1, source_target_pairs={{1,3},{3,5},{5,7},{7,9},{9,11},{11,13},{13,15},{2,0},{4,2},{6,4},{... | collective-permute-start | bytes 12296 | tf_op jit(solution)/shard_map/ppermute | solution.py:514

commit v5 on v4

--- a/solution.py
+++ b/solution.py
@@ -37,57 +37,79 @@
 
 
 def pack_object(
-    ids_ref, phase_ref, atten_ref, measured_ref, angles_ref,
-    out_ref, half_ref, head_ref, place_ref,
+    phase_ref, atten_ref, measured_ref, angles_ref,
+    out_ref, whole_ref, head_ref,
     phase, atten, turns, sems,
 ):
     copies = [
-        pltpu.make_async_copy(
-            measured_ref.at[0, :, pl.ds(pl.multiple_of(16 * ids_ref[2], 16), 16), :],
-            half_ref,
-            sems.at[0],
-        ),
-        pltpu.make_async_copy(angles_ref, turns, sems.at[1]),
-        pltpu.make_async_copy(phase_ref, phase, sems.at[2]),
-        pltpu.make_async_copy(atten_ref, atten, sems.at[3]),
+        pltpu.make_async_copy(phase_ref, phase, sems.at[0]),
+        pltpu.make_async_copy(atten_ref, atten, sems.at[1]),
+        pltpu.make_async_copy(angles_ref, turns, sems.at[2]),
+        pltpu.make_async_copy(measured_ref.at[0], whole_ref, sems.at[3]),
     ]
     for copy in copies:
         copy.start()
-    for n in range(3):
-        place_ref[n] = jnp.full((8, 128), ids_ref[n], jnp.int32)
-    for copy in copies[1:]:
+    for copy in copies[:3]:
         copy.wait()
     for n, (ref, layer) in enumerate(((phase, 0), (phase, 1), (atten, 0), (atten, 1))):
         out_ref[:, 32 * n : 32 * n + 32] = ref[layer]
     lane = lanes_of((8, 128))
     head_ref[...] = jnp.where(lane == 0, turns[0, 0], turns[0, 1]).astype(jnp.float32)
-    copies[0].wait()
-
-
-def pack_edges(place_ref, mine_ref, other_ref, out_ref):
-    first = place_ref[2] == 0
-    for pair, (a, b) in enumerate(((mine_ref, other_ref), (other_ref, mine_ref))):
-        out_ref[pair] = jnp.where(
-            first, jnp.where(first, a[0:8], b[0:8]), jnp.where(first, a[24:32], b[24:32])
-        )
-
-
-def pack_rows(place_ref, mine_ref, other_ref, edge_ref, out_ref, right_ref, left_ref):
+    copies[3].wait()
+
+
+def pairs_of(first, mine_ref, other_ref, rows):
+    mine, other = mine_ref[rows], other_ref[rows]
+    return [jnp.where(first, mine, other), jnp.where(first, other, mine)]
+
+
+def sides_of(first, near_ref, far_ref, rows):
+    near, far = near_ref[rows], far_ref[rows]
+    return [jnp.where(first, near, far), jnp.where(first, far, near)]
+
+
+def pack_sides(place_ref, mine_ref, other_ref, out_ref):
     first = place_ref[2] == 0
     lane = lanes_of((8, 128))
     spots = 32 * jnp.bitwise_and(lane // 16, 3) + jnp.bitwise_and(lane, 15)
     for block in range(4):
         rows = slice(8 * block, 8 * block + 8)
-        both = []
-        for pair in range(2):
-            refs = (mine_ref, other_ref) if pair == 0 else (other_ref, mine_ref)
-            above = refs[0][8 * block - 8 : 8 * block] if block else edge_ref[pair]
-            below = refs[1][8 * block + 8 : 8 * block + 16] if block < 3 else edge_ref[pair]
-            both.append(jnp.where(first, above, below))
-            out_ref[pair, rows] = both[pair]
-        for ref, shift in ((right_ref, 16), (left_ref, 0)):
-            parts = [picked(x, spots + shift) for x in both]
-            ref[rows] = jnp.where(lane < 64, parts[0], parts[1])
+        both = pairs_of(first, mine_ref, other_ref, rows)
+        left, right = (
+            jnp.where(lane < 64, *(picked(x, spots + shift) for x in both)) for shift in (0, 16)
+        )
+        out_ref[rows] = jnp.where(first, left, right)
+
+
+def pack_edges(place_ref, mine_ref, other_ref, near_ref, far_ref, out_ref):
+    first = place_ref[2] == 0
+    for n, (of, refs) in enumerate(
+        ((pairs_of, (mine_ref, other_ref)), (sides_of, (near_ref, far_ref)))
+    ):
+        top, bottom = (of(first, *refs, rows) for rows in (slice(0, 8), slice(24, 32)))
+        for k in range(2):
+            out_ref[2 * n + k] = jnp.where(first, top[k], bottom[k])
+
+
+def pack_rows(
+    place_ref, mine_ref, other_ref, near_ref, far_ref, edge_ref, out_ref, left_ref, right_ref
+):
+    first = place_ref[2] == 0
+    blocks = []
+    for block in range(4):
+        rows = slice(8 * block, 8 * block + 8)
+        blocks.append(
+            pairs_of(first, mine_ref, other_ref, rows)
+            + sides_of(first, near_ref, far_ref, rows)
+        )
+    for block in range(4):
+        rows = slice(8 * block, 8 * block + 8)
+        new = []
+        for k in range(4):
+            above = blocks[block - 1][k] if block else edge_ref[k]
+            below = blocks[block + 1][k] if block < 3 else edge_ref[k]
+            new.append(jnp.where(first, above, below))
+        out_ref[0, rows], out_ref[1, rows], left_ref[rows], right_ref[rows] = new
 
 
 def flipped(x):
@@ -122,18 +144,28 @@
     return lax.broadcasted_iota(jnp.int32, shape, 0), lanes_of(shape)
 
 
-def pack_measured(place_ref, half, head_ref, out_ref, plain, packed, sems):
+def pack_measured(place_ref, whole_ref, head_ref, out_ref, plain, packed, sems):
     lane = lanes_of((8, 128))
     head = head_ref[...]
     zero = jnp.zeros((8, 128), jnp.float32)
     source, target = square_iotas()
     m = jnp.bitwise_and(target // 16 - jnp.tile(place_ref[0] // 8, (16, 1)), 3)
     chosen = source == jnp.bitwise_and(target, 64) + 4 * jnp.bitwise_and(target, 15) + m
+    cut = place_ref[2]
     regs = []
     for comp in range(2):
-        first = [half[comp, 0:8, 128 * n : 128 * n + 128] for n in range(8)]
-        second = [flipped(half[comp, 8:16, 128 * n : 128 * n + 128]) for n in range(8)]
-        regs.append((first, second))
+        rows = []
+        for a in range(2):
+            rows.append([])
+            for n in range(8):
+                at = slice(128 * n, 128 * n + 128)
+                x = jnp.where(
+                    cut == 0,
+                    whole_ref[comp, 8 * a : 8 * a + 8, at],
+                    whole_ref[comp, 8 * a + 16 : 8 * a + 24, at],
+                )
+                rows[a].append(flipped(x) if a else x)
+        regs.append(rows)
     copies = []
     for j in range(32):
         v, r = divmod(32 * j - REACH, 128)
@@ -164,7 +196,7 @@
 
 def march(
     place_ref, here_ref, left_ref, right_ref, got_ref,
-    mine_ref, other_ref, across_ref, along_ref,
+    mine_ref, other_ref, edge_ref,
     table, flat, field, stored, sums,
 ):
     block, slab, cut = place_ref[0], place_ref[1], place_ref[2]
@@ -407,19 +439,29 @@
             ref[8 * b : 8 * b + 8] = jnp.where(
                 first, parts[b + 1] if b < 3 else none, parts[b - 1] if b > 0 else none
             )
-    across_ref[...] = jnp.where(first, other[0], other[3])
-    along_ref[...] = jnp.where(first, mine[0], mine[3])
-
-
-def combine(place_ref, mine_ref, other_ref, across_ref, along_ref, phase_ref, atten_ref):
+    for pair in range(2):
+        edge_ref[pair] = jnp.where(first, blocks[pair][0], blocks[pair][3])
+
+
+def add_edges(place_ref, other_ref, edge_ref, out_ref):
     first = place_ref[2] == 0
+    edge = jnp.where(first, edge_ref[1], edge_ref[0])
+    none = jnp.zeros((8, 128), jnp.float32)
+    out_ref[0:8] = other_ref[0:8] + jnp.where(first, edge, none)
+    out_ref[8:24] = other_ref[8:24]
+    out_ref[24:32] = other_ref[24:32] + jnp.where(first, none, edge)
+
+
+def combine(place_ref, mine_ref, other_ref, edge_ref, phase_ref, atten_ref):
+    first = place_ref[2] == 0
+    edge = jnp.where(first, edge_ref[0], edge_ref[1])
     for b in range(4):
         rows = slice(8 * b, 8 * b + 8)
         total = mine_ref[rows] + other_ref[rows]
         if b == 0:
-            total = total + jnp.where(first, across_ref[...], along_ref[...])
+            total = total + jnp.where(first, edge, 0.0)
         if b == 3:
-            total = total + jnp.where(first, along_ref[...], across_ref[...])
+            total = total + jnp.where(first, 0.0, edge)
         for sl in range(2):
             phase_ref[sl, rows] = turn(total, -32 * sl)[:, 0:32]
             atten_ref[sl, rows] = turn(total, -64 - 32 * sl)[:, 0:32]
@@ -429,7 +471,7 @@
     block = lax.axis_index("illum")
     slab = lax.axis_index("slab")
     cut = lax.axis_index("cuts")
-    ids = jnp.stack([block, slab, cut]).astype(jnp.int32)
+    place = jnp.stack([jnp.full((8, 128), n, jnp.int32) for n in (block, slab, cut)])
     n_slabs, n_blocks = lax.axis_size("slab"), lax.axis_size("illum")
     rows_axis = ("slab", "cuts")
 
@@ -438,23 +480,16 @@
 
     partner = both_ways([(2 * s, 2 * s + 1) for s in range(n_slabs)])
     across = both_ways([(2 * s + 1, 2 * s + 2) for s in range(n_slabs - 1)])
-    along = [(2 * s + 1, 2 * s + 3) for s in range(n_slabs - 1)]
-    along += [(2 * s + 2, 2 * s) for s in range(n_slabs - 1)]
-
+    beside = both_ways([(2 * i + 1, 2 * i + 2) for i in range(n_blocks - 1)])
     phase_delay, attenuation, measured, angles = (
         pltpu.with_memory_space_constraint(x, pltpu.HBM)
         for x in (phase_delay, attenuation, measured, angles)
     )
-    mine, half, head, place = pl.pallas_call(
+    mine, whole, head = pl.pallas_call(
         pack_object,
-        out_shape=(
-            f32(32, 128),
-            f32(2, 16, 1024),
-            f32(8, 128),
-            jax.ShapeDtypeStruct((3, 8, 128), jnp.int32),
-        ),
-        in_specs=[SMEM] + [HBM] * 4,
-        out_specs=(VMEM,) * 4,
+        out_shape=(f32(32, 128), f32(2, 32, 1024), f32(8, 128)),
+        in_specs=[HBM] * 4,
+        out_specs=(VMEM,) * 3,
         scratch_shapes=[
             pltpu.VMEM((2, 32, 32), jnp.float32),
             pltpu.VMEM((2, 32, 32), jnp.float32),
@@ -462,7 +497,7 @@
             pltpu.SemaphoreType.DMA((4,)),
         ],
         compiler_params=small,
-    )(ids, phase_delay, attenuation, measured, angles)
+    )(phase_delay, attenuation, measured, angles)
     other = lax.ppermute(mine, rows_axis, partner)
     sent = pl.pallas_call(
         pack_measured,
@@ -475,31 +510,38 @@
             pltpu.SemaphoreType.DMA((4,)),
         ],
         compiler_params=small,
-    )(place, half, head)
+    )(place, whole, head)
+    near = pl.pallas_call(
+        pack_sides,
+        out_shape=f32(32, 128),
+        in_specs=[VMEM] * 3,
+        out_specs=VMEM,
+        compiler_params=small,
+    )(place, mine, other)
+    near = lax.ppermute(near, ("illum", "cuts"), beside)
+    got = lax.all_to_all(sent, "illum", 0, 0, tiled=True)
+    far = lax.ppermute(near, rows_axis, partner)
     edges = pl.pallas_call(
         pack_edges,
-        out_shape=f32(2, 8, 128),
-        in_specs=[VMEM] * 3,
+        out_shape=f32(4, 8, 128),
+        in_specs=[VMEM] * 5,
         out_specs=VMEM,
         compiler_params=small,
-    )(place, mine, other)
+    )(place, mine, other, near, far)
     edges = lax.ppermute(edges, rows_axis, across)
-    got = lax.all_to_all(sent, "illum", 0, 0, tiled=True)
-    here, to_right, to_left = pl.pallas_call(
+    here, from_left, from_right = pl.pallas_call(
         pack_rows,
         out_shape=(f32(2, 32, 128), f32(32, 128), f32(32, 128)),
-        in_specs=[VMEM] * 4,
+        in_specs=[VMEM] * 6,
         out_specs=(VMEM,) * 3,
         compiler_params=small,
-    )(place, mine, other, edges)
-    from_left = lax.ppermute(to_right, "illum", [(i, i + 1) for i in range(n_blocks - 1)])
-    from_right = lax.ppermute(to_left, "illum", [(i + 1, i) for i in range(n_blocks - 1)])
-
-    mine, other, across_part, along_part = pl.pallas_call(
+    )(place, mine, other, near, far, edges)
+
+    mine, other, edges = pl.pallas_call(
         march,
-        out_shape=(f32(32, 128), f32(32, 128), f32(8, 128), f32(8, 128)),
+        out_shape=(f32(32, 128), f32(32, 128), f32(2, 8, 128)),
         in_specs=[VMEM] * 5,
-        out_specs=(VMEM,) * 4,
+        out_specs=(VMEM,) * 3,
         scratch_shapes=[
             pltpu.VMEM((9, 4, 16, 128), jnp.float32),
             pltpu.VMEM((128, 128), jnp.float32),
@@ -509,16 +551,22 @@
         ],
         compiler_params=large,
     )(place, here, from_left, from_right, got.reshape(512, 128))
+    edges = lax.ppermute(edges, rows_axis, across)
+    other = pl.pallas_call(
+        add_edges,
+        out_shape=f32(32, 128),
+        in_specs=[VMEM] * 3,
+        out_specs=VMEM,
+        compiler_params=small,
+    )(place, other, edges)
     other = lax.ppermute(other, rows_axis, partner)
-    across_part = lax.ppermute(across_part, rows_axis, across)
-    along_part = lax.ppermute(along_part, rows_axis, along)
     return pl.pallas_call(
         combine,
         out_shape=(f32(2, 32, 32), f32(2, 32, 32)),
-        in_specs=[VMEM] * 5,
+        in_specs=[VMEM] * 4,
         out_specs=(VMEM, VMEM),
         compiler_params=small,
-    )(place, mine, other, across_part, along_part)
+    )(place, mine, other, edges)
 
 
 def solution(mesh):

time: 60.5 us -> 59.6 us (0.985)
  the two profiles are of different devices: /device:TPU:19 before, /device:TPU:34 now
where the time goes in v5:
time: 59.6 us; the launch traced here: 59.3 us
  starting transfers between devices  28 us (47%)
  waiting for transfers between devices  24.5 us (41%)
  Pallas kernels  5.93 us (10%)
  between operations  0.73 us (1%)
    all_to_all x1, starting transfers between devices, body(): got = lax.all_to_all(sent, 'illum', 0, 0, tiled=True)  15.8 us
    ppermute x2, waiting for transfers between devices, body(): edges = lax.ppermute(edges, rows_axis, across)  7.97 us
    ppermute x1, waiting for transfers between devices, body(): near = lax.ppermute(near, ('illum', 'cuts'), beside)  4.91 us
    ppermute x1, waiting for transfers between devices, body(): other = lax.ppermute(mine, rows_axis, partner)  4.16 us
    ppermute x2, starting transfers between devices, body(): edges = lax.ppermute(edges, rows_axis, across)  3.83 us
    ppermute x1, waiting for transfers between devices, body(): other = lax.ppermute(other, rows_axis, partner)  3.7 us
    ppermute x1, waiting for transfers between devices, body(): far = lax.ppermute(near, rows_axis, partner)  3.7 us
    pallas_call x1, Pallas kernels, body(): pl.pallas_call(march, out_shape=(f32(32, 128), f32(32, 128), f32(2, 8, 12...  3.07 us
  transfers between devices with their start and end apart: 7, of which 6 were waited for; matrix products, arithmetic and copies ran while one was open for 0% of the time, Pallas kernels for 0%

profile of v5, /device:TPU:34, one launch (start us, length us, event | category | flops | bytes accessed | tf_op | source)
XLA Modules:
  0.0 59.3 jit_solution(17062411670397744586)
XLA Ops:
  0.6 0.1 add_add_fusion
  0.7 1.0 %shard_map.59 = (f32[32,128]{1,0:T(8,128)S(1)}, f32[2,32,1024]{2,1,0:T(8,128)S(1)}, f32[8,128]{1,0:T(8,128)S(1)}) custom-call(f32[2,32,32]{2,1,0:T(8,128)} %phase_ref.1, f32[2,32,32]{2,1,0:T(8,128)} %atten_ref.1, f32[1,2,32,1024]{3,2,1,0:T(8,128)} %measured_ref.1, s32[1,2]{1,0:T(1,128)} %angles_ref.1), custom_call_target="tpu_custom_call" | custom-call | tf_op jit(solution)/shard_map/pallas_call | solution.py:488
  1.7 0.1 broadcast.4.place_ref
  1.8 1.0 %shard_map.63 = f32[32,16,128]{2,1,0:T(8,128)} custom-call(s32[3,8,128]{2,1,0:T(8,128)S(1)} %broadcast.4.place_ref, f32[2,32,1024]{2,1,0:T(8,128)S(1)} %get-tuple-element.15.whole_ref, f32[8,128]{1,0:T(8,128)S(1)} %get-tuple-element.16.head_ref), custom_call_target="tpu_custom_call" | custom-call | tf_op jit(solution)/shard_map/pallas_call | solution.py:502
  2.8 15.8 %all-to-all-start = ((f32[32,16,128]{2,1,0:T(8,128)}), f32[32,16,128]{2,1,0:T(8,128)S(1)}, u32[]{:S(2)}, u32[]{:S(2)}) async-start(f32[32,16,128]{2,1,0:T(8,128)} %shard_map.63), calls=%async_computation | async-start | bytes 524288 | tf_op jit(solution)/shard_map/all_to_all | solution.py:522
  18.7 2.6 %collective-permute-start = (f32[32,128]{1,0:T(8,128)S(1)}, f32[32,128]{1,0:T(8,128)S(1)}, u32[]{:S(2)}, u32[]{:S(2)}) collective-permute-start(f32[32,128]{1,0:T(8,128)S(1)} %get-tuple-element.11.mine_ref), channel_id=1, source_target_pairs={{0,1},{2,3},{4,5},{6,7},{8,9},{10,11},{12,13},{14,15},{1,0},{3,2},... | collective-permute-start | bytes 49160 | tf_op jit(solution)/shard_map/ppermute | solution.py:501
  21.3 4.2 %collective-permute-done.other_ref = f32[32,128]{1,0:T(8,128)S(1)} collective-permute-done((f32[32,128]{1,0:T(8,128)S(1)}, f32[32,128]{1,0:T(8,128)S(1)}, u32[]{:S(2)}, u32[]{:S(2)}) %collective-permute-start) | collective-permute-done | bytes 16416 | tf_op jit(solution)/shard_map/ppermute | solution.py:501
  25.4 0.1 shard_map.60
  25.6 1.9 %collective-permute-start.1 = (f32[32,128]{1,0:T(8,128)S(1)}, f32[32,128]{1,0:T(8,128)S(1)}, u32[]{:S(2)}, u32[]{:S(2)}) collective-permute-start(f32[32,128]{1,0:T(8,128)S(1)} %shard_map.60), channel_id=1, source_target_pairs={{1,16},{17,32},{33,48},{49,64},{65,80},{81,96},{97,112},{113,128},... | collective-permute-start | bytes 49160 | tf_op jit(solution)/shard_map/ppermute | solution.py:521
  27.5 4.9 %collective-permute-done.1.near_ref = f32[32,128]{1,0:T(8,128)S(1)} collective-permute-done((f32[32,128]{1,0:T(8,128)S(1)}, f32[32,128]{1,0:T(8,128)S(1)}, u32[]{:S(2)}, u32[]{:S(2)}) %collective-permute-start.1) | collective-permute-done | bytes 16416 | tf_op jit(solution)/shard_map/ppermute | solution.py:521
  32.4 1.9 %collective-permute-start.2 = (f32[32,128]{1,0:T(8,128)S(1)}, f32[32,128]{1,0:T(8,128)S(1)}, u32[]{:S(2)}, u32[]{:S(2)}) collective-permute-start(f32[32,128]{1,0:T(8,128)S(1)} %collective-permute-done.1.near_ref), channel_id=1, source_target_pairs={{0,1},{2,3},{4,5},{6,7},{8,9},{10,11},{12,13},{14,15},{1,0},{3,2},... | collective-permute-start | bytes 49160 | tf_op jit(solution)/shard_map/ppermute | solution.py:523
  34.3 3.7 %collective-permute-done.2.far_ref = f32[32,128]{1,0:T(8,128)S(1)} collective-permute-done((f32[32,128]{1,0:T(8,128)S(1)}, f32[32,128]{1,0:T(8,128)S(1)}, u32[]{:S(2)}, u32[]{:S(2)}) %collective-permute-start.2) | collective-permute-done | bytes 16416 | tf_op jit(solution)/shard_map/ppermute | solution.py:523
  38.0 1.9 %collective-permute-start.3 = (f32[4,8,128]{2,1,0:T(8,128)S(1)}, f32[4,8,128]{2,1,0:T(8,128)S(1)}, u32[]{:S(2)}, u32[]{:S(2)}) collective-permute-start(f32[4,8,128]{2,1,0:T(8,128)S(1)} %shard_map.61), channel_id=1, source_target_pairs={{1,2},{3,4},{5,6},{7,8},{9,10},{11,12},{13,14},{2,1},{4,3},{6,5},{... | collective-permute-start | bytes 49160 | tf_op jit(solution)/shard_map/ppermute | solution.py:531
  39.9 4.0 %collective-permute-done.3.edge_ref = f32[4,8,128]{2,1,0:T(8,128)S(1)} collective-permute-done((f32[4,8,128]{2,1,0:T(8,128)S(1)}, f32[4,8,128]{2,1,0:T(8,128)S(1)}, u32[]{:S(2)}, u32[]{:S(2)}) %collective-permute-start.3) | collective-permute-done | bytes 16416 | tf_op jit(solution)/shard_map/ppermute | solution.py:531
  44.0 0.0 all-to-all-done
  44.0 3.1 %shard_map.64 = (f32[32,128]{1,0:T(8,128)S(1)}, f32[32,128]{1,0:T(8,128)S(1)}, f32[2,8,128]{2,1,0:T(8,128)S(1)}) custom-call(s32[3,8,128]{2,1,0:T(8,128)S(1)} %broadcast.4.place_ref, f32[2,32,128]{2,1,0:T(8,128)S(1)} %get-tuple-element.12.here_ref, f32[32,128]{1,0:T(8,128)S(1)} %get-tuple-element.13.left_ref, f32[32,128]{1,0:T(8,128)S(1)} %get-tuple-element.14.right_ref, ...), custom_call_target="tpu_custom_call" | custom-call | tf_op jit(solution)/shard_map/pallas_call | solution.py:540
  47.1 1.9 %collective-permute-start.4 = (f32[2,8,128]{2,1,0:T(8,128)S(1)}, f32[2,8,128]{2,1,0:T(8,128)S(1)}, u32[]{:S(2)}, u32[]{:S(2)}) collective-permute-start(f32[2,8,128]{2,1,0:T(8,128)S(1)} %get-tuple-element.19), channel_id=1, source_target_pairs={{1,2},{3,4},{5,6},{7,8},{9,10},{11,12},{13,14},{2,1},{4,3},{6,5},{... | collective-permute-start | bytes 24584 | tf_op jit(solution)/shard_map/ppermute | solution.py:554
  49.0 3.9 %collective-permute-done.4.edge_ref = f32[2,8,128]{2,1,0:T(8,128)S(1)} collective-permute-done((f32[2,8,128]{2,1,0:T(8,128)S(1)}, f32[2,8,128]{2,1,0:T(8,128)S(1)}, u32[]{:S(2)}, u32[]{:S(2)}) %collective-permute-start.4) | collective-permute-done | bytes 8224 | tf_op jit(solution)/shard_map/ppermute | solution.py:554
  52.9 1.9 %collective-permute-start.5 = (f32[32,128]{1,0:T(8,128)S(1)}, f32[32,128]{1,0:T(8,128)S(1)}, u32[]{:S(2)}, u32[]{:S(2)}) collective-permute-start(f32[32,128]{1,0:T(8,128)S(1)} %shard_map.65), channel_id=1, source_target_pairs={{0,1},{2,3},{4,5},{6,7},{8,9},{10,11},{12,13},{14,15},{1,0},{3,2},... | collective-permute-start | bytes 49160 | tf_op jit(solution)/shard_map/ppermute | solution.py:562
  54.8 3.7 %collective-permute-done.5.other_ref = f32[32,128]{1,0:T(8,128)S(1)} collective-permute-done((f32[32,128]{1,0:T(8,128)S(1)}, f32[32,128]{1,0:T(8,128)S(1)}, u32[]{:S(2)}, u32[]{:S(2)}) %collective-permute-start.5) | collective-permute-done | bytes 16416 | tf_op jit(solution)/shard_map/ppermute | solution.py:562
  58.6 0.7 %shard_map.66 = (f32[2,32,32]{2,1,0:T(8,128)}, f32[2,32,32]{2,1,0:T(8,128)}) custom-call(s32[3,8,128]{2,1,0:T(8,128)S(1)} %broadcast.4.place_ref, f32[32,128]{1,0:T(8,128)S(1)} %get-tuple-element.17.mine_ref, f32[32,128]{1,0:T(8,128)S(1)} %collective-permute-done.5.other_ref, f32[2,8,128]{2,1,0:T(8,128)S(1)} %collective-permute-done.4.edge_ref), custom_call_target="tpu_custom_call" | custom-call | tf_op jit(solution)/shard_map/pallas_call | solution.py:563
  (3 shorter events, 0.0 us)
Async XLA Ops:
  2.8 41.1 %all-to-all-start = ((f32[32,16,128]{2,1,0:T(8,128)}), f32[32,16,128]{2,1,0:T(8,128)S(1)}, u32[]{:S(2)}, u32[]{:S(2)}) async-start(f32[32,16,128]{2,1,0:T(8,128)} %shard_map.63), calls=%async_computation | async-start | bytes 524288 | tf_op jit(solution)/shard_map/all_to_all | solution.py:522
  18.7 6.8 %collective-permute-start = (f32[32,128]{1,0:T(8,128)S(1)}, f32[32,128]{1,0:T(8,128)S(1)}, u32[]{:S(2)}, u32[]{:S(2)}) collective-permute-start(f32[32,128]{1,0:T(8,128)S(1)} %get-tuple-element.11.mine_ref), channel_id=1, source_target_pairs={{0,1},{2,3},{4,5},{6,7},{8,9},{10,11},{12,13},{14,15},{1,0},{3,2},... | collective-permute-start | bytes 49160 | tf_op jit(solution)/shard_map/ppermute | solution.py:501
  25.6 6.8 %collective-permute-start.1 = (f32[32,128]{1,0:T(8,128)S(1)}, f32[32,128]{1,0:T(8,128)S(1)}, u32[]{:S(2)}, u32[]{:S(2)}) collective-permute-start(f32[32,128]{1,0:T(8,128)S(1)} %shard_map.60), channel_id=1, source_target_pairs={{1,16},{17,32},{33,48},{49,64},{65,80},{81,96},{97,112},{113,128},... | collective-permute-start | bytes 49160 | tf_op jit(solution)/shard_map/ppermute | solution.py:521
  32.4 5.6 %collective-permute-start.2 = (f32[32,128]{1,0:T(8,128)S(1)}, f32[32,128]{1,0:T(8,128)S(1)}, u32[]{:S(2)}, u32[]{:S(2)}) collective-permute-start(f32[32,128]{1,0:T(8,128)S(1)} %collective-permute-done.1.near_ref), channel_id=1, source_target_pairs={{0,1},{2,3},{4,5},{6,7},{8,9},{10,11},{12,13},{14,15},{1,0},{3,2},... | collective-permute-start | bytes 49160 | tf_op jit(solution)/shard_map/ppermute | solution.py:523
  38.0 5.9 %collective-permute-start.3 = (f32[4,8,128]{2,1,0:T(8,128)S(1)}, f32[4,8,128]{2,1,0:T(8,128)S(1)}, u32[]{:S(2)}, u32[]{:S(2)}) collective-permute-start(f32[4,8,128]{2,1,0:T(8,128)S(1)} %shard_map.61), channel_id=1, source_target_pairs={{1,2},{3,4},{5,6},{7,8},{9,10},{11,12},{13,14},{2,1},{4,3},{6,5},{... | collective-permute-start | bytes 49160 | tf_op jit(solution)/shard_map/ppermute | solution.py:531
  47.1 5.9 %collective-permute-start.4 = (f32[2,8,128]{2,1,0:T(8,128)S(1)}, f32[2,8,128]{2,1,0:T(8,128)S(1)}, u32[]{:S(2)}, u32[]{:S(2)}) collective-permute-start(f32[2,8,128]{2,1,0:T(8,128)S(1)} %get-tuple-element.19), channel_id=1, source_target_pairs={{1,2},{3,4},{5,6},{7,8},{9,10},{11,12},{13,14},{2,1},{4,3},{6,5},{... | collective-permute-start | bytes 24584 | tf_op jit(solution)/shard_map/ppermute | solution.py:554
  52.9 5.6 %collective-permute-start.5 = (f32[32,128]{1,0:T(8,128)S(1)}, f32[32,128]{1,0:T(8,128)S(1)}, u32[]{:S(2)}, u32[]{:S(2)}) collective-permute-start(f32[32,128]{1,0:T(8,128)S(1)} %shard_map.65), channel_id=1, source_target_pairs={{0,1},{2,3},{4,5},{6,7},{8,9},{10,11},{12,13},{14,15},{1,0},{3,2},... | collective-permute-start | bytes 49160 | tf_op jit(solution)/shard_map/ppermute | solution.py:562

commit v6 on v5

--- a/solution.py
+++ b/solution.py
@@ -194,20 +194,13 @@
         copy.wait()
 
 
-def march(
-    place_ref, here_ref, left_ref, right_ref, got_ref,
-    mine_ref, other_ref, edge_ref,
-    table, flat, field, stored, sums,
-):
+def transmit(place_ref, here_ref, left_ref, right_ref, table, flat):
+    sub = lax.broadcasted_iota(jnp.int32, (8, 128), 0)
     block, slab, cut = place_ref[0], place_ref[1], place_ref[2]
-    first = cut == 0
     lane = lanes_of((8, 128))
-    sub = lax.broadcasted_iota(jnp.int32, (8, 128), 0)
     upper = lane < 64
     window = jnp.bitwise_and(lane, 63)
-    half = jnp.bitwise_and(lane, 64)
     place = jnp.bitwise_and(lane, 15)
-    group = jnp.bitwise_and(lane // 16, 3)
     top = 32 * slab + 16 * cut - HALO
     left_column = 32 * block - REACH
 
@@ -254,6 +247,26 @@
     for m in range(4):
         table[0:8, m] = wide[:, 128 * m : 128 * m + 128].reshape(8, 16, 128)
 
+
+def march(
+    place_ref, table, got_ref,
+    mine_ref, other_ref, edge_ref,
+    flat, field, stored, sums,
+):
+    block, slab, cut = place_ref[0], place_ref[1], place_ref[2]
+    first = cut == 0
+    lane = lanes_of((8, 128))
+    upper = lane < 64
+    window = jnp.bitwise_and(lane, 63)
+    half = jnp.bitwise_and(lane, 64)
+    place = jnp.bitwise_and(lane, 15)
+    group = jnp.bitwise_and(lane // 16, 3)
+    top = 32 * slab + 16 * cut - HALO
+    left_column = 32 * block - REACH
+
+    def columns(m):
+        return left_column + 4 * place + m
+
     def spread(n, m, r):
         return jnp.broadcast_to(table[n, m, r : r + 1], (8, 128))
 
@@ -537,20 +550,27 @@
         compiler_params=small,
     )(place, mine, other, near, far, edges)
 
+    table = pl.pallas_call(
+        transmit,
+        out_shape=f32(9, 4, 16, 128),
+        in_specs=[VMEM] * 4,
+        out_specs=VMEM,
+        scratch_shapes=[pltpu.VMEM((128, 128), jnp.float32)],
+        compiler_params=small,
+    )(place, here, from_left, from_right)
     mine, other, edges = pl.pallas_call(
         march,
         out_shape=(f32(32, 128), f32(32, 128), f32(2, 8, 128)),
-        in_specs=[VMEM] * 5,
+        in_specs=[VMEM] * 3,
         out_specs=(VMEM,) * 3,
         scratch_shapes=[
-            pltpu.VMEM((9, 4, 16, 128), jnp.float32),
             pltpu.VMEM((128, 128), jnp.float32),
             pltpu.VMEM((2, 16, 4, 8, 128), jnp.float32),
             pltpu.VMEM((8, 16, 4, 8, 128), jnp.float32),
             pltpu.VMEM((8, 4, 16, 128), jnp.float32),
         ],
         compiler_params=large,
-    )(place, here, from_left, from_right, got.reshape(512, 128))
+    )(place, table, got.reshape(512, 128))
     edges = lax.ppermute(edges, rows_axis, across)
     other = pl.pallas_call(
         add_edges,

time: 59.6 us -> 59.9 us (level)
  the two profiles are of different devices: /device:TPU:34 before, /device:TPU:38 now
where the time goes in v6:
time: 59.9 us; the launch traced here: 59.5 us
  starting transfers between devices  28 us (47%)
  waiting for transfers between devices  24.5 us (41%)
  Pallas kernels  6.15 us (10%)
  between operations  0.74 us (1%)
    all_to_all x1, starting transfers between devices, body(): got = lax.all_to_all(sent, 'illum', 0, 0, tiled=True)  15.9 us
    ppermute x2, waiting for transfers between devices, body(): edges = lax.ppermute(edges, rows_axis, across)  7.97 us
    ppermute x1, waiting for transfers between devices, body(): near = lax.ppermute(near, ('illum', 'cuts'), beside)  4.91 us
    ppermute x1, waiting for transfers between devices, body(): other = lax.ppermute(mine, rows_axis, partner)  4.16 us
    ppermute x2, starting transfers between devices, body(): edges = lax.ppermute(edges, rows_axis, across)  3.83 us
    ppermute x1, waiting for transfers between devices, body(): other = lax.ppermute(other, rows_axis, partner)  3.7 us
    ppermute x1, waiting for transfers between devices, body(): far = lax.ppermute(near, rows_axis, partner)  3.7 us
    pallas_call x1, Pallas kernels, body(): pl.pallas_call(march, out_shape=(f32(32, 128), f32(32, 128), f32(2, 8, 12...  2.86 us
  transfers between devices with their start and end apart: 7, of which 6 were waited for; matrix products, arithmetic and copies ran while one was open for 0% of the time, Pallas kernels for 1%

profile of v6, /device:TPU:38, one launch (start us, length us, event | category | flops | bytes accessed | tf_op | source)
XLA Modules:
  0.0 59.5 jit_solution(4974027584665429582)
XLA Ops:
  0.6 0.1 add_add_fusion
  0.7 1.0 %shard_map.59 = (f32[32,128]{1,0:T(8,128)S(1)}, f32[2,32,1024]{2,1,0:T(8,128)S(1)}, f32[8,128]{1,0:T(8,128)S(1)}) custom-call(f32[2,32,32]{2,1,0:T(8,128)} %phase_ref.1, f32[2,32,32]{2,1,0:T(8,128)} %atten_ref.1, f32[1,2,32,1024]{3,2,1,0:T(8,128)} %measured_ref.1, s32[1,2]{1,0:T(1,128)} %angles_ref.1), custom_call_target="tpu_custom_call" | custom-call | tf_op jit(solution)/shard_map/pallas_call | solution.py:501
  1.7 0.1 broadcast.4.place_ref
  1.8 1.0 %shard_map.64 = f32[32,16,128]{2,1,0:T(8,128)} custom-call(s32[3,8,128]{2,1,0:T(8,128)S(1)} %broadcast.4.place_ref, f32[2,32,1024]{2,1,0:T(8,128)S(1)} %get-tuple-element.15.whole_ref, f32[8,128]{1,0:T(8,128)S(1)} %get-tuple-element.16.head_ref), custom_call_target="tpu_custom_call" | custom-call | tf_op jit(solution)/shard_map/pallas_call | solution.py:515
  2.8 15.9 %all-to-all-start = ((f32[32,16,128]{2,1,0:T(8,128)}), f32[32,16,128]{2,1,0:T(8,128)S(1)}, u32[]{:S(2)}, u32[]{:S(2)}) async-start(f32[32,16,128]{2,1,0:T(8,128)} %shard_map.64), calls=%async_computation | async-start | bytes 524288 | tf_op jit(solution)/shard_map/all_to_all | solution.py:535
  18.7 2.6 %collective-permute-start = (f32[32,128]{1,0:T(8,128)S(1)}, f32[32,128]{1,0:T(8,128)S(1)}, u32[]{:S(2)}, u32[]{:S(2)}) collective-permute-start(f32[32,128]{1,0:T(8,128)S(1)} %get-tuple-element.11.mine_ref), channel_id=1, source_target_pairs={{0,1},{2,3},{4,5},{6,7},{8,9},{10,11},{12,13},{14,15},{1,0},{3,2},... | collective-permute-start | bytes 49160 | tf_op jit(solution)/shard_map/ppermute | solution.py:514
  21.3 4.2 %collective-permute-done.other_ref = f32[32,128]{1,0:T(8,128)S(1)} collective-permute-done((f32[32,128]{1,0:T(8,128)S(1)}, f32[32,128]{1,0:T(8,128)S(1)}, u32[]{:S(2)}, u32[]{:S(2)}) %collective-permute-start) | collective-permute-done | bytes 16416 | tf_op jit(solution)/shard_map/ppermute | solution.py:514
  25.4 0.1 shard_map.60
  25.5 1.9 %collective-permute-start.1 = (f32[32,128]{1,0:T(8,128)S(1)}, f32[32,128]{1,0:T(8,128)S(1)}, u32[]{:S(2)}, u32[]{:S(2)}) collective-permute-start(f32[32,128]{1,0:T(8,128)S(1)} %shard_map.60), channel_id=1, source_target_pairs={{1,16},{17,32},{33,48},{49,64},{65,80},{81,96},{97,112},{113,128},... | collective-permute-start | bytes 49160 | tf_op jit(solution)/shard_map/ppermute | solution.py:534
  27.5 4.9 %collective-permute-done.1.near_ref = f32[32,128]{1,0:T(8,128)S(1)} collective-permute-done((f32[32,128]{1,0:T(8,128)S(1)}, f32[32,128]{1,0:T(8,128)S(1)}, u32[]{:S(2)}, u32[]{:S(2)}) %collective-permute-start.1) | collective-permute-done | bytes 16416 | tf_op jit(solution)/shard_map/ppermute | solution.py:534
  32.4 1.9 %collective-permute-start.2 = (f32[32,128]{1,0:T(8,128)S(1)}, f32[32,128]{1,0:T(8,128)S(1)}, u32[]{:S(2)}, u32[]{:S(2)}) collective-permute-start(f32[32,128]{1,0:T(8,128)S(1)} %collective-permute-done.1.near_ref), channel_id=1, source_target_pairs={{0,1},{2,3},{4,5},{6,7},{8,9},{10,11},{12,13},{14,15},{1,0},{3,2},... | collective-permute-start | bytes 49160 | tf_op jit(solution)/shard_map/ppermute | solution.py:536
  34.3 3.7 %collective-permute-done.2.far_ref = f32[32,128]{1,0:T(8,128)S(1)} collective-permute-done((f32[32,128]{1,0:T(8,128)S(1)}, f32[32,128]{1,0:T(8,128)S(1)}, u32[]{:S(2)}, u32[]{:S(2)}) %collective-permute-start.2) | collective-permute-done | bytes 16416 | tf_op jit(solution)/shard_map/ppermute | solution.py:536
  38.0 1.9 %collective-permute-start.3 = (f32[4,8,128]{2,1,0:T(8,128)S(1)}, f32[4,8,128]{2,1,0:T(8,128)S(1)}, u32[]{:S(2)}, u32[]{:S(2)}) collective-permute-start(f32[4,8,128]{2,1,0:T(8,128)S(1)} %shard_map.61), channel_id=1, source_target_pairs={{1,2},{3,4},{5,6},{7,8},{9,10},{11,12},{13,14},{2,1},{4,3},{6,5},{... | collective-permute-start | bytes 49160 | tf_op jit(solution)/shard_map/ppermute | solution.py:544
  39.9 4.0 %collective-permute-done.3.edge_ref = f32[4,8,128]{2,1,0:T(8,128)S(1)} collective-permute-done((f32[4,8,128]{2,1,0:T(8,128)S(1)}, f32[4,8,128]{2,1,0:T(8,128)S(1)}, u32[]{:S(2)}, u32[]{:S(2)}) %collective-permute-start.3) | collective-permute-done | bytes 16416 | tf_op jit(solution)/shard_map/ppermute | solution.py:544
  44.0 0.4 shard_map.63.table
  44.4 0.0 all-to-all-done
  44.4 2.9 %shard_map.65 = (f32[32,128]{1,0:T(8,128)S(1)}, f32[32,128]{1,0:T(8,128)S(1)}, f32[2,8,128]{2,1,0:T(8,128)S(1)}) custom-call(s32[3,8,128]{2,1,0:T(8,128)S(1)} %broadcast.4.place_ref, f32[9,4,16,128]{3,2,1,0:T(8,128)S(1)} %shard_map.63.table, f32[512,128]{1,0:T(8,128)S(1)} %bitcast.4), custom_call_target="tpu_custom_call" | custom-call | tf_op jit(solution)/shard_map/pallas_call | solution.py:561
  47.3 1.9 %collective-permute-start.4 = (f32[2,8,128]{2,1,0:T(8,128)S(1)}, f32[2,8,128]{2,1,0:T(8,128)S(1)}, u32[]{:S(2)}, u32[]{:S(2)}) collective-permute-start(f32[2,8,128]{2,1,0:T(8,128)S(1)} %get-tuple-element.19), channel_id=1, source_target_pairs={{1,2},{3,4},{5,6},{7,8},{9,10},{11,12},{13,14},{2,1},{4,3},{6,5},{... | collective-permute-start | bytes 24584 | tf_op jit(solution)/shard_map/ppermute | solution.py:574
  49.2 3.9 %collective-permute-done.4.edge_ref = f32[2,8,128]{2,1,0:T(8,128)S(1)} collective-permute-done((f32[2,8,128]{2,1,0:T(8,128)S(1)}, f32[2,8,128]{2,1,0:T(8,128)S(1)}, u32[]{:S(2)}, u32[]{:S(2)}) %collective-permute-start.4) | collective-permute-done | bytes 8224 | tf_op jit(solution)/shard_map/ppermute | solution.py:574
  53.2 1.9 %collective-permute-start.5 = (f32[32,128]{1,0:T(8,128)S(1)}, f32[32,128]{1,0:T(8,128)S(1)}, u32[]{:S(2)}, u32[]{:S(2)}) collective-permute-start(f32[32,128]{1,0:T(8,128)S(1)} %shard_map.66), channel_id=1, source_target_pairs={{0,1},{2,3},{4,5},{6,7},{8,9},{10,11},{12,13},{14,15},{1,0},{3,2},... | collective-permute-start | bytes 49160 | tf_op jit(solution)/shard_map/ppermute | solution.py:582
  55.1 3.7 %collective-permute-done.5.other_ref = f32[32,128]{1,0:T(8,128)S(1)} collective-permute-done((f32[32,128]{1,0:T(8,128)S(1)}, f32[32,128]{1,0:T(8,128)S(1)}, u32[]{:S(2)}, u32[]{:S(2)}) %collective-permute-start.5) | collective-permute-done | bytes 16416 | tf_op jit(solution)/shard_map/ppermute | solution.py:582
  58.8 0.7 %shard_map.67 = (f32[2,32,32]{2,1,0:T(8,128)}, f32[2,32,32]{2,1,0:T(8,128)}) custom-call(s32[3,8,128]{2,1,0:T(8,128)S(1)} %broadcast.4.place_ref, f32[32,128]{1,0:T(8,128)S(1)} %get-tuple-element.17.mine_ref, f32[32,128]{1,0:T(8,128)S(1)} %collective-permute-done.5.other_ref, f32[2,8,128]{2,1,0:T(8,128)S(1)} %collective-permute-done.4.edge_ref), custom_call_target="tpu_custom_call" | custom-call | tf_op jit(solution)/shard_map/pallas_call | solution.py:583
  (3 shorter events, 0.0 us)
Async XLA Ops:
  2.8 41.6 %all-to-all-start = ((f32[32,16,128]{2,1,0:T(8,128)}), f32[32,16,128]{2,1,0:T(8,128)S(1)}, u32[]{:S(2)}, u32[]{:S(2)}) async-start(f32[32,16,128]{2,1,0:T(8,128)} %shard_map.64), calls=%async_computation | async-start | bytes 524288 | tf_op jit(solution)/shard_map/all_to_all | solution.py:535
  18.7 6.8 %collective-permute-start = (f32[32,128]{1,0:T(8,128)S(1)}, f32[32,128]{1,0:T(8,128)S(1)}, u32[]{:S(2)}, u32[]{:S(2)}) collective-permute-start(f32[32,128]{1,0:T(8,128)S(1)} %get-tuple-element.11.mine_ref), channel_id=1, source_target_pairs={{0,1},{2,3},{4,5},{6,7},{8,9},{10,11},{12,13},{14,15},{1,0},{3,2},... | collective-permute-start | bytes 49160 | tf_op jit(solution)/shard_map/ppermute | solution.py:514
  25.5 6.8 %collective-permute-start.1 = (f32[32,128]{1,0:T(8,128)S(1)}, f32[32,128]{1,0:T(8,128)S(1)}, u32[]{:S(2)}, u32[]{:S(2)}) collective-permute-start(f32[32,128]{1,0:T(8,128)S(1)} %shard_map.60), channel_id=1, source_target_pairs={{1,16},{17,32},{33,48},{49,64},{65,80},{81,96},{97,112},{113,128},... | collective-permute-start | bytes 49160 | tf_op jit(solution)/shard_map/ppermute | solution.py:534
  32.4 5.6 %collective-permute-start.2 = (f32[32,128]{1,0:T(8,128)S(1)}, f32[32,128]{1,0:T(8,128)S(1)}, u32[]{:S(2)}, u32[]{:S(2)}) collective-permute-start(f32[32,128]{1,0:T(8,128)S(1)} %collective-permute-done.1.near_ref), channel_id=1, source_target_pairs={{0,1},{2,3},{4,5},{6,7},{8,9},{10,11},{12,13},{14,15},{1,0},{3,2},... | collective-permute-start | bytes 49160 | tf_op jit(solution)/shard_map/ppermute | solution.py:536
  38.0 5.9 %collective-permute-start.3 = (f32[4,8,128]{2,1,0:T(8,128)S(1)}, f32[4,8,128]{2,1,0:T(8,128)S(1)}, u32[]{:S(2)}, u32[]{:S(2)}) collective-permute-start(f32[4,8,128]{2,1,0:T(8,128)S(1)} %shard_map.61), channel_id=1, source_target_pairs={{1,2},{3,4},{5,6},{7,8},{9,10},{11,12},{13,14},{2,1},{4,3},{6,5},{... | collective-permute-start | bytes 49160 | tf_op jit(solution)/shard_map/ppermute | solution.py:544
  47.3 5.9 %collective-permute-start.4 = (f32[2,8,128]{2,1,0:T(8,128)S(1)}, f32[2,8,128]{2,1,0:T(8,128)S(1)}, u32[]{:S(2)}, u32[]{:S(2)}) collective-permute-start(f32[2,8,128]{2,1,0:T(8,128)S(1)} %get-tuple-element.19), channel_id=1, source_target_pairs={{1,2},{3,4},{5,6},{7,8},{9,10},{11,12},{13,14},{2,1},{4,3},{6,5},{... | collective-permute-start | bytes 24584 | tf_op jit(solution)/shard_map/ppermute | solution.py:574
  53.2 5.6 %collective-permute-start.5 = (f32[32,128]{1,0:T(8,128)S(1)}, f32[32,128]{1,0:T(8,128)S(1)}, u32[]{:S(2)}, u32[]{:S(2)}) collective-permute-start(f32[32,128]{1,0:T(8,128)S(1)} %shard_map.66), channel_id=1, source_target_pairs={{0,1},{2,3},{4,5},{6,7},{8,9},{10,11},{12,13},{14,15},{1,0},{3,2},... | collective-permute-start | bytes 49160 | tf_op jit(solution)/shard_map/ppermute | solution.py:582

commit v7 on v6

--- a/solution.py
+++ b/solution.py
@@ -194,7 +194,13 @@
         copy.wait()
 
 
-def transmit(place_ref, here_ref, left_ref, right_ref, table, flat):
+def transmit(
+    place_ref, mine_ref, other_ref, near_ref, far_ref, edge_ref,
+    table, flat, here_ref, left_ref, right_ref,
+):
+    pack_rows(
+        place_ref, mine_ref, other_ref, near_ref, far_ref, edge_ref, here_ref, left_ref, right_ref
+    )
     sub = lax.broadcasted_iota(jnp.int32, (8, 128), 0)
     block, slab, cut = place_ref[0], place_ref[1], place_ref[2]
     lane = lanes_of((8, 128))
@@ -542,22 +548,19 @@
         compiler_params=small,
     )(place, mine, other, near, far)
     edges = lax.ppermute(edges, rows_axis, across)
-    here, from_left, from_right = pl.pallas_call(
-        pack_rows,
-        out_shape=(f32(2, 32, 128), f32(32, 128), f32(32, 128)),
-        in_specs=[VMEM] * 6,
-        out_specs=(VMEM,) * 3,
-        compiler_params=small,
-    )(place, mine, other, near, far, edges)
-
     table = pl.pallas_call(
         transmit,
         out_shape=f32(9, 4, 16, 128),
-        in_specs=[VMEM] * 4,
+        in_specs=[VMEM] * 6,
         out_specs=VMEM,
-        scratch_shapes=[pltpu.VMEM((128, 128), jnp.float32)],
+        scratch_shapes=[
+            pltpu.VMEM((128, 128), jnp.float32),
+            pltpu.VMEM((2, 32, 128), jnp.float32),
+            pltpu.VMEM((32, 128), jnp.float32),
+            pltpu.VMEM((32, 128), jnp.float32),
+        ],
         compiler_params=small,
-    )(place, here, from_left, from_right)
+    )(place, mine, other, near, far, edges)
     mine, other, edges = pl.pallas_call(
         march,
         out_shape=(f32(32, 128), f32(32, 128), f32(2, 8, 128)),

time: 59.9 us -> 59.8 us (level)
  the two profiles are of different devices: /device:TPU:38 before, /device:TPU:34 now
where the time goes in v7:
time: 59.8 us; the launch traced here: 59.5 us
  starting transfers between devices  28 us (47%)
  waiting for transfers between devices  24.5 us (41%)
  Pallas kernels  6.13 us (10%)
  between operations  0.74 us (1%)
    all_to_all x1, starting transfers between devices, body(): got = lax.all_to_all(sent, 'illum', 0, 0, tiled=True)  15.8 us
    ppermute x2, waiting for transfers between devices, body(): edges = lax.ppermute(edges, rows_axis, across)  7.97 us
    ppermute x1, waiting for transfers between devices, body(): near = lax.ppermute(near, ('illum', 'cuts'), beside)  4.91 us
    ppermute x1, waiting for transfers between devices, body(): other = lax.ppermute(mine, rows_axis, partner)  4.16 us
    ppermute x2, starting transfers between devices, body(): edges = lax.ppermute(edges, rows_axis, across)  3.83 us
    ppermute x1, waiting for transfers between devices, body(): far = lax.ppermute(near, rows_axis, partner)  3.7 us
    ppermute x1, waiting for transfers between devices, body(): other = lax.ppermute(other, rows_axis, partner)  3.7 us
    pallas_call x1, Pallas kernels, body(): pl.pallas_call(march, out_shape=(f32(32, 128), f32(32, 128), f32(2, 8, 12...  2.86 us
  transfers between devices with their start and end apart: 7, of which 6 were waited for; matrix products, arithmetic and copies ran while one was open for 0% of the time, Pallas kernels for 1%

profile of v7, /device:TPU:34, one launch (start us, length us, event | category | flops | bytes accessed | tf_op | source)
XLA Modules:
  0.0 59.5 jit_solution(9635710363141028680)
XLA Ops:
  0.6 0.1 add_add_fusion
  0.7 1.0 %shard_map.59 = (f32[32,128]{1,0:T(8,128)S(1)}, f32[2,32,1024]{2,1,0:T(8,128)S(1)}, f32[8,128]{1,0:T(8,128)S(1)}) custom-call(f32[2,32,32]{2,1,0:T(8,128)} %phase_ref.1, f32[2,32,32]{2,1,0:T(8,128)} %atten_ref.1, f32[1,2,32,1024]{3,2,1,0:T(8,128)} %measured_ref.1, s32[1,2]{1,0:T(1,128)} %angles_ref.1), custom_call_target="tpu_custom_call" | custom-call | tf_op jit(solution)/shard_map/pallas_call | solution.py:507
  1.7 0.1 broadcast.4.place_ref
  1.8 1.0 %shard_map.63 = f32[32,16,128]{2,1,0:T(8,128)} custom-call(s32[3,8,128]{2,1,0:T(8,128)S(1)} %broadcast.4.place_ref, f32[2,32,1024]{2,1,0:T(8,128)S(1)} %get-tuple-element.9.whole_ref, f32[8,128]{1,0:T(8,128)S(1)} %get-tuple-element.10.head_ref), custom_call_target="tpu_custom_call" | custom-call | tf_op jit(solution)/shard_map/pallas_call | solution.py:521
  2.8 15.8 %all-to-all-start = ((f32[32,16,128]{2,1,0:T(8,128)}), f32[32,16,128]{2,1,0:T(8,128)S(1)}, u32[]{:S(2)}, u32[]{:S(2)}) async-start(f32[32,16,128]{2,1,0:T(8,128)} %shard_map.63), calls=%async_computation | async-start | bytes 524288 | tf_op jit(solution)/shard_map/all_to_all | solution.py:541
  18.7 2.6 %collective-permute-start = (f32[32,128]{1,0:T(8,128)S(1)}, f32[32,128]{1,0:T(8,128)S(1)}, u32[]{:S(2)}, u32[]{:S(2)}) collective-permute-start(f32[32,128]{1,0:T(8,128)S(1)} %get-tuple-element.8.mine_ref), channel_id=1, source_target_pairs={{0,1},{2,3},{4,5},{6,7},{8,9},{10,11},{12,13},{14,15},{1,0},{3,2},... | collective-permute-start | bytes 49160 | tf_op jit(solution)/shard_map/ppermute | solution.py:520
  21.3 4.2 %collective-permute-done.other_ref = f32[32,128]{1,0:T(8,128)S(1)} collective-permute-done((f32[32,128]{1,0:T(8,128)S(1)}, f32[32,128]{1,0:T(8,128)S(1)}, u32[]{:S(2)}, u32[]{:S(2)}) %collective-permute-start) | collective-permute-done | bytes 16416 | tf_op jit(solution)/shard_map/ppermute | solution.py:520
  25.4 0.1 shard_map.60
  25.5 1.9 %collective-permute-start.1 = (f32[32,128]{1,0:T(8,128)S(1)}, f32[32,128]{1,0:T(8,128)S(1)}, u32[]{:S(2)}, u32[]{:S(2)}) collective-permute-start(f32[32,128]{1,0:T(8,128)S(1)} %shard_map.60), channel_id=1, source_target_pairs={{1,16},{17,32},{33,48},{49,64},{65,80},{81,96},{97,112},{113,128},... | collective-permute-start | bytes 49160 | tf_op jit(solution)/shard_map/ppermute | solution.py:540
  27.5 4.9 %collective-permute-done.1.near_ref = f32[32,128]{1,0:T(8,128)S(1)} collective-permute-done((f32[32,128]{1,0:T(8,128)S(1)}, f32[32,128]{1,0:T(8,128)S(1)}, u32[]{:S(2)}, u32[]{:S(2)}) %collective-permute-start.1) | collective-permute-done | bytes 16416 | tf_op jit(solution)/shard_map/ppermute | solution.py:540
  32.4 1.9 %collective-permute-start.2 = (f32[32,128]{1,0:T(8,128)S(1)}, f32[32,128]{1,0:T(8,128)S(1)}, u32[]{:S(2)}, u32[]{:S(2)}) collective-permute-start(f32[32,128]{1,0:T(8,128)S(1)} %collective-permute-done.1.near_ref), channel_id=1, source_target_pairs={{0,1},{2,3},{4,5},{6,7},{8,9},{10,11},{12,13},{14,15},{1,0},{3,2},... | collective-permute-start | bytes 49160 | tf_op jit(solution)/shard_map/ppermute | solution.py:542
  34.3 3.7 %collective-permute-done.2.far_ref = f32[32,128]{1,0:T(8,128)S(1)} collective-permute-done((f32[32,128]{1,0:T(8,128)S(1)}, f32[32,128]{1,0:T(8,128)S(1)}, u32[]{:S(2)}, u32[]{:S(2)}) %collective-permute-start.2) | collective-permute-done | bytes 16416 | tf_op jit(solution)/shard_map/ppermute | solution.py:542
  38.0 1.9 %collective-permute-start.3 = (f32[4,8,128]{2,1,0:T(8,128)S(1)}, f32[4,8,128]{2,1,0:T(8,128)S(1)}, u32[]{:S(2)}, u32[]{:S(2)}) collective-permute-start(f32[4,8,128]{2,1,0:T(8,128)S(1)} %shard_map.61), channel_id=1, source_target_pairs={{1,2},{3,4},{5,6},{7,8},{9,10},{11,12},{13,14},{2,1},{4,3},{6,5},{... | collective-permute-start | bytes 49160 | tf_op jit(solution)/shard_map/ppermute | solution.py:550
  39.9 4.0 %collective-permute-done.3.edge_ref = f32[4,8,128]{2,1,0:T(8,128)S(1)} collective-permute-done((f32[4,8,128]{2,1,0:T(8,128)S(1)}, f32[4,8,128]{2,1,0:T(8,128)S(1)}, u32[]{:S(2)}, u32[]{:S(2)}) %collective-permute-start.3) | collective-permute-done | bytes 16416 | tf_op jit(solution)/shard_map/ppermute | solution.py:550
  44.0 0.4 shard_map.62.table
  44.4 0.0 all-to-all-done
  44.4 2.9 %shard_map.64 = (f32[32,128]{1,0:T(8,128)S(1)}, f32[32,128]{1,0:T(8,128)S(1)}, f32[2,8,128]{2,1,0:T(8,128)S(1)}) custom-call(s32[3,8,128]{2,1,0:T(8,128)S(1)} %broadcast.4.place_ref, f32[9,4,16,128]{3,2,1,0:T(8,128)S(1)} %shard_map.62.table, f32[512,128]{1,0:T(8,128)S(1)} %bitcast.4), custom_call_target="tpu_custom_call" | custom-call | tf_op jit(solution)/shard_map/pallas_call | solution.py:564
  47.3 1.9 %collective-permute-start.4 = (f32[2,8,128]{2,1,0:T(8,128)S(1)}, f32[2,8,128]{2,1,0:T(8,128)S(1)}, u32[]{:S(2)}, u32[]{:S(2)}) collective-permute-start(f32[2,8,128]{2,1,0:T(8,128)S(1)} %get-tuple-element.13), channel_id=1, source_target_pairs={{1,2},{3,4},{5,6},{7,8},{9,10},{11,12},{13,14},{2,1},{4,3},{6,5},{... | collective-permute-start | bytes 24584 | tf_op jit(solution)/shard_map/ppermute | solution.py:577
  49.2 3.9 %collective-permute-done.4.edge_ref = f32[2,8,128]{2,1,0:T(8,128)S(1)} collective-permute-done((f32[2,8,128]{2,1,0:T(8,128)S(1)}, f32[2,8,128]{2,1,0:T(8,128)S(1)}, u32[]{:S(2)}, u32[]{:S(2)}) %collective-permute-start.4) | collective-permute-done | bytes 8224 | tf_op jit(solution)/shard_map/ppermute | solution.py:577
  53.1 1.9 %collective-permute-start.5 = (f32[32,128]{1,0:T(8,128)S(1)}, f32[32,128]{1,0:T(8,128)S(1)}, u32[]{:S(2)}, u32[]{:S(2)}) collective-permute-start(f32[32,128]{1,0:T(8,128)S(1)} %shard_map.65), channel_id=1, source_target_pairs={{0,1},{2,3},{4,5},{6,7},{8,9},{10,11},{12,13},{14,15},{1,0},{3,2},... | collective-permute-start | bytes 49160 | tf_op jit(solution)/shard_map/ppermute | solution.py:585
  55.1 3.7 %collective-permute-done.5.other_ref = f32[32,128]{1,0:T(8,128)S(1)} collective-permute-done((f32[32,128]{1,0:T(8,128)S(1)}, f32[32,128]{1,0:T(8,128)S(1)}, u32[]{:S(2)}, u32[]{:S(2)}) %collective-permute-start.5) | collective-permute-done | bytes 16416 | tf_op jit(solution)/shard_map/ppermute | solution.py:585
  58.8 0.7 %shard_map.66 = (f32[2,32,32]{2,1,0:T(8,128)}, f32[2,32,32]{2,1,0:T(8,128)}) custom-call(s32[3,8,128]{2,1,0:T(8,128)S(1)} %broadcast.4.place_ref, f32[32,128]{1,0:T(8,128)S(1)} %get-tuple-element.11.mine_ref, f32[32,128]{1,0:T(8,128)S(1)} %collective-permute-done.5.other_ref, f32[2,8,128]{2,1,0:T(8,128)S(1)} %collective-permute-done.4.edge_ref), custom_call_target="tpu_custom_call" | custom-call | tf_op jit(solution)/shard_map/pallas_call | solution.py:586
  (2 shorter events, 0.0 us)
Async XLA Ops:
  2.8 41.6 %all-to-all-start = ((f32[32,16,128]{2,1,0:T(8,128)}), f32[32,16,128]{2,1,0:T(8,128)S(1)}, u32[]{:S(2)}, u32[]{:S(2)}) async-start(f32[32,16,128]{2,1,0:T(8,128)} %shard_map.63), calls=%async_computation | async-start | bytes 524288 | tf_op jit(solution)/shard_map/all_to_all | solution.py:541
  18.7 6.8 %collective-permute-start = (f32[32,128]{1,0:T(8,128)S(1)}, f32[32,128]{1,0:T(8,128)S(1)}, u32[]{:S(2)}, u32[]{:S(2)}) collective-permute-start(f32[32,128]{1,0:T(8,128)S(1)} %get-tuple-element.8.mine_ref), channel_id=1, source_target_pairs={{0,1},{2,3},{4,5},{6,7},{8,9},{10,11},{12,13},{14,15},{1,0},{3,2},... | collective-permute-start | bytes 49160 | tf_op jit(solution)/shard_map/ppermute | solution.py:520
  25.5 6.8 %collective-permute-start.1 = (f32[32,128]{1,0:T(8,128)S(1)}, f32[32,128]{1,0:T(8,128)S(1)}, u32[]{:S(2)}, u32[]{:S(2)}) collective-permute-start(f32[32,128]{1,0:T(8,128)S(1)} %shard_map.60), channel_id=1, source_target_pairs={{1,16},{17,32},{33,48},{49,64},{65,80},{81,96},{97,112},{113,128},... | collective-permute-start | bytes 49160 | tf_op jit(solution)/shard_map/ppermute | solution.py:540
  32.4 5.6 %collective-permute-start.2 = (f32[32,128]{1,0:T(8,128)S(1)}, f32[32,128]{1,0:T(8,128)S(1)}, u32[]{:S(2)}, u32[]{:S(2)}) collective-permute-start(f32[32,128]{1,0:T(8,128)S(1)} %collective-permute-done.1.near_ref), channel_id=1, source_target_pairs={{0,1},{2,3},{4,5},{6,7},{8,9},{10,11},{12,13},{14,15},{1,0},{3,2},... | collective-permute-start | bytes 49160 | tf_op jit(solution)/shard_map/ppermute | solution.py:542
  38.0 5.9 %collective-permute-start.3 = (f32[4,8,128]{2,1,0:T(8,128)S(1)}, f32[4,8,128]{2,1,0:T(8,128)S(1)}, u32[]{:S(2)}, u32[]{:S(2)}) collective-permute-start(f32[4,8,128]{2,1,0:T(8,128)S(1)} %shard_map.61), channel_id=1, source_target_pairs={{1,2},{3,4},{5,6},{7,8},{9,10},{11,12},{13,14},{2,1},{4,3},{6,5},{... | collective-permute-start | bytes 49160 | tf_op jit(solution)/shard_map/ppermute | solution.py:550
  47.3 5.9 %collective-permute-start.4 = (f32[2,8,128]{2,1,0:T(8,128)S(1)}, f32[2,8,128]{2,1,0:T(8,128)S(1)}, u32[]{:S(2)}, u32[]{:S(2)}) collective-permute-start(f32[2,8,128]{2,1,0:T(8,128)S(1)} %get-tuple-element.13), channel_id=1, source_target_pairs={{1,2},{3,4},{5,6},{7,8},{9,10},{11,12},{13,14},{2,1},{4,3},{6,5},{... | collective-permute-start | bytes 24584 | tf_op jit(solution)/shard_map/ppermute | solution.py:577
  53.1 5.6 %collective-permute-start.5 = (f32[32,128]{1,0:T(8,128)S(1)}, f32[32,128]{1,0:T(8,128)S(1)}, u32[]{:S(2)}, u32[]{:S(2)}) collective-permute-start(f32[32,128]{1,0:T(8,128)S(1)} %shard_map.65), channel_id=1, source_target_pairs={{0,1},{2,3},{4,5},{6,7},{8,9},{10,11},{12,13},{14,15},{1,0},{3,2},... | collective-permute-start | bytes 49160 | tf_op jit(solution)/shard_map/ppermute | solution.py:585
